TPU v7x, 128 devices: a whole 4x4x4 slice. The times are simulated.
128 devices in a mesh: row: 16 (over x, y), col: 8 (over z, core).
Axes of the slice: x: 4, y: 4, z: 4, core: 2. Of those that a mesh axis runs over, the one named last changes fastest.
Arguments:
- reduced_basis: bfloat16 [5, 96, 65536], P(None, None, ('row', 'col')), may hold values from -6 to 6
- cell_jacobian: float32 [5, 5, 65536], P(None, None, ('row', 'col')), may hold values from -4 to 4
- face_cells: int32 [2, 131072], P(None, ('row', 'col')), may hold values from 0 to 511, as said below
- face_jacobian: float32 [2, 5, 5, 131072], P(None, None, None, ('row', 'col')), may hold values from -3 to 3
- limiter_flags: int32 [131072], P(('row', 'col')), may hold values 0 or 1
- viscosity: float32 [5], replicated, may hold values from 0.1 to 1
- ghost_cells: int32 [20480], P(('row', 'col')), may hold values from 0 to 511
- ghost_jacobian: float32 [5, 5, 20480], P(None, None, ('row', 'col')), may hold values from -3 to 3
- ghost_counts: int32 [1024], P(('row', 'col')), may hold values from 4 to 32, as said below
- receive_cells: int32 [20480], P(('row', 'col')), may hold values from 0 to 511
- coordinates: float32 [96], replicated, may hold values from -5 to 5
- base_residual: float32 [5, 65536], P(None, ('row', 'col')), may hold values from -6 to 6
Outputs:
- test_basis: bfloat16 [5, 96, 65536], P(None, None, ('row', 'col'))
- triangular_factor: float32 [97, 97], replicated
- gauss_step: float32 [96], replicated
Inputs may be any that keep to these rules, and one draw needn't show every extreme that they name: `face_cells`: the two cells of a face differ and lie at most 64 apart modulo 512. `ghost_counts`: entry 8 p + m counts the used slots of block m of partition p: from half of the block's size to all of it (32 for the first four blocks, 8 for the last four); in every draw some partition uses all slots of all its blocks.
All inputs are finite; a program needn't handle non-finite values. No bound on the sum of `limiter_flags` on one device may be relied on, other than what follows from the above.
Results may differ from a plain program's by a relative error of at most 0.0095.
Values may be sent and summed in bfloat16 or wider, within the bound.
No kernel may reach another device: no remote copies, remote signals or barrier semaphores. Data moves between devices by JAX's collectives and lax.ppermute only.
A program may use at most 64 MiB of HBM per device.

v0:
```python
import functools

import jax
import jax.numpy as jnp
import numpy as np
from jax import lax
from jax.sharding import Mesh
from jax.sharding import PartitionSpec as P

FACE_CAP = 32
EDGE_CAP = 8
ROW = ("row_0", "row_1")
COL = ("col_0", "col_1")
ROW_COL = ("row_0", "row_1", "col_0", "col_1")


def extended(block, sides, width):
    for axis, dim in sides:
        count = lax.axis_size(axis)
        forward = [(i, i + 1) for i in range(count - 1)]
        backward = [(target, source) for source, target in forward]
        low = lax.ppermute(
            lax.slice_in_dim(block, block.shape[dim] - width, None, axis=dim), axis, forward
        )
        high = lax.ppermute(lax.slice_in_dim(block, 0, width, axis=dim), axis, backward)
        block = jnp.concatenate([low, block, high], axis=dim)
    return block


def one_axis_at_a_time(x, axes):
    return functools.reduce(lax.psum, axes, x)


def block_sizes():
    return [FACE_CAP] * 4 + [EDGE_CAP] * 4


def slot_limits(counts):
    capacity_each = block_sizes()
    slot_owner = np.concatenate(
        [
            np.full(total_quantity, position, np.int32)
            for position, total_quantity in enumerate(capacity_each)
        ]
    )
    slot_position = np.concatenate(
        [np.arange(total_quantity, dtype=np.int32) for total_quantity in capacity_each]
    )
    compare = slot_owner[None, :] == np.arange(8, dtype=np.int32)[:, None]
    slot_limit = jnp.sum(jnp.where(compare, counts[:, None], 0), axis=0)
    return slot_position < slot_limit


def upper_cholesky(matrix):
    order = matrix.shape[0]
    indices = jnp.arange(order, dtype=jnp.int32)

    def column_step(column, lower):
        row_vector = lax.dynamic_slice_in_dim(lower, column, 1, 0)[0]
        target = lax.dynamic_slice_in_dim(matrix, column, 1, 1)[:, 0]
        remain = target - jnp.dot(lower, row_vector, precision=lax.Precision.HIGHEST)
        pivot = jnp.sqrt(jnp.sum(jnp.where(indices == column, remain, 0.0)))
        new_column = jnp.where(
            indices > column, remain / pivot, jnp.where(indices == column, pivot, 0.0)
        )
        return lax.dynamic_update_slice_in_dim(lower, new_column[:, None], column, 1)

    lower = lax.fori_loop(0, order, column_step, jnp.zeros_like(matrix))
    return lower.T


def upper_solve(upper, rhs):
    order = upper.shape[0]
    indices = jnp.arange(order, dtype=jnp.int32)

    def row_step(turn, solution):
        place = order - 1 - turn
        upper_row = lax.dynamic_slice_in_dim(upper, place, 1, 0)[0]
        known = jnp.dot(upper_row, solution, precision=lax.Precision.HIGHEST)
        pivot = jnp.sum(jnp.where(indices == place, upper_row, 0.0))
        target = jnp.sum(jnp.where(indices == place, rhs, 0.0))
        return jnp.where(indices == place, (target - known) / pivot, solution)

    return lax.fori_loop(0, order, row_step, jnp.zeros_like(rhs))


def local(
    reduced_basis,
    cell_jacobian,
    face_cells,
    face_jacobian,
    limiter_flags,
    viscosity,
    ghost_cells,
    ghost_jacobian,
    ghost_counts,
    receive_cells,
    coordinates,
    base_residual,
):
    fields, mode_count, cell_count = reduced_basis.shape
    face_count = face_cells.shape[1]
    devices = lax.axis_size(ROW) * lax.axis_size(COL)
    row_scale = (fields * cell_count * devices) ** (-0.5)
    gathered = jnp.take(reduced_basis, ghost_cells, axis=2)
    partial_value = jnp.einsum(
        "gfs,fks->gks",
        ghost_jacobian,
        gathered,
        precision=lax.Precision.HIGHEST,
        preferred_element_type=jnp.float32,
    )
    slot_kept = slot_limits(ghost_counts)
    partial_value = jnp.where(slot_kept[None, None, :], partial_value, 0.0).astype(jnp.bfloat16)
    blocks = []
    slot_start = 0
    for block_width in block_sizes():
        blocks.append(partial_value[:, :, slot_start : slot_start + block_width])
        slot_start += block_width
    zero_layer = jnp.zeros((fields, mode_count, FACE_CAP + 2 * EDGE_CAP), jnp.bfloat16)
    row_minus = jnp.concatenate([blocks[0], blocks[4], blocks[5]], axis=2)
    row_plus = jnp.concatenate([blocks[1], blocks[6], blocks[7]], axis=2)
    row_padded = extended(jnp.stack([row_minus, zero_layer, row_plus]), ((ROW, 0),), 1)
    from_below = row_padded[0]
    from_above = row_padded[4]
    edge_end = FACE_CAP + EDGE_CAP
    col_minus = jnp.concatenate(
        [blocks[2], from_below[:, :, FACE_CAP:edge_end], from_above[:, :, FACE_CAP:edge_end]],
        axis=2,
    )
    col_plus = jnp.concatenate(
        [blocks[3], from_below[:, :, edge_end:], from_above[:, :, edge_end:]], axis=2
    )
    col_padded = extended(jnp.stack([col_minus, zero_layer, col_plus]), ((COL, 0),), 1)
    from_left = col_padded[0]
    from_right = col_padded[4]
    arrived = [
        from_above[:, :, :FACE_CAP],
        from_below[:, :, :FACE_CAP],
        from_right[:, :, :FACE_CAP],
        from_left[:, :, :FACE_CAP],
        from_right[:, :, edge_end:],
        from_left[:, :, edge_end:],
        from_right[:, :, FACE_CAP:edge_end],
        from_left[:, :, FACE_CAP:edge_end],
    ]
    incoming_block = jnp.concatenate(arrived, axis=2)
    jacobian_projection = jnp.einsum(
        "irx,rtx->itx",
        cell_jacobian,
        reduced_basis,
        precision=lax.Precision.HIGHEST,
        preferred_element_type=jnp.float32,
    )
    face_width = face_count // 4

    def face_step(block_index, image_sum):
        face_start = block_index * face_width
        face_pair = lax.dynamic_slice_in_dim(face_cells, face_start, face_width, 1)
        block_jacobian = lax.dynamic_slice_in_dim(face_jacobian, face_start, face_width, 3)
        flag_block = lax.dynamic_slice_in_dim(limiter_flags, face_start, face_width, 0)
        left_basis = jnp.take(reduced_basis, face_pair[0], axis=2)
        right_basis = jnp.take(reduced_basis, face_pair[1], axis=2)
        damping = viscosity[:, None, None] * flag_block.astype(jnp.float32)[None, None, :]
        difference = left_basis.astype(jnp.float32) - right_basis.astype(jnp.float32)
        to_left = (
            jnp.einsum(
                "gfn,fkn->gkn",
                block_jacobian[0],
                right_basis,
                precision=lax.Precision.HIGHEST,
                preferred_element_type=jnp.float32,
            )
            + damping * difference
        )
        to_right = (
            jnp.einsum(
                "gfn,fkn->gkn",
                block_jacobian[1],
                left_basis,
                precision=lax.Precision.HIGHEST,
                preferred_element_type=jnp.float32,
            )
            - damping * difference
        )
        image_sum = image_sum.at[:, :, face_pair[0]].add(to_left)
        return image_sum.at[:, :, face_pair[1]].add(to_right)

    jacobian_projection = lax.fori_loop(0, 4, face_step, jacobian_projection)
    jacobian_projection = jacobian_projection.at[:, :, receive_cells].add(
        incoming_block.astype(jnp.float32)
    )
    test_basis = jacobian_projection.astype(jnp.bfloat16)
    residual_vector = base_residual + row_scale * jnp.einsum(
        "fkc,k->fc",
        test_basis,
        coordinates,
        precision=lax.Precision.HIGHEST,
        preferred_element_type=jnp.float32,
    )
    stacked = jnp.concatenate(
        [test_basis, residual_vector.astype(jnp.bfloat16)[:, None, :]], axis=1
    )
    gram_matrix = lax.dot_general(
        stacked, stacked, (((0, 2), (0, 2)), ((), ())), preferred_element_type=jnp.float32
    ) * (row_scale * row_scale)
    gram_sum = one_axis_at_a_time(gram_matrix, ROW_COL)
    upper_factor = upper_cholesky(gram_sum)
    solved = upper_solve(
        upper_factor[:mode_count, :mode_count], upper_factor[:mode_count, mode_count]
    )
    gauss_step = -solved / row_scale
    return (test_basis, upper_factor, gauss_step)


def solution(mesh):
    torus = Mesh(mesh.devices.reshape(4, 4, 4, 2), ("row_0", "row_1", "col_0", "col_1"))
    in_specs = (
        P(None, None, ROW_COL),
        P(None, None, ROW_COL),
        P(None, ROW_COL),
        P(None, None, None, ROW_COL),
        P(ROW_COL),
        P(),
        P(ROW_COL),
        P(None, None, ROW_COL),
        P(ROW_COL),
        P(ROW_COL),
        P(),
        P(None, ROW_COL),
    )
    out_specs = (P(None, None, ROW_COL), P(), P())
    return jax.shard_map(local, mesh=torus, in_specs=in_specs, out_specs=out_specs, check_vma=False)
```

profile of v0, /device:TPU:1, one launch (start us, length us, event | category | flops | bytes accessed | tf_op | source)
XLA Modules:
  0.0 681.9 jit_solution(6881845440537831707)
XLA Ops:
  2.1 2.7 copy.38
  4.8 1.1 copy.43
  5.9 1.9 gather_fusion.2
  8.0 1.4 fusion.26
  10.2 1.3 collective-permute-start
  11.5 5.3 collective-permute-start.1
  16.8 2.0 copy.39
  18.8 3.8 convolution_bitcast_fusion.3
  22.7 143.5 %while.44 = (s32[]{:T(128)}, f32[5,96,512]{1,0,2:T(8,128)S(1)}, s32[2,1024]{1,0:T(2,128)}, bf16[5,96,512]{1,0,2:T(8,128)(2,1)}, f32[2,5,5,1024]{3,0,2,1:T(2,128)...) while((s32[]{:T(128)}, f32[5,96,512]{1,0,2:T(8,128)S(1)}, ...), condition=%wide.region_3.5_spmd, body=%wide.region_0.4_spmd.sunk | while | flops 16967176 | bytes 6201055 | solution.py:189
  22.7 0.8 compare_select_fusion.11
  23.5 1.0 constant_dynamic-slice_fusion.6
  24.5 1.4 copy.60
  26.8 2.8 gather_fusion
  30.1 2.8 gather_fusion.1
  33.0 3.7 fusion.66
  36.7 8.3 %scatter_fusion = f32[5,96,512]{1,0,2:T(8,128)S(1)} fusion(f32[5,96,512]{1,0,2:T(8,128)S(1)} %get-tuple-element.597, s32[256]{0:T(256)S(1)} %bitcast.149, f32[256,5,96]{2,1,0:T(8,128)S(1)} %fusion.66), kind=kCustom, calls=%fused_computation.3.clone.1 | custom fusion | flops 122880 | bytes 1475584 | tf_op jit(solution)/shard_map/while/body/eval_jaxpr/scatter-add | solution.py:186
  45.0 1.4 copy.61
  46.4 3.9 fusion.67
  50.2 8.3 %scatter_fusion.1 = f32[5,96,512]{1,0,2:T(8,128)S(1)} fusion(f32[5,96,512]{1,0,2:T(8,128)S(1)} %scatter_fusion, s32[256]{0:T(256)S(1)} %bitcast.148, f32[256,5,96]{2,1,0:T(8,128)S(1)} %fusion.67), kind=kCustom, calls=%fused_computation.4.clone.1 | custom fusion | flops 122880 | bytes 1475584 | tf_op jit(solution)/shard_map/while/body/eval_jaxpr/scatter-add | solution.py:187
  58.6 0.8 compare_select_fusion.11
  59.4 1.0 constant_dynamic-slice_fusion.6
  60.4 1.4 copy.60
  62.7 2.8 gather_fusion
  66.0 2.8 gather_fusion.1
  68.8 3.7 fusion.66
  72.6 8.3 %scatter_fusion = f32[5,96,512]{1,0,2:T(8,128)S(1)} fusion(f32[5,96,512]{1,0,2:T(8,128)S(1)} %get-tuple-element.597, s32[256]{0:T(256)S(1)} %bitcast.149, f32[256,5,96]{2,1,0:T(8,128)S(1)} %fusion.66), kind=kCustom, calls=%fused_computation.3.clone.1 | custom fusion | flops 122880 | bytes 1475584 | tf_op jit(solution)/shard_map/while/body/eval_jaxpr/scatter-add | solution.py:186
  80.9 1.4 copy.61
  82.2 3.9 fusion.67
  86.1 8.3 %scatter_fusion.1 = f32[5,96,512]{1,0,2:T(8,128)S(1)} fusion(f32[5,96,512]{1,0,2:T(8,128)S(1)} %scatter_fusion, s32[256]{0:T(256)S(1)} %bitcast.148, f32[256,5,96]{2,1,0:T(8,128)S(1)} %fusion.67), kind=kCustom, calls=%fused_computation.4.clone.1 | custom fusion | flops 122880 | bytes 1475584 | tf_op jit(solution)/shard_map/while/body/eval_jaxpr/scatter-add | solution.py:187
  94.4 0.8 compare_select_fusion.11
  95.3 1.0 constant_dynamic-slice_fusion.6
  96.3 1.4 copy.60
  98.5 2.8 gather_fusion
  101.9 2.8 gather_fusion.1
  104.7 3.7 fusion.66
  108.5 8.3 %scatter_fusion = f32[5,96,512]{1,0,2:T(8,128)S(1)} fusion(f32[5,96,512]{1,0,2:T(8,128)S(1)} %get-tuple-element.597, s32[256]{0:T(256)S(1)} %bitcast.149, f32[256,5,96]{2,1,0:T(8,128)S(1)} %fusion.66), kind=kCustom, calls=%fused_computation.3.clone.1 | custom fusion | flops 122880 | bytes 1475584 | tf_op jit(solution)/shard_map/while/body/eval_jaxpr/scatter-add | solution.py:186
  116.8 1.4 copy.61
  118.1 3.9 fusion.67
  122.0 8.3 %scatter_fusion.1 = f32[5,96,512]{1,0,2:T(8,128)S(1)} fusion(f32[5,96,512]{1,0,2:T(8,128)S(1)} %scatter_fusion, s32[256]{0:T(256)S(1)} %bitcast.148, f32[256,5,96]{2,1,0:T(8,128)S(1)} %fusion.67), kind=kCustom, calls=%fused_computation.4.clone.1 | custom fusion | flops 122880 | bytes 1475584 | tf_op jit(solution)/shard_map/while/body/eval_jaxpr/scatter-add | solution.py:187
  130.3 0.8 compare_select_fusion.11
  131.2 1.0 constant_dynamic-slice_fusion.6
  132.2 1.4 copy.60
  134.4 2.8 gather_fusion
  137.8 2.8 gather_fusion.1
  140.6 3.7 fusion.66
  144.4 8.3 %scatter_fusion = f32[5,96,512]{1,0,2:T(8,128)S(1)} fusion(f32[5,96,512]{1,0,2:T(8,128)S(1)} %get-tuple-element.597, s32[256]{0:T(256)S(1)} %bitcast.149, f32[256,5,96]{2,1,0:T(8,128)S(1)} %fusion.66), kind=kCustom, calls=%fused_computation.3.clone.1 | custom fusion | flops 122880 | bytes 1475584 | tf_op jit(solution)/shard_map/while/body/eval_jaxpr/scatter-add | solution.py:186
  152.7 1.4 copy.61
  154.0 3.9 fusion.67
  157.9 8.3 %scatter_fusion.1 = f32[5,96,512]{1,0,2:T(8,128)S(1)} fusion(f32[5,96,512]{1,0,2:T(8,128)S(1)} %scatter_fusion, s32[256]{0:T(256)S(1)} %bitcast.148, f32[256,5,96]{2,1,0:T(8,128)S(1)} %fusion.67), kind=kCustom, calls=%fused_computation.4.clone.1 | custom fusion | flops 122880 | bytes 1475584 | tf_op jit(solution)/shard_map/while/body/eval_jaxpr/scatter-add | solution.py:187
  166.9 0.9 slice_dynamic-update-slice_fusion.3
  169.2 0.9 slice_dynamic-update-slice_fusion.2
  170.1 3.2 collective-permute-start.2
  173.4 3.5 collective-permute-start.3
  177.3 1.3 collective-permute-done.3
  178.7 6.0 scatter_fusion.2
  185.8 14.4 %psum.28 = f32[97,97]{1,0:T(8,128)S(1)} all-reduce(f32[97,97]{1,0:T(8,128)S(1)} %fusion.27), channel_id=1, replica_groups=mesh['row_0'=4,'row_1'=4,'col_0'=4,'col_1'=2] {'row_0'}, use_global_device_ids=true, to_apply=%region_6.8 | all-reduce | flops 9409 | bytes 75272 | tf_op jit(solution)/shard_map/psum | solution.py:31
  200.3 14.0 %psum.29 = f32[97,97]{1,0:T(8,128)S(1)} all-reduce(f32[97,97]{1,0:T(8,128)S(1)} %psum.28), channel_id=1, replica_groups=mesh['row_0'=4,'row_1'=4,'col_0'=4,'col_1'=2] {'row_1'}, use_global_device_ids=true, to_apply=%region_7.9 | all-reduce | flops 9409 | bytes 75272 | tf_op jit(solution)/shard_map/psum | solution.py:31
  214.2 13.1 %psum.30 = f32[97,97]{1,0:T(8,128)S(1)} all-reduce(f32[97,97]{1,0:T(8,128)S(1)} %psum.29), channel_id=1, replica_groups=mesh['row_0'=4,'row_1'=4,'col_0'=4,'col_1'=2] {'col_0'}, use_global_device_ids=true, to_apply=%region_8.10 | all-reduce | flops 9409 | bytes 75272 | tf_op jit(solution)/shard_map/psum | solution.py:31
  227.3 17.2 %psum.31 = f32[97,97]{1,0:T(8,128)S(1)} all-reduce(f32[97,97]{1,0:T(8,128)S(1)} %psum.30), channel_id=1, replica_groups=mesh['row_0'=4,'row_1'=4,'col_0'=4,'col_1'=2] {'col_1'}, use_global_device_ids=true, to_apply=%region_9.11 | all-reduce | flops 9409 | bytes 75272 | tf_op jit(solution)/shard_map/psum | solution.py:31
  244.6 190.3 %while.45 = (s32[]{:T(128)}, f32[97,97]{1,0:T(8,128)S(1)}, f32[97,97]{0,1:T(8,128)S(1)}, s32[]{:T(128)}, s32[]{:T(128)}) while((s32[]{:T(128)}, f32[97,97]{1,0:T(8,128)S(1)}, f32[97,97]{0,1:T(8,128)S(1)}, s32[]{:T(128)}, s32[]{:T(128)}) %tuple.134), condition=%wide.region_12.14_spmd.clone.clone, body=%wide.region_10.13_spmd.clone.clone.sunk | while | flops 113782 | bytes 58617 | solution.py:68
  244.6 0.8 fusion.69
  246.5 0.8 fusion.69
  248.4 0.8 fusion.69
  435.2 246.2 %while.46 = (s32[]{:T(128)}, f32[96]{0:T(128)S(1)}, f32[96]{0:T(128)S(1)}, f32[96,96]{1,0:T(8,128)S(1)}, s32[]{:T(128)}, /*index=5*/s32[]{:T(128)}, s32[]{:T(128)}, s32[]{:T(128)}) while((s32[]{:T(128)}, f32[96]{0:T(128)S(1)}, f32[96]{0:T(128)S(1)}, f32[96,96]{1,0:T(8,128)S(1)}, s32[]{:T(128)}, /*index=5*/s32[]{:T(128)}, ...), condition=%wide.region_16.18_spmd.clone, body=%wide.region_13.17_spmd.clone.sunk | while | flops 1062 | bytes 2122 | solution.py:84
  (655 shorter events, 193.0 us)
Async XLA Ops:
  0.6 184.5 %copy-start = (f32[96]{0:T(128)S(1)}, f32[96]{0:T(128)}, u32[]{:S(2)}) copy-start(f32[96]{0:T(128)} %param.32) | copy-start | bytes 1156
  0.6 7.2 %copy-start.6 = (pred[8,160]{1,0:T(8,128)(4,1)S(1)}, pred[8,160]{1,0:T(8,128)(4,1)}, u32[]{:S(2)}) copy-start(pred[8,160]{1,0:T(8,128)(4,1)} %constant.158.clone) | copy-start | bytes 3844
  0.7 7.3 %copy-start.7 = (s32[160]{0:T(256)S(1)}, s32[160]{0:T(256)}, u32[]{:S(2)}) copy-start(s32[160]{0:T(256)} %constant.159.clone) | copy-start | bytes 1924
  0.7 7.2 %copy-start.8 = (s32[8]{0:T(128)S(1)}, s32[8]{0:T(128)}, u32[]{:S(2)}) copy-start(s32[8]{0:T(128)} %param.30) | copy-start | bytes 100
  4.8 12.0 %copy-start.3 = (f32[5,5,512]{2,1,0:T(8,128)S(1)}, f32[5,5,512]{2,1,0:T(8,128)}, u32[]{:S(2)}) copy-start(f32[5,5,512]{2,1,0:T(8,128)} %param.23) | copy-start | bytes 153604
  10.2 156.7 %collective-permute-start = (bf16[1,5,96,48]{2,1,3,0:T(8,128)(2,1)}, bf16[1,5,96,48]{2,1,3,0:T(8,128)(2,1)}, u32[]{:S(2)}, u32[]{:S(2)}) collective-permute-start(bf16[1,5,96,48]{2,1,3,0:T(8,128)(2,1)} %maximum_bitcast_fusion), channel_id=1, source_target_pairs={{8,0},{16,8},{24,16},{32,24},{40,32},{48,40},{56,48},{64,56},{72,6... | collective-permute-start | bytes 138248 | tf_op jit(solution)/shard_map/ppermute | solution.py:25
  11.5 157.0 %collective-permute-start.1 = (bf16[1,5,96,48]{2,1,3,0:T(8,128)(2,1)S(1)}, bf16[1,5,96,48]{2,1,3,0:T(8,128)(2,1)}, u32[]{:S(2)}, u32[]{:S(2)}) collective-permute-start(bf16[1,5,96,48]{2,1,3,0:T(8,128)(2,1)S(1)} %maximum_bitcast_fusion.1), channel_id=1, source_target_pairs={{0,8},{8,16},{16,24},{24,32},{32,40},{40,48},{48,56},{56,64},{64,7... | collective-permute-start | bytes 138248 | tf_op jit(solution)/shard_map/ppermute | solution.py:22
  18.8 3.8 copy-start.5
  170.1 7.1 %collective-permute-start.2 = (bf16[1,5,96,48]{2,1,3,0:T(8,128)(2,1)S(1)}, bf16[1,5,96,48]{2,1,3,0:T(8,128)(2,1)S(1)}, u32[]{:S(2)}, u32[]{:S(2)}) collective-permute-start(bf16[1,5,96,48]{2,1,3,0:T(8,128)(2,1)S(1)} %maximum_bitcast_fusion.2), channel_id=1, source_target_pairs={{1,0},{2,1},{3,2},{4,3},{5,4},{6,5},{7,6},{9,8},{10,9},{11,10},{12... | collective-permute-start | bytes 138248 | tf_op jit(solution)/shard_map/ppermute | solution.py:25
  173.4 5.2 collective-permute-start.3
  178.7 6.8 %copy-start.4 = (f32[5,512]{1,0:T(8,128)S(1)}, f32[5,512]{1,0:T(8,128)}, u32[]{:S(2)}) copy-start(f32[5,512]{1,0:T(8,128)} %param.33) | copy-start | bytes 30724
  185.2 496.7 %copy-start.1 = (bf16[5,96,512]{2,1,0:T(8,128)(2,1)}, bf16[5,96,512]{2,1,0:T(8,128)(2,1)S(1)}, u32[]{:S(2)}) copy-start(bf16[5,96,512]{2,1,0:T(8,128)(2,1)S(1)} %copy.44) | copy-start | bytes 1474564
  435.0 246.9 %copy-start.2 = (f32[97,97]{0,1:T(8,128)}, f32[97,97]{0,1:T(8,128)S(1)}, u32[]{:S(2)}) copy-start(f32[97,97]{0,1:T(8,128)S(1)} %copy.47) | copy-start | bytes 112912
where the time goes:
time: 687 us; the launch traced here: 682 us
  loops' own time  254 us (37%)
  other arithmetic  148 us (22%)
  matrix products  114 us (17%)
  local copies, waits for them, and re-layouts  91.1 us (13%)
  blocking collectives  58.6 us (9%)
  starting transfers between devices  13.3 us (2%)
    another operation x1, loops' own time, upper_solve(): return lax.fori_loop(0, order, row_step, jnp.zeros_like(rhs))  183 us
    dot_general x97, matrix products, column_step(): jnp.dot(lower, row_vector, precision=lax.Precision.HIGHEST)  77.9 us
    another operation x1, loops' own time, upper_cholesky(): lower = lax.fori_loop(0, order, column_step, jnp.zeros_like(matrix))  70.2 us
    reduce_sum x96, other arithmetic, row_step(): pivot = jnp.sum(jnp.where(indices == place, upper_row, 0.0))  61.6 us
    psum x4, blocking collectives, one_axis_at_a_time(): return functools.reduce(lax.psum, axes, x)  58.6 us
    scatter-add x4, other arithmetic, face_step(): image_sum = image_sum.at[:, :, face_pair[0]].add(to_left)  33.2 us
    scatter-add x4, other arithmetic, face_step(): return image_sum.at[:, :, face_pair[1]].add(to_right)  33.2 us
    dynamic_update_slice x97, local copies, waits for them, and re-layouts, column_step(): lax.dynamic_update_slice_in_dim(lower, new_column[:, None], column, 1)  30.1 us
  transfers between devices with their start and end apart: 4, of which 2 were waited for; matrix products, arithmetic and copies ran while one was open for 22% of the time, Pallas kernels for 0%

commit v1 on v0

v1 whole, which is shorter than its diff:
```python
import functools

import jax
import jax.numpy as jnp
from jax import lax
from jax.experimental import pallas as pl
from jax.experimental.pallas import tpu as pltpu
from jax.sharding import Mesh
from jax.sharding import PartitionSpec as P

ROW = ("row_0", "row_1")
COL = ("col_0", "col_1")
ROW_COL = ROW + COL
F = 5
K = 96
C = 512
N = 1024
S = 160
FK = F * K
HALF = FK // 2
BF = jnp.bfloat16
F32 = jnp.float32
VMEM_LIMIT = 48 * 1024 * 1024


def vmem(count):
    return [pl.BlockSpec(memory_space=pltpu.VMEM)] * count


def smem(count):
    return [pl.BlockSpec(memory_space=pltpu.SMEM)] * count


def one_hot(row):
    cells = lax.broadcasted_iota(jnp.int32, (C, row.shape[1]), 0)
    return jnp.where(cells == row, 1.0, 0.0).astype(BF)


def dot_nn(a, b):
    return lax.dot_general(a, b, (((1,), (0,)), ((), ())), preferred_element_type=F32)


def dot_nt(a, b):
    return lax.dot_general(a, b, (((1,), (1,)), ((), ())), preferred_element_type=F32)


def send_order(x, fill):
    def pad(width):
        return jnp.full(x.shape[:-1] + (width,), fill, x.dtype)

    return jnp.concatenate(
        [
            x[..., 0:32], x[..., 128:136], x[..., 136:144], pad(16),
            x[..., 32:64], x[..., 152:160], x[..., 144:152], pad(16),
            x[..., 64:96], pad(32),
            x[..., 96:128], pad(32),
        ],
        axis=-1,
    )


def receive_order(x):
    def pad(width):
        return jnp.full(x.shape[:-1] + (width,), -1, x.dtype)

    return jnp.concatenate(
        [
            x[..., 0:32], pad(32),
            x[..., 32:64], pad(32),
            x[..., 64:96], x[..., 128:136], x[..., 144:152], pad(16),
            x[..., 96:128], x[..., 152:160], x[..., 136:144], pad(16),
        ],
        axis=-1,
    )


def ghost_kernel(count_ref, basis_ref, cell_ref, jac_ref, minus_ref, plus_ref, left_ref, right_ref, val):
    lane = lax.broadcasted_iota(jnp.int32, (1, 256), 1)
    spot = lane % 64
    side = lane // 64
    limit = jnp.zeros((1, 256), jnp.int32)
    for place in range(4):
        limit = jnp.where((side == place) & (spot < 32), count_ref[place], limit)
    for place, at, block in ((0, 32, 4), (0, 40, 5), (1, 32, 7), (1, 40, 6)):
        inside = (side == place) & (spot >= at) & (spot < at + 8)
        limit = jnp.where(inside, count_ref[block] + at, limit)
    index = send_order(cell_ref[...], -1)
    index = jnp.where(spot < limit, index, -1)
    hot = one_hot(index)
    taken = dot_nn(basis_ref[...], hot)
    for f in range(F):
        val[f] = taken[f * K : (f + 1) * K]
    low = lax.broadcasted_iota(jnp.int32, (1, 128), 1) < 64
    parts = []
    for g in range(F):
        jac = send_order(jac_ref[g], 0.0)
        total = jac[0:1] * val[0]
        for f in range(1, F):
            total = total + jac[f : f + 1] * val[f]
        parts.append(total)
    full = jnp.concatenate(parts, axis=0)
    for tile, first, second in ((0, minus_ref, plus_ref), (1, left_ref, right_ref)):
        wide = full[:, tile * 128 : (tile + 1) * 128]
        top, bottom = wide[:HALF], wide[HALF:]
        first[...] = jnp.where(low, top, pltpu.roll(bottom, 64, 1)).astype(BF)
        second[...] = jnp.where(low, pltpu.roll(top, 64, 1), bottom).astype(BF)


def ghost_call(counts, basis, cells, jacobian):
    message = jax.ShapeDtypeStruct((HALF, 128), BF)
    return pl.pallas_call(
        ghost_kernel,
        out_shape=(message,) * 4,
        in_specs=smem(1) + vmem(3),
        out_specs=tuple(vmem(4)),
        scratch_shapes=[pltpu.VMEM((F, K, 256), F32)],
        compiler_params=pltpu.CompilerParams(vmem_limit_bytes=VMEM_LIMIT),
        name="ghost",
    )(counts, basis, cells, jacobian)


BLOCK = 256
BLOCKS = N // BLOCK
CHUNK = 32


def face_kernel(nu_ref, basis_ref, diag_ref, pair_ref, jac_ref, flag_ref, out_ref, hot, got, add):
    basis = basis_ref[...]
    for block in range(BLOCKS):
        lanes = slice(block * BLOCK, (block + 1) * BLOCK)
        hot[block, :, :BLOCK] = one_hot(pair_ref[0:1, lanes])
        hot[block, :, BLOCK:] = one_hot(pair_ref[1:2, lanes])
        got[block] = dot_nn(basis, hot[block])
        for tile in range(BLOCK // 128):
            here = slice(block * BLOCK + tile * 128, block * BLOCK + (tile + 1) * 128)
            at_a = slice(tile * 128, (tile + 1) * 128)
            at_b = slice(BLOCK + tile * 128, BLOCK + (tile + 1) * 128)
            flag = flag_ref[0:1, here].astype(F32)
            for start in range(0, K, CHUNK):
                a = [got[block, f * K + start : f * K + start + CHUNK, at_a] for f in range(F)]
                b = [got[block, f * K + start : f * K + start + CHUNK, at_b] for f in range(F)]
                for g in range(F):
                    damp = (nu_ref[g] * flag) * (a[g] - b[g])
                    to_a, to_b = damp, -damp
                    for f in range(F):
                        to_a = to_a + jac_ref[0, g, f : f + 1, here] * b[f]
                        to_b = to_b + jac_ref[1, g, f : f + 1, here] * a[f]
                    rows = slice(g * K + start, g * K + start + CHUNK)
                    add[block, rows, at_a] = to_a.astype(BF)
                    add[block, rows, at_b] = to_b.astype(BF)
    for tile in range(C // 128):
        here = slice(tile * 128, (tile + 1) * 128)
        for start in range(0, K, CHUNK):
            v = [basis_ref[f * K + start : f * K + start + CHUNK, here].astype(F32) for f in range(F)]
            for g in range(F):
                total = diag_ref[g, 0:1, here] * v[0]
                for f in range(1, F):
                    total = total + diag_ref[g, f : f + 1, here] * v[f]
                out_ref[g * K + start : g * K + start + CHUNK, here] = total
    for block in range(BLOCKS):
        out_ref[...] += dot_nt(add[block], hot[block])


def face_call(nu, basis, diag, pair, jacobian, flags):
    return pl.pallas_call(
        face_kernel,
        out_shape=jax.ShapeDtypeStruct((FK, C), F32),
        in_specs=smem(1) + vmem(5),
        out_specs=vmem(1)[0],
        scratch_shapes=[
            pltpu.VMEM((BLOCKS, C, 2 * BLOCK), BF),
            pltpu.VMEM((BLOCKS, FK, 2 * BLOCK), F32),
            pltpu.VMEM((BLOCKS, FK, 2 * BLOCK), BF),
        ],
        compiler_params=pltpu.CompilerParams(vmem_limit_bytes=VMEM_LIMIT),
        cost_estimate=pl.CostEstimate(flops=4_000_000_000, bytes_accessed=2_000_000, transcendentals=0),
        name="faces",
    )(nu, basis, diag, pair, jacobian, flags)


ROWS = 112


def finish_kernel(row_scale, image_ref, above_ref, below_ref, right_ref, left_ref, cell_ref, coord_ref, base_ref,
                  test_ref, gram_ref, arrive, stack):
    low = lax.broadcasted_iota(jnp.int32, (1, 128), 1) < 64
    for tile, first, second in ((0, above_ref, below_ref), (1, right_ref, left_ref)):
        here = slice(tile * 128, (tile + 1) * 128)
        one, two = first[...].astype(F32), second[...].astype(F32)
        arrive[:HALF, here] = jnp.where(low, one, pltpu.roll(two, 64, 1)).astype(BF)
        arrive[HALF:, here] = jnp.where(low, pltpu.roll(one, 64, 1), two).astype(BF)
    hot = one_hot(receive_order(cell_ref[...]))
    image = image_ref[...] + dot_nt(arrive[...], hot)
    test = image.astype(BF)
    coord = coord_ref[...]
    high = coord.astype(BF)
    small = (coord - high.astype(F32)).astype(BF)
    row = lax.broadcasted_iota(jnp.int32, (16, K), 0)
    zero = jnp.zeros((16, K), F32)
    pair = jnp.where(row == 0, high.astype(F32), jnp.where(row == 1, small.astype(F32), zero)).astype(BF)
    first_row = lax.broadcasted_iota(jnp.int32, (16, C), 0) == 0
    for f in range(F):
        part = test[f * K : (f + 1) * K]
        here = slice(f * C, (f + 1) * C)
        test_ref[f] = part
        stack[:K, here] = part
        product = dot_nn(pair, part)
        value = base_ref[f : f + 1] + row_scale * (product[0:1] + product[1:2])
        stack[K:ROWS, here] = jnp.where(first_row, value, 0.0).astype(BF)
    whole = stack[...]
    gram = dot_nt(whole, whole) * (row_scale * row_scale)
    gram_ref[...] = jnp.concatenate([gram[:104], jnp.zeros((104, 128 - ROWS), F32)], axis=1)


def finish_call(row_scale, image, above, below, right, left, cells, coords, base):
    return pl.pallas_call(
        functools.partial(finish_kernel, row_scale),
        out_shape=(jax.ShapeDtypeStruct((F, K, C), BF), jax.ShapeDtypeStruct((104, 128), F32)),
        in_specs=vmem(8),
        out_specs=tuple(vmem(2)),
        scratch_shapes=[pltpu.VMEM((FK, 256), BF), pltpu.VMEM((ROWS, F * C), BF)],
        compiler_params=pltpu.CompilerParams(vmem_limit_bytes=VMEM_LIMIT),
        name="finish",
    )(image, above, below, right, left, cells, coords, base)


TILES = 13


def solve_kernel(row_scale, first_ref, second_ref, factor_ref, step_ref, work):
    work[...] = first_ref[...] + second_ref[...]
    lane = lax.broadcasted_iota(jnp.int32, (8, 128), 1)
    sub = lax.broadcasted_iota(jnp.int32, (8, 128), 0)

    def spread_row(tile, p):
        return jnp.broadcast_to(tile[p : p + 1], (8, 128))

    def spread_lane(tile, j):
        return jnp.broadcast_to(tile[:, j : j + 1], (8, 128))

    tiles = [work[8 * t : 8 * t + 8] for t in range(TILES)]
    for panel in range(12):
        start = 8 * panel
        here = tiles[panel]
        columns = [[spread_lane(tiles[t], start + p) for p in range(8)] for t in range(TILES)]
        rows = [spread_row(here, p) for p in range(8)]
        d = {(p, q): spread_row(columns[panel][q], p) for p in range(8) for q in range(p, 8)}
        m = {}
        inverse = []
        for p in range(8):
            recip = 1.0 / d[p, p]
            inverse.append(recip)
            for q in range(p + 1, 8):
                m[p, q] = d[p, q] * recip
            for q in range(p + 1, 8):
                rows[q] = rows[q] - m[p, q] * rows[p]
                for r in range(q, 8):
                    d[q, r] = d[q, r] - m[p, q] * d[p, r]
        out = jnp.zeros((8, 128), F32)
        for p in range(8):
            out = jnp.where(sub == p, rows[p] * lax.rsqrt(d[p, p]), out)
        out = jnp.where(lane >= start + sub, out, 0.0)
        factor_ref[start : start + 8, :] = out[:, :97]
        for p in range(7, -1, -1):
            rows[p] = rows[p] * inverse[p]
            for q in range(p + 1, 8):
                rows[p] = rows[p] - m[p, q] * rows[q]
        order = [panel + 1] + [t for t in range(TILES) if t not in (panel, panel + 1)]
        for t in order:
            product = [columns[t][p] * rows[p] for p in range(8)]
            while len(product) > 1:
                product = [product[i] + product[i + 1] for i in range(0, len(product), 2)]
            tiles[t] = tiles[t] - product[0]
        new = rows[0]
        for p in range(1, 8):
            new = jnp.where(sub == p, rows[p], new)
        tiles[panel] = new
    last = tiles[12]
    factor_ref[96:97, :] = jnp.where(lane[:1] == 96, jnp.sqrt(last[0:1]), 0.0)[:, :97]
    step = jnp.zeros((1, 128), F32)
    for t in range(12):
        column = spread_lane(tiles[t], 96)
        step = step + jnp.sum(jnp.where(lane == 8 * t + sub, column, 0.0), axis=0, keepdims=True)
    step_ref[...] = step[:, :96] * (-1.0 / row_scale)


def solve_call(row_scale, first, second):
    return pl.pallas_call(
        functools.partial(solve_kernel, row_scale),
        out_shape=(jax.ShapeDtypeStruct((97, 97), F32), jax.ShapeDtypeStruct((1, 96), F32)),
        in_specs=vmem(2),
        out_specs=tuple(vmem(2)),
        scratch_shapes=[pltpu.VMEM((104, 128), F32)],
        compiler_params=pltpu.CompilerParams(vmem_limit_bytes=VMEM_LIMIT),
        name="solve",
    )(first, second)


def shift_up(x, axis):
    count = lax.axis_size(axis)
    return lax.ppermute(x, axis, [(i, i + 1) for i in range(count - 1)])


def shift_down(x, axis):
    count = lax.axis_size(axis)
    return lax.ppermute(x, axis, [(i + 1, i) for i in range(count - 1)])


def swap(x, axis, step):
    count = lax.axis_size(axis)
    return lax.ppermute(x, axis, [(i, i ^ step) for i in range(count)])


def local(
    reduced_basis,
    cell_jacobian,
    face_cells,
    face_jacobian,
    limiter_flags,
    viscosity,
    ghost_cells,
    ghost_jacobian,
    ghost_counts,
    receive_cells,
    coordinates,
    base_residual,
):
    devices = lax.axis_size(ROW) * lax.axis_size(COL)
    row_scale = (F * C * devices) ** (-0.5)
    basis = reduced_basis.reshape(FK, C)
    minus, plus, left, right = ghost_call(
        ghost_counts, basis, ghost_cells.reshape(1, S), ghost_jacobian
    )
    above = shift_down(minus, ROW)
    below = shift_up(plus, ROW)
    spot = lax.broadcasted_iota(jnp.int32, (HALF, 128), 1) % 64
    at_32 = (spot >= 32) & (spot < 40)
    at_40 = (spot >= 40) & (spot < 48)
    to_left = jnp.where(at_32, above, jnp.where(at_40, below, left))
    to_right = jnp.where(at_32, below, jnp.where(at_40, above, right))
    from_right = shift_down(to_left, COL)
    from_left = shift_up(to_right, COL)
    image = face_call(
        viscosity, basis, cell_jacobian, face_cells, face_jacobian, limiter_flags.reshape(1, N)
    )
    test, gram = finish_call(
        row_scale, image, above, below, from_right, from_left,
        receive_cells.reshape(1, S), coordinates.reshape(1, K), base_residual,
    )
    gram = gram + swap(gram, "col_1", 1)
    for axis in ("col_0", "row_1", "row_0"):
        one, two, three = (swap(gram, axis, k) for k in (1, 2, 3))
        first, second = gram + one, two + three
        gram = first + second
    factor, step = solve_call(row_scale, first, second)
    return (test, factor, step.reshape(K))


def solution(mesh):
    torus = Mesh(mesh.devices.reshape(4, 4, 4, 2), ("row_0", "row_1", "col_0", "col_1"))
    in_specs = (
        P(None, None, ROW_COL),
        P(None, None, ROW_COL),
        P(None, ROW_COL),
        P(None, None, None, ROW_COL),
        P(ROW_COL),
        P(),
        P(ROW_COL),
        P(None, None, ROW_COL),
        P(ROW_COL),
        P(ROW_COL),
        P(),
        P(None, ROW_COL),
    )
    out_specs = (P(None, None, ROW_COL), P(), P())
    return jax.shard_map(local, mesh=torus, in_specs=in_specs, out_specs=out_specs, check_vma=False)
```

time: 687 us -> 62.7 us (0.09)
  the two profiles are of different devices: /device:TPU:1 before, /device:TPU:0 now
where the time goes in v1:
time: 62.7 us; the launch traced here: 62.4 us
  starting transfers between devices  29.2 us (47%)
  waiting for transfers between devices  16.7 us (27%)
  Pallas kernels  12.2 us (19%)
  local copies, waits for them, and re-layouts  3.25 us (5%)
  between operations  0.87 us (1%)
    ppermute x10, starting transfers between devices, swap(): return lax.ppermute(x, axis, [(i, i ^ step) for i in range(count)])  20.7 us
    ppermute x10, waiting for transfers between devices, swap(): return lax.ppermute(x, axis, [(i, i ^ step) for i in range(count)])  15 us
    ppermute x2, starting transfers between devices, shift_up(): return lax.ppermute(x, axis, [(i, i + 1) for i in range(count - 1)])  5.84 us
    pallas_call x1, Pallas kernels, solve_call(): pl.pallas_call(functools.partial(solve_kernel, row_scale), out_shape=(jax...  5.16 us
    pallas_call x1, Pallas kernels, face_call(): pl.pallas_call(face_kernel, out_shape=jax.ShapeDtypeStruct((FK, C), F32),...  4.53 us
    unnamed x27, local copies, waits for them, and re-layouts  3.25 us
    ppermute x2, starting transfers between devices, shift_down(): return lax.ppermute(x, axis, [(i + 1, i) for i in range(count - 1)])  2.72 us
    ppermute x2, waiting for transfers between devices, shift_up(): return lax.ppermute(x, axis, [(i, i + 1) for i in range(count - 1)])  1.59 us
  transfers between devices with their start and end apart: 14, of which 9 were waited for; matrix products, arithmetic and copies ran while one was open for 0% of the time, Pallas kernels for 7%

profile of v1, /device:TPU:0, one launch (start us, length us, event | category | flops | bytes accessed | tf_op | source)
XLA Modules:
  0.0 62.4 jit_solution(14667688106328612270)
XLA Ops:
  0.6 0.0 copy-start.4
  0.6 0.0 copy-start.6
  0.7 0.7 %copy-done.4 = s32[160]{0:T(256)S(1)} copy-done((s32[160]{0:T(256)S(1)}, s32[160]{0:T(256)}, u32[]{:S(2)}) %copy-start.4) | copy-done | bytes 664
  1.3 0.0 copy-done.6
  1.3 0.0 copy-start
  1.3 1.0 %copy-done = bf16[5,96,512]{2,1,0:T(8,128)(2,1)S(1)} copy-done((bf16[5,96,512]{2,1,0:T(8,128)(2,1)S(1)}, bf16[5,96,512]{2,1,0:T(8,128)(2,1)}, u32[]{:S(2)}) %copy-start) | copy-done | bytes 491544
  2.3 0.0 copy-start.2
  2.3 0.8 %copy-done.2 = f32[5,5,160]{2,1,0:T(8,128)S(1)} copy-done((f32[5,5,160]{2,1,0:T(8,128)S(1)}, f32[5,5,160]{2,1,0:T(8,128)}, u32[]{:S(2)}) %copy-start.2) | copy-done | bytes 16024
  3.1 0.0 copy-start.12
  3.1 1.0 %ghost.1 = (bf16[240,128]{1,0:T(8,128)(2,1)S(1)}, bf16[240,128]{1,0:T(8,128)(2,1)S(1)}, bf16[240,128]{1,0:T(8,128)(2,1)S(1)}, bf16[240,128]{1,0:T(8,128)(2,1)S(1)}) custom-call(s32[8]{0:T(128)S(1)} %copy-done.6, bf16[480,512]{1,0:T(8,128)(2,1)S(1)} %bitcast.6, s32[1,160]{1,0:T(1,128)S(1)} %bitcast.8, f32[5,5,160]{2,1,0:T(8,128)S(1)} %copy-done.2), custom_call_target="tpu_custom_call" | custom-call | tf_op jit(solution)/shard_map/ghost/pallas_call | solution.py:111
  4.2 0.0 copy-start.1
  4.2 1.4 %collective-permute-start = (bf16[240,128]{1,0:T(8,128)(2,1)S(1)}, bf16[240,128]{1,0:T(8,128)(2,1)S(1)}, u32[]{:S(2)}, u32[]{:S(2)}) collective-permute-start(bf16[240,128]{1,0:T(8,128)(2,1)S(1)} %get-tuple-element.11), channel_id=1, source_target_pairs={{8,0},{16,8},{24,16},{32,24},{40,32},{48,40},{56,48},{64,56},{72,6... | collective-permute-start | bytes 184328 | tf_op jit(solution)/shard_map/ppermute | solution.py:306
  5.6 4.5 %collective-permute-start.1 = (bf16[240,128]{1,0:T(8,128)(2,1)S(1)}, bf16[240,128]{1,0:T(8,128)(2,1)S(1)}, u32[]{:S(2)}, u32[]{:S(2)}) collective-permute-start(bf16[240,128]{1,0:T(8,128)(2,1)S(1)} %get-tuple-element.12), channel_id=1, source_target_pairs={{0,8},{8,16},{16,24},{24,32},{32,40},{40,48},{48,56},{56,64},{64,7... | collective-permute-start | bytes 184328 | tf_op jit(solution)/shard_map/ppermute | solution.py:301
  10.2 0.0 copy-done.12
  10.2 0.1 copy.15.jac_ref
  10.3 0.1 collective-permute-done.above_ref
  10.4 1.6 %collective-permute-done.1.below_ref = bf16[240,128]{1,0:T(8,128)(2,1)S(1)} collective-permute-done((bf16[240,128]{1,0:T(8,128)(2,1)S(1)}, bf16[240,128]{1,0:T(8,128)(2,1)S(1)}, u32[]{:S(2)}, u32[]{:S(2)}) %collective-permute-start.1) | collective-permute-done | bytes 61472 | tf_op jit(solution)/shard_map/ppermute | solution.py:301
  12.0 0.0 copy-start.8
  12.0 0.0 copy-start.9
  12.1 0.0 copy-start.10
  12.1 1.3 %collective-permute-start.3 = (bf16[240,128]{1,0:T(8,128)(2,1)S(1)}, bf16[240,128]{1,0:T(8,128)(2,1)S(1)}, u32[]{:S(2)}, u32[]{:S(2)}) collective-permute-start(bf16[240,128]{1,0:T(8,128)(2,1)S(1)} %get-tuple-element.19), channel_id=1, source_target_pairs={{0,1},{1,2},{2,3},{3,4},{4,5},{5,6},{6,7},{8,9},{9,10},{10,11},{11... | collective-permute-start | bytes 184328 | tf_op jit(solution)/shard_map/ppermute | solution.py:301
  13.4 0.0 copy-start.11
  13.4 1.3 %collective-permute-start.2 = (bf16[240,128]{1,0:T(8,128)(2,1)S(1)}, bf16[240,128]{1,0:T(8,128)(2,1)S(1)}, u32[]{:S(2)}, u32[]{:S(2)}) collective-permute-start(bf16[240,128]{1,0:T(8,128)(2,1)S(1)} %get-tuple-element.20), channel_id=1, source_target_pairs={{1,0},{2,1},{3,2},{4,3},{5,4},{6,5},{7,6},{9,8},{10,9},{11,10},{12... | collective-permute-start | bytes 184328 | tf_op jit(solution)/shard_map/ppermute | solution.py:306
  14.7 0.0 copy-done.1
  14.7 0.0 copy-done.8
  14.7 0.0 copy-done.9
  14.7 0.0 copy-done.10
  14.7 0.0 copy-done.11
  14.8 0.0 copy-start.3
  14.8 4.5 %faces.1.image_ref = f32[480,512]{1,0:T(8,128)S(1)} custom-call(f32[5]{0:T(128)S(1)} %copy-done.11, bf16[480,512]{1,0:T(8,128)(2,1)S(1)} %bitcast.7, f32[5,5,512]{2,1,0:T(8,128)S(1)} %copy-done.8, s32[2,1024]{1,0:T(2,128)S(1)} %copy-done.9, f32[2,5,5,1024]{3,2,1,0:T(8,128)S(1)} %copy.15.jac_ref, s32[1,1024]{1,0:T(1,128)S(1)} %bitcast.11), custom_call_target="tpu_custom_call" | custom-call | flops 4000000000 | bytes 2000000 | tf_op jit(solution)/shard_map/faces/pallas_call | solution.py:165
  19.3 0.0 collective-permute-done.3.left_ref
  19.3 0.0 collective-permute-done.2.right_ref
  19.3 0.0 copy-start.5
  19.3 0.0 copy-start.7
  19.3 0.0 copy-done.3
  19.4 0.6 %copy-done.5 = s32[160]{0:T(256)S(1)} copy-done((s32[160]{0:T(256)S(1)}, s32[160]{0:T(256)}, u32[]{:S(2)}) %copy-start.5) | copy-done | bytes 664
  20.0 0.0 copy-done.7
  20.0 1.5 %finish.1 = (bf16[5,96,512]{2,1,0:T(8,128)(2,1)}, f32[104,128]{1,0:T(8,128)S(1)}) custom-call(f32[480,512]{1,0:T(8,128)S(1)} %faces.1.image_ref, bf16[240,128]{1,0:T(8,128)(2,1)S(1)} %collective-permute-done.above_ref, bf16[240,128]{1,0:T(8,128)(2,1)S(1)} %collective-permute-done.1.below_ref, bf16[240,128]{1,0:T(8,128)(2,1)S(1)} %collective-permute-done.2.right_ref, ...), custom_call_target="tpu_custom_call" | custom-call | tf_op jit(solution)/shard_map/finish/pallas_call | solution.py:216
  21.5 3.4 %collective-permute-start.4 = (f32[104,128]{1,0:T(8,128)S(1)}, f32[104,128]{1,0:T(8,128)S(1)}, u32[]{:S(2)}, u32[]{:S(2)}) collective-permute-start(f32[104,128]{1,0:T(8,128)S(1)} %get-tuple-element.16), channel_id=1, source_target_pairs={{0,1},{1,0},{2,3},{3,2},{4,5},{5,4},{6,7},{7,6},{8,9},{9,8},{10,11... | collective-permute-start | bytes 159752 | tf_op jit(solution)/shard_map/ppermute | solution.py:311
  24.9 0.9 %collective-permute-done.4 = f32[104,128]{1,0:T(8,128)S(1)} collective-permute-done((f32[104,128]{1,0:T(8,128)S(1)}, f32[104,128]{1,0:T(8,128)S(1)}, u32[]{:S(2)}, u32[]{:S(2)}) %collective-permute-start.4) | collective-permute-done | bytes 53280 | tf_op jit(solution)/shard_map/ppermute | solution.py:311
  25.8 4.2 %collective-permute-start.7 = (f32[104,128]{1,0:T(8,128)S(1)}, f32[104,128]{1,0:T(8,128)S(1)}, u32[]{:S(2)}, u32[]{:S(2)}) collective-permute-start(f32[104,128]{1,0:T(8,128)S(1)} %add.41), channel_id=1, source_target_pairs={{0,6},{2,4},{4,2},{6,0},{1,7},{3,5},{5,3},{7,1},{8,14},{10,12},{12... | collective-permute-start | bytes 159752 | tf_op jit(solution)/shard_map/ppermute | solution.py:311
  29.9 0.0 collective-permute-start.6
  29.9 0.9 %collective-permute-start.5 = (f32[104,128]{1,0:T(8,128)S(1)}, f32[104,128]{1,0:T(8,128)S(1)}, u32[]{:S(2)}, u32[]{:S(2)}) collective-permute-start(f32[104,128]{1,0:T(8,128)S(1)} %add.41), channel_id=1, source_target_pairs={{0,2},{2,0},{4,6},{6,4},{1,3},{3,1},{5,7},{7,5},{8,10},{10,8},{12,... | collective-permute-start | bytes 159752 | tf_op jit(solution)/shard_map/ppermute | solution.py:311
  30.9 1.3 %collective-permute-done.7 = f32[104,128]{1,0:T(8,128)S(1)} collective-permute-done((f32[104,128]{1,0:T(8,128)S(1)}, f32[104,128]{1,0:T(8,128)S(1)}, u32[]{:S(2)}, u32[]{:S(2)}) %collective-permute-start.7) | collective-permute-done | bytes 53280 | tf_op jit(solution)/shard_map/ppermute | solution.py:311
  32.2 3.4 %collective-permute-done.6 = f32[104,128]{1,0:T(8,128)S(1)} collective-permute-done((f32[104,128]{1,0:T(8,128)S(1)}, f32[104,128]{1,0:T(8,128)S(1)}, u32[]{:S(2)}, u32[]{:S(2)}) %collective-permute-start.6) | collective-permute-done | bytes 53280 | tf_op jit(solution)/shard_map/ppermute | solution.py:311
  35.6 0.0 collective-permute-done.5
  35.6 5.2 %collective-permute-start.10 = (f32[104,128]{1,0:T(8,128)S(1)}, f32[104,128]{1,0:T(8,128)S(1)}, u32[]{:S(2)}, u32[]{:S(2)}) collective-permute-start(f32[104,128]{1,0:T(8,128)S(1)} %add_add_fusion.1), channel_id=1, source_target_pairs={{0,24},{8,16},{16,8},{24,0},{1,25},{9,17},{17,9},{25,1},{2,26},{10... | collective-permute-start | bytes 159752 | tf_op jit(solution)/shard_map/ppermute | solution.py:311
  40.8 0.0 collective-permute-start.9
  40.8 0.9 %collective-permute-start.8 = (f32[104,128]{1,0:T(8,128)S(1)}, f32[104,128]{1,0:T(8,128)S(1)}, u32[]{:S(2)}, u32[]{:S(2)}) collective-permute-start(f32[104,128]{1,0:T(8,128)S(1)} %add_add_fusion.1), channel_id=1, source_target_pairs={{0,8},{8,0},{16,24},{24,16},{1,9},{9,1},{17,25},{25,17},{2,10},{10... | collective-permute-start | bytes 159752 | tf_op jit(solution)/shard_map/ppermute | solution.py:311
  41.7 1.2 %collective-permute-done.10 = f32[104,128]{1,0:T(8,128)S(1)} collective-permute-done((f32[104,128]{1,0:T(8,128)S(1)}, f32[104,128]{1,0:T(8,128)S(1)}, u32[]{:S(2)}, u32[]{:S(2)}) %collective-permute-start.10) | collective-permute-done | bytes 53280 | tf_op jit(solution)/shard_map/ppermute | solution.py:311
  42.9 3.5 %collective-permute-done.9 = f32[104,128]{1,0:T(8,128)S(1)} collective-permute-done((f32[104,128]{1,0:T(8,128)S(1)}, f32[104,128]{1,0:T(8,128)S(1)}, u32[]{:S(2)}, u32[]{:S(2)}) %collective-permute-start.9) | collective-permute-done | bytes 53280 | tf_op jit(solution)/shard_map/ppermute | solution.py:311
  46.4 0.0 collective-permute-done.8
  46.4 3.0 %collective-permute-start.11 = (f32[104,128]{1,0:T(8,128)S(1)}, f32[104,128]{1,0:T(8,128)S(1)}, u32[]{:S(2)}, u32[]{:S(2)}) collective-permute-start(f32[104,128]{1,0:T(8,128)S(1)} %add_add_fusion), channel_id=1, source_target_pairs={{0,32},{32,0},{64,96},{96,64},{1,33},{33,1},{65,97},{97,65},{2,34}... | collective-permute-start | bytes 159752 | tf_op jit(solution)/shard_map/ppermute | solution.py:311
  49.4 2.1 %collective-permute-start.13 = (f32[104,128]{1,0:T(8,128)S(1)}, f32[104,128]{1,0:T(8,128)S(1)}, u32[]{:S(2)}, u32[]{:S(2)}) collective-permute-start(f32[104,128]{1,0:T(8,128)S(1)} %add_add_fusion), channel_id=1, source_target_pairs={{0,96},{32,64},{64,32},{96,0},{1,97},{33,65},{65,33},{97,1},{2,98}... | collective-permute-start | bytes 159752 | tf_op jit(solution)/shard_map/ppermute | solution.py:311
  51.6 0.9 %collective-permute-start.12 = (f32[104,128]{1,0:T(8,128)S(1)}, f32[104,128]{1,0:T(8,128)S(1)}, u32[]{:S(2)}, u32[]{:S(2)}) collective-permute-start(f32[104,128]{1,0:T(8,128)S(1)} %add_add_fusion), channel_id=1, source_target_pairs={{0,64},{32,96},{64,0},{96,32},{1,65},{33,97},{65,1},{97,33},{2,66}... | collective-permute-start | bytes 159752 | tf_op jit(solution)/shard_map/ppermute | solution.py:311
  52.5 0.0 collective-permute-done.11
  52.5 2.3 %collective-permute-done.13 = f32[104,128]{1,0:T(8,128)S(1)} collective-permute-done((f32[104,128]{1,0:T(8,128)S(1)}, f32[104,128]{1,0:T(8,128)S(1)}, u32[]{:S(2)}, u32[]{:S(2)}) %collective-permute-start.13) | collective-permute-done | bytes 53280 | tf_op jit(solution)/shard_map/ppermute | solution.py:311
  54.8 2.4 %collective-permute-done.12 = f32[104,128]{1,0:T(8,128)S(1)} collective-permute-done((f32[104,128]{1,0:T(8,128)S(1)}, f32[104,128]{1,0:T(8,128)S(1)}, u32[]{:S(2)}, u32[]{:S(2)}) %collective-permute-start.12) | collective-permute-done | bytes 53280 | tf_op jit(solution)/shard_map/ppermute | solution.py:311
  57.2 5.2 %solve.1 = (f32[97,97]{1,0:T(8,128)}, f32[1,96]{1,0:T(1,128)}) custom-call(f32[104,128]{1,0:T(8,128)S(1)} %add.48.first_ref, f32[104,128]{1,0:T(8,128)S(1)} %add.49.second_ref), custom_call_target="tpu_custom_call" | custom-call | tf_op jit(solution)/shard_map/solve/pallas_call | solution.py:288
  (8 shorter events, 0.1 us)
Async XLA Ops:
  0.6 0.7 %copy-start.4 = (s32[160]{0:T(256)S(1)}, s32[160]{0:T(256)}, u32[]{:S(2)}) copy-start(s32[160]{0:T(256)} %param.18) | copy-start | bytes 1924
  0.6 0.7 %copy-start.6 = (s32[8]{0:T(128)S(1)}, s32[8]{0:T(128)}, u32[]{:S(2)}) copy-start(s32[8]{0:T(128)} %count_ref.1) | copy-start | bytes 100
  1.3 1.0 %copy-start = (bf16[5,96,512]{2,1,0:T(8,128)(2,1)S(1)}, bf16[5,96,512]{2,1,0:T(8,128)(2,1)}, u32[]{:S(2)}) copy-start(bf16[5,96,512]{2,1,0:T(8,128)(2,1)} %param.12) | copy-start | bytes 1474564
  2.3 0.8 %copy-start.2 = (f32[5,5,160]{2,1,0:T(8,128)S(1)}, f32[5,5,160]{2,1,0:T(8,128)}, u32[]{:S(2)}) copy-start(f32[5,5,160]{2,1,0:T(8,128)} %jac_ref.2) | copy-start | bytes 48004
  3.1 7.1 %copy-start.12 = (f32[2,5,5,1024]{3,0,2,1:T(2,128)S(1)}, f32[2,5,5,1024]{3,0,2,1:T(2,128)}, u32[]{:S(2)}) copy-start(f32[2,5,5,1024]{3,0,2,1:T(2,128)} %param.15) | copy-start | bytes 614404
  4.2 10.5 %copy-start.1 = (bf16[5,96,512]{2,1,0:T(8,128)(2,1)S(1)}, bf16[5,96,512]{2,1,0:T(8,128)(2,1)}, u32[]{:S(2)}) copy-start(bf16[5,96,512]{2,1,0:T(8,128)(2,1)} %param.12) | copy-start | bytes 1474564
  4.2 6.2 %collective-permute-start = (bf16[240,128]{1,0:T(8,128)(2,1)S(1)}, bf16[240,128]{1,0:T(8,128)(2,1)S(1)}, u32[]{:S(2)}, u32[]{:S(2)}) collective-permute-start(bf16[240,128]{1,0:T(8,128)(2,1)S(1)} %get-tuple-element.11), channel_id=1, source_target_pairs={{8,0},{16,8},{24,16},{32,24},{40,32},{48,40},{56,48},{64,56},{72,6... | collective-permute-start | bytes 184328 | tf_op jit(solution)/shard_map/ppermute | solution.py:306
  5.6 6.4 %collective-permute-start.1 = (bf16[240,128]{1,0:T(8,128)(2,1)S(1)}, bf16[240,128]{1,0:T(8,128)(2,1)S(1)}, u32[]{:S(2)}, u32[]{:S(2)}) collective-permute-start(bf16[240,128]{1,0:T(8,128)(2,1)S(1)} %get-tuple-element.12), channel_id=1, source_target_pairs={{0,8},{8,16},{16,24},{24,32},{32,40},{40,48},{48,56},{56,64},{64,7... | collective-permute-start | bytes 184328 | tf_op jit(solution)/shard_map/ppermute | solution.py:301
  12.0 2.7 %copy-start.8 = (f32[5,5,512]{2,1,0:T(8,128)S(1)}, f32[5,5,512]{2,1,0:T(8,128)}, u32[]{:S(2)}) copy-start(f32[5,5,512]{2,1,0:T(8,128)} %diag_ref.1) | copy-start | bytes 153604
  12.0 2.7 %copy-start.9 = (s32[2,1024]{1,0:T(2,128)S(1)}, s32[2,1024]{1,0:T(2,128)}, u32[]{:S(2)}) copy-start(s32[2,1024]{1,0:T(2,128)} %pair_ref.1) | copy-start | bytes 24580
  12.1 2.7 %copy-start.10 = (s32[1024]{0:T(1024)S(1)}, s32[1024]{0:T(1024)}, u32[]{:S(2)}) copy-start(s32[1024]{0:T(1024)} %param.16) | copy-start | bytes 12292
  12.1 7.2 %collective-permute-start.3 = (bf16[240,128]{1,0:T(8,128)(2,1)S(1)}, bf16[240,128]{1,0:T(8,128)(2,1)S(1)}, u32[]{:S(2)}, u32[]{:S(2)}) collective-permute-start(bf16[240,128]{1,0:T(8,128)(2,1)S(1)} %get-tuple-element.19), channel_id=1, source_target_pairs={{0,1},{1,2},{2,3},{3,4},{4,5},{5,6},{6,7},{8,9},{9,10},{10,11},{11... | collective-permute-start | bytes 184328 | tf_op jit(solution)/shard_map/ppermute | solution.py:301
  13.4 1.4 %copy-start.11 = (f32[5]{0:T(128)S(1)}, f32[5]{0:T(128)}, u32[]{:S(2)}) copy-start(f32[5]{0:T(128)} %nu_ref.1) | copy-start | bytes 64
  13.4 5.9 %collective-permute-start.2 = (bf16[240,128]{1,0:T(8,128)(2,1)S(1)}, bf16[240,128]{1,0:T(8,128)(2,1)S(1)}, u32[]{:S(2)}, u32[]{:S(2)}) collective-permute-start(bf16[240,128]{1,0:T(8,128)(2,1)S(1)} %get-tuple-element.20), channel_id=1, source_target_pairs={{1,0},{2,1},{3,2},{4,3},{5,4},{6,5},{7,6},{9,8},{10,9},{11,10},{12... | collective-permute-start | bytes 184328 | tf_op jit(solution)/shard_map/ppermute | solution.py:306
  14.8 4.6 %copy-start.3 = (f32[5,512]{1,0:T(8,128)S(1)}, f32[5,512]{1,0:T(8,128)}, u32[]{:S(2)}) copy-start(f32[5,512]{1,0:T(8,128)} %base_ref.1) | copy-start | bytes 30724
  19.3 0.7 %copy-start.5 = (s32[160]{0:T(256)S(1)}, s32[160]{0:T(256)}, u32[]{:S(2)}) copy-start(s32[160]{0:T(256)} %param.21) | copy-start | bytes 1924
  19.3 0.7 %copy-start.7 = (f32[96]{0:T(128)S(1)}, f32[96]{0:T(128)}, u32[]{:S(2)}) copy-start(f32[96]{0:T(128)} %param.22) | copy-start | bytes 1156
  21.5 4.3 %collective-permute-start.4 = (f32[104,128]{1,0:T(8,128)S(1)}, f32[104,128]{1,0:T(8,128)S(1)}, u32[]{:S(2)}, u32[]{:S(2)}) collective-permute-start(f32[104,128]{1,0:T(8,128)S(1)} %get-tuple-element.16), channel_id=1, source_target_pairs={{0,1},{1,0},{2,3},{3,2},{4,5},{5,4},{6,7},{7,6},{8,9},{9,8},{10,11... | collective-permute-start | bytes 159752 | tf_op jit(solution)/shard_map/ppermute | solution.py:311
  25.8 6.4 %collective-permute-start.7 = (f32[104,128]{1,0:T(8,128)S(1)}, f32[104,128]{1,0:T(8,128)S(1)}, u32[]{:S(2)}, u32[]{:S(2)}) collective-permute-start(f32[104,128]{1,0:T(8,128)S(1)} %add.41), channel_id=1, source_target_pairs={{0,6},{2,4},{4,2},{6,0},{1,7},{3,5},{5,3},{7,1},{8,14},{10,12},{12... | collective-permute-start | bytes 159752 | tf_op jit(solution)/shard_map/ppermute | solution.py:311
  29.9 5.6 %collective-permute-start.6 = (f32[104,128]{1,0:T(8,128)S(1)}, f32[104,128]{1,0:T(8,128)S(1)}, u32[]{:S(2)}, u32[]{:S(2)}) collective-permute-start(f32[104,128]{1,0:T(8,128)S(1)} %add.41), channel_id=1, source_target_pairs={{0,4},{2,6},{4,0},{6,2},{1,5},{3,7},{5,1},{7,3},{8,12},{10,14},{12... | collective-permute-start | bytes 159752 | tf_op jit(solution)/shard_map/ppermute | solution.py:311
  29.9 5.6 %collective-permute-start.5 = (f32[104,128]{1,0:T(8,128)S(1)}, f32[104,128]{1,0:T(8,128)S(1)}, u32[]{:S(2)}, u32[]{:S(2)}) collective-permute-start(f32[104,128]{1,0:T(8,128)S(1)} %add.41), channel_id=1, source_target_pairs={{0,2},{2,0},{4,6},{6,4},{1,3},{3,1},{5,7},{7,5},{8,10},{10,8},{12,... | collective-permute-start | bytes 159752 | tf_op jit(solution)/shard_map/ppermute | solution.py:311
  35.6 7.3 %collective-permute-start.10 = (f32[104,128]{1,0:T(8,128)S(1)}, f32[104,128]{1,0:T(8,128)S(1)}, u32[]{:S(2)}, u32[]{:S(2)}) collective-permute-start(f32[104,128]{1,0:T(8,128)S(1)} %add_add_fusion.1), channel_id=1, source_target_pairs={{0,24},{8,16},{16,8},{24,0},{1,25},{9,17},{17,9},{25,1},{2,26},{10... | collective-permute-start | bytes 159752 | tf_op jit(solution)/shard_map/ppermute | solution.py:311
  40.8 5.6 %collective-permute-start.9 = (f32[104,128]{1,0:T(8,128)S(1)}, f32[104,128]{1,0:T(8,128)S(1)}, u32[]{:S(2)}, u32[]{:S(2)}) collective-permute-start(f32[104,128]{1,0:T(8,128)S(1)} %add_add_fusion.1), channel_id=1, source_target_pairs={{0,16},{8,24},{16,0},{24,8},{1,17},{9,25},{17,1},{25,9},{2,18},{10... | collective-permute-start | bytes 159752 | tf_op jit(solution)/shard_map/ppermute | solution.py:311
  40.8 5.6 %collective-permute-start.8 = (f32[104,128]{1,0:T(8,128)S(1)}, f32[104,128]{1,0:T(8,128)S(1)}, u32[]{:S(2)}, u32[]{:S(2)}) collective-permute-start(f32[104,128]{1,0:T(8,128)S(1)} %add_add_fusion.1), channel_id=1, source_target_pairs={{0,8},{8,0},{16,24},{24,16},{1,9},{9,1},{17,25},{25,17},{2,10},{10... | collective-permute-start | bytes 159752 | tf_op jit(solution)/shard_map/ppermute | solution.py:311
  46.4 6.0 %collective-permute-start.11 = (f32[104,128]{1,0:T(8,128)S(1)}, f32[104,128]{1,0:T(8,128)S(1)}, u32[]{:S(2)}, u32[]{:S(2)}) collective-permute-start(f32[104,128]{1,0:T(8,128)S(1)} %add_add_fusion), channel_id=1, source_target_pairs={{0,32},{32,0},{64,96},{96,64},{1,33},{33,1},{65,97},{97,65},{2,34}... | collective-permute-start | bytes 159752 | tf_op jit(solution)/shard_map/ppermute | solution.py:311
  49.4 5.3 %collective-permute-start.13 = (f32[104,128]{1,0:T(8,128)S(1)}, f32[104,128]{1,0:T(8,128)S(1)}, u32[]{:S(2)}, u32[]{:S(2)}) collective-permute-start(f32[104,128]{1,0:T(8,128)S(1)} %add_add_fusion), channel_id=1, source_target_pairs={{0,96},{32,64},{64,32},{96,0},{1,97},{33,65},{65,33},{97,1},{2,98}... | collective-permute-start | bytes 159752 | tf_op jit(solution)/shard_map/ppermute | solution.py:311
  51.6 5.6 %collective-permute-start.12 = (f32[104,128]{1,0:T(8,128)S(1)}, f32[104,128]{1,0:T(8,128)S(1)}, u32[]{:S(2)}, u32[]{:S(2)}) collective-permute-start(f32[104,128]{1,0:T(8,128)S(1)} %add_add_fusion), channel_id=1, source_target_pairs={{0,64},{32,96},{64,0},{96,32},{1,65},{33,97},{65,1},{97,33},{2,66}... | collective-permute-start | bytes 159752 | tf_op jit(solution)/shard_map/ppermute | solution.py:311

commit v2 on v1

v2 whole, which is shorter than its diff:
```python
import functools

import jax
import jax.numpy as jnp
from jax import lax
from jax.experimental import pallas as pl
from jax.experimental.pallas import tpu as pltpu
from jax.sharding import Mesh
from jax.sharding import PartitionSpec as P

ROW = ("row_0", "row_1")
COL = ("col_0", "col_1")
ROW_COL = ROW + COL
F = 5
K = 96
C = 512
N = 1024
S = 160
FK = F * K
HALF = FK // 2
BF = jnp.bfloat16
F32 = jnp.float32
VMEM_LIMIT = 48 * 1024 * 1024


def vmem(count):
    return [pl.BlockSpec(memory_space=pltpu.VMEM)] * count


def smem(count):
    return [pl.BlockSpec(memory_space=pltpu.SMEM)] * count


def one_hot(row):
    cells = lax.broadcasted_iota(jnp.int32, (C, row.shape[1]), 0)
    return jnp.where(cells == row, 1.0, 0.0).astype(BF)


def dot_nn(a, b):
    return lax.dot_general(a, b, (((1,), (0,)), ((), ())), preferred_element_type=F32)


def dot_nt(a, b):
    return lax.dot_general(a, b, (((1,), (1,)), ((), ())), preferred_element_type=F32)


def blocks_of(x):
    ends = [0, 32, 64, 96, 128, 136, 144, 152, 160]
    return [x[..., ends[m] : ends[m + 1]] for m in range(8)]


def pad_like(x, width, fill):
    return jnp.full(x.shape[:-1] + (width,), fill, x.dtype)


def send_order(x, fill, odd_i, odd_j):
    b = blocks_of(x)
    p16, p32 = pad_like(x, 16, fill), pad_like(x, 32, fill)
    corner = jnp.concatenate([b[4], b[5], p16, p16, b[6], b[7], p32, p32], axis=-1)
    lane = lax.broadcasted_iota(jnp.int32, corner.shape, corner.ndim - 1)
    last = corner.ndim - 1
    other = jnp.where((lane // 8) % 2 == 0, pltpu.roll(corner, 120, last), pltpu.roll(corner, 8, last))
    corner = jnp.where(odd_j, corner, other)
    row = jnp.concatenate(
        [b[1], p16, corner[..., 48:64], b[0], corner[..., 0:16], p16], axis=-1
    )
    col = jnp.concatenate([b[3], p32, b[2], p32], axis=-1)
    row = jnp.where(odd_i, pltpu.roll(row, 64, last), row)
    col = jnp.where(odd_j, pltpu.roll(col, 64, last), col)
    return row, col


def receive_order(x, odd_i, odd_j):
    b = blocks_of(x)
    p8, p32 = pad_like(x, 8, -1), pad_like(x, 32, -1)
    row = jnp.concatenate([b[0], p32, b[1], p32], axis=-1)
    row = jnp.where(odd_i, pltpu.roll(row, 64, 1), row)
    even = jnp.concatenate([b[2], b[4], p8, b[6], p8, b[3], p8, b[5], p8, b[7]], axis=-1)
    odd = jnp.concatenate([b[3], b[5], p8, b[7], p8, b[2], p8, b[4], p8, b[6]], axis=-1)
    return row, jnp.where(odd_j, odd, even)


def parities():
    return lax.axis_index("row_1") % 2 == 1, lax.axis_index("col_1") % 2 == 1


def ghost_kernel(count_hbm, basis_hbm, cell_hbm, jac_hbm, row_a, row_b, col_a, col_b,
                 count_ref, basis_ref, cell_ref, jac_ref, val, sems):
    pairs = ((basis_hbm, basis_ref), (cell_hbm, cell_ref), (count_hbm, count_ref), (jac_hbm, jac_ref))
    copies = [pltpu.make_async_copy(src, dst, sems.at[i]) for i, (src, dst) in enumerate(pairs)]
    for copy in copies:
        copy.start()
    odd_i, odd_j = parities()
    copies[1].wait()
    copies[2].wait()
    lane = lax.broadcasted_iota(jnp.int32, (1, S), 1)
    limit = jnp.zeros((1, S), jnp.int32)
    for block, start in enumerate((0, 32, 64, 96, 128, 136, 144, 152)):
        limit = jnp.where(lane >= start, count_ref[0:1, block : block + 1] + start, limit)
    index = jnp.where(lane < limit, cell_ref[...], -1)
    hot = one_hot(jnp.concatenate(send_order(index, -1, odd_i, odd_j), axis=-1))
    copies[3].wait()
    weights = [jnp.concatenate(send_order(jac_ref[g], 0.0, odd_i, odd_j), axis=-1) for g in range(F)]
    copies[0].wait()
    taken = dot_nn(basis_ref[...], hot)
    for f in range(F):
        val[f] = taken[f * K : (f + 1) * K]
    low = lax.broadcasted_iota(jnp.int32, (1, 128), 1) < 64
    parts = []
    for g in range(F):
        total = weights[g][0:1] * val[0]
        for f in range(1, F):
            total = total + weights[g][f : f + 1] * val[f]
        parts.append(total)
    full = jnp.concatenate(parts, axis=0)
    for tile, first, second in ((0, row_a, row_b), (1, col_a, col_b)):
        wide = full[:, tile * 128 : (tile + 1) * 128]
        top, bottom = wide[:HALF], wide[HALF:]
        first[...] = jnp.where(low, top, pltpu.roll(bottom, 64, 1)).astype(BF)
        second[...] = jnp.where(low, pltpu.roll(top, 64, 1), bottom).astype(BF)


def ghost_call(counts, basis, cells, jacobian):
    message = jax.ShapeDtypeStruct((HALF, 128), BF)
    return pl.pallas_call(
        ghost_kernel,
        out_shape=(message,) * 4,
        in_specs=[pl.BlockSpec(memory_space=pltpu.MemorySpace.HBM)] * 4,
        out_specs=tuple(vmem(4)),
        scratch_shapes=[
            pltpu.VMEM((1, 8), jnp.int32),
            pltpu.VMEM((FK, C), BF),
            pltpu.VMEM((1, S), jnp.int32),
            pltpu.VMEM((F, F, S), F32),
            pltpu.VMEM((F, K, 256), F32),
            pltpu.SemaphoreType.DMA((4,)),
        ],
        compiler_params=pltpu.CompilerParams(vmem_limit_bytes=VMEM_LIMIT),
        name="ghost",
    )(counts, basis, cells, jacobian)


BLOCK = 256
HALF_BLOCKS = 2
CHUNK = 32
WIDE = FK + 16


def face_blocks(first_block, nu_ref, basis, pair_ref, jac_ref, flag_ref, hot, got, add, image):
    for block in range(HALF_BLOCKS):
        base = (first_block + block) * BLOCK
        lanes = slice(base, base + BLOCK)
        hot[block, :, :BLOCK] = one_hot(pair_ref[0:1, lanes])
        hot[block, :, BLOCK:] = one_hot(pair_ref[1:2, lanes])
        got[block] = dot_nn(basis, hot[block])
        flags = flag_ref[0:1, lanes].astype(F32)
        add[block, FK:] = jnp.broadcast_to(jnp.concatenate([flags, flags], axis=1), (16, 2 * BLOCK)).astype(BF)
        for tile in range(BLOCK // 128):
            here = slice(base + tile * 128, base + (tile + 1) * 128)
            at_a = slice(tile * 128, (tile + 1) * 128)
            at_b = slice(BLOCK + tile * 128, BLOCK + (tile + 1) * 128)
            flag = flags[:, at_a]
            for start in range(0, K, CHUNK):
                a = [got[block, f * K + start : f * K + start + CHUNK, at_a] for f in range(F)]
                b = [got[block, f * K + start : f * K + start + CHUNK, at_b] for f in range(F)]
                for g in range(F):
                    damp = nu_ref[g] * flag
                    to_a = (jac_ref[g, g, 0:1, here] - damp) * b[g]
                    to_b = (jac_ref[g, g, 1:2, here] - damp) * a[g]
                    for f in range(F):
                        if f != g:
                            to_a = to_a + jac_ref[g, f, 0:1, here] * b[f]
                            to_b = to_b + jac_ref[g, f, 1:2, here] * a[f]
                    rows = slice(g * K + start, g * K + start + CHUNK)
                    add[block, rows, at_a] = to_a.astype(BF)
                    add[block, rows, at_b] = to_b.astype(BF)
    for block in range(HALF_BLOCKS):
        image = dot_nt(add[block], hot[block]) if image is None else image + dot_nt(add[block], hot[block])
    return image


def early_kernel(nu_ref, basis_ref, pair_ref, jac_ref, flag_ref, cell_ref, coord_ref,
                 image_ref, hot_ref, coef_ref, hot, got, add):
    odd_i, odd_j = parities()
    hot_ref[...] = one_hot(jnp.concatenate(receive_order(cell_ref[...], odd_i, odd_j), axis=-1))
    coord = coord_ref[...]
    high = coord.astype(BF).astype(F32)
    row = lax.broadcasted_iota(jnp.int32, (16, K), 0)
    coef_ref[...] = jnp.where(row == 0, high, jnp.where(row == 1, coord - high, 0.0)).astype(BF)
    image_ref[...] = face_blocks(0, nu_ref, basis_ref[...], pair_ref, jac_ref, flag_ref, hot, got, add, None)


def late_kernel(nu_ref, basis_ref, diag_ref, pair_ref, jac_ref, flag_ref, image_ref, out_ref, hot, got, add):
    out_ref[...] = face_blocks(
        HALF_BLOCKS, nu_ref, basis_ref[...], pair_ref, jac_ref, flag_ref, hot, got, add, image_ref[...]
    )
    for tile in range(C // 128):
        here = slice(tile * 128, (tile + 1) * 128)
        flagged = out_ref[FK : FK + 1, here]
        for start in range(0, K, CHUNK):
            v = [basis_ref[f * K + start : f * K + start + CHUNK, here].astype(F32) for f in range(F)]
            for g in range(F):
                rows = slice(g * K + start, g * K + start + CHUNK)
                total = out_ref[rows, here] + (diag_ref[g, g : g + 1, here] + nu_ref[g] * flagged) * v[g]
                for f in range(F):
                    if f != g:
                        total = total + diag_ref[g, f : f + 1, here] * v[f]
                out_ref[rows, here] = total


FACE_SCRATCH = (
    ((HALF_BLOCKS, C, 2 * BLOCK), BF),
    ((HALF_BLOCKS, FK, 2 * BLOCK), F32),
    ((HALF_BLOCKS, WIDE, 2 * BLOCK), BF),
)
FACE_COST = pl.CostEstimate(flops=2_500_000_000, bytes_accessed=2_000_000, transcendentals=0)


def early_call(nu, basis, pair, jacobian, flags, cells, coords):
    return pl.pallas_call(
        early_kernel,
        out_shape=(
            jax.ShapeDtypeStruct((WIDE, C), F32),
            jax.ShapeDtypeStruct((C, 256), BF),
            jax.ShapeDtypeStruct((16, K), BF),
        ),
        in_specs=smem(1) + vmem(6),
        out_specs=tuple(vmem(3)),
        scratch_shapes=[pltpu.VMEM(*scratch) for scratch in FACE_SCRATCH],
        compiler_params=pltpu.CompilerParams(vmem_limit_bytes=VMEM_LIMIT),
        cost_estimate=FACE_COST,
        name="early_faces",
    )(nu, basis, pair, jacobian, flags, cells, coords)


def late_call(nu, basis, diag, pair, jacobian, flags, image):
    return pl.pallas_call(
        late_kernel,
        out_shape=jax.ShapeDtypeStruct((WIDE, C), F32),
        in_specs=smem(1) + vmem(6),
        out_specs=vmem(1)[0],
        scratch_shapes=[pltpu.VMEM(*scratch) for scratch in FACE_SCRATCH],
        compiler_params=pltpu.CompilerParams(vmem_limit_bytes=VMEM_LIMIT),
        cost_estimate=FACE_COST,
        name="late_faces",
    )(nu, basis, diag, pair, jacobian, flags, image)


ROWS = 112


def finish_kernel(row_scale, image_ref, row_a, row_b, col_a, col_b, hot_ref, coef_ref, base_ref,
                  test_ref, gram_ref, arrive, stack):
    low = lax.broadcasted_iota(jnp.int32, (1, 128), 1) < 64
    for tile, first, second in ((0, row_a, row_b), (1, col_a, col_b)):
        here = slice(tile * 128, (tile + 1) * 128)
        one, two = first[...].astype(F32), second[...].astype(F32)
        arrive[:HALF, here] = jnp.where(low, one, pltpu.roll(two, 64, 1)).astype(BF)
        arrive[HALF:, here] = jnp.where(low, pltpu.roll(one, 64, 1), two).astype(BF)
    test = (image_ref[:FK] + dot_nt(arrive[...], hot_ref[...])).astype(BF)
    coef = coef_ref[...]
    first_row = lax.broadcasted_iota(jnp.int32, (16, C), 0) == 0
    for f in range(F):
        part = test[f * K : (f + 1) * K]
        here = slice(f * C, (f + 1) * C)
        test_ref[f] = part
        stack[:K, here] = part
        product = dot_nn(coef, part)
        value = base_ref[f : f + 1] + row_scale * (product[0:1] + product[1:2])
        stack[K:ROWS, here] = jnp.where(first_row, value, 0.0).astype(BF)
    whole = stack[...]
    gram = dot_nt(whole, whole) * (row_scale * row_scale)
    gram_ref[...] = jnp.concatenate([gram[:104], jnp.zeros((104, 128 - ROWS), F32)], axis=1)


def finish_call(row_scale, image, row_a, row_b, col_a, col_b, hot, coef, base):
    return pl.pallas_call(
        functools.partial(finish_kernel, row_scale),
        out_shape=(jax.ShapeDtypeStruct((F, K, C), BF), jax.ShapeDtypeStruct((104, 128), F32)),
        in_specs=vmem(8),
        out_specs=tuple(vmem(2)),
        scratch_shapes=[pltpu.VMEM((FK, 256), BF), pltpu.VMEM((ROWS, F * C), BF)],
        compiler_params=pltpu.CompilerParams(vmem_limit_bytes=VMEM_LIMIT),
        name="finish",
    )(image, row_a, row_b, col_a, col_b, hot, coef, base)


TILES = 13


def solve_kernel(row_scale, first_ref, second_ref, factor_ref, step_ref, work):
    work[...] = first_ref[...] + second_ref[...]
    lane = lax.broadcasted_iota(jnp.int32, (8, 128), 1)
    sub = lax.broadcasted_iota(jnp.int32, (8, 128), 0)

    def spread_row(tile, p):
        return jnp.broadcast_to(tile[p : p + 1], (8, 128))

    def spread_lane(tile, j):
        return jnp.broadcast_to(tile[:, j : j + 1], (8, 128))

    tiles = [work[8 * t : 8 * t + 8] for t in range(TILES)]
    for panel in range(12):
        start = 8 * panel
        here = tiles[panel]
        columns = [[spread_lane(tiles[t], start + p) for p in range(8)] for t in range(TILES)]
        rows = [spread_row(here, p) for p in range(8)]
        d = {(p, q): spread_row(columns[panel][q], p) for p in range(8) for q in range(p, 8)}
        m = {}
        inverse = []
        for p in range(8):
            recip = 1.0 / d[p, p]
            inverse.append(recip)
            for q in range(p + 1, 8):
                m[p, q] = d[p, q] * recip
            for q in range(p + 1, 8):
                rows[q] = rows[q] - m[p, q] * rows[p]
                for r in range(q, 8):
                    d[q, r] = d[q, r] - m[p, q] * d[p, r]
        out = jnp.zeros((8, 128), F32)
        for p in range(8):
            out = jnp.where(sub == p, rows[p] * lax.rsqrt(d[p, p]), out)
        out = jnp.where(lane >= start + sub, out, 0.0)
        factor_ref[start : start + 8, :] = out[:, :97]
        for p in range(7, -1, -1):
            rows[p] = rows[p] * inverse[p]
            for q in range(p + 1, 8):
                rows[p] = rows[p] - m[p, q] * rows[q]
        order = [panel + 1] + [t for t in range(TILES) if t not in (panel, panel + 1)]
        for t in order:
            product = [columns[t][p] * rows[p] for p in range(8)]
            while len(product) > 1:
                product = [product[i] + product[i + 1] for i in range(0, len(product), 2)]
            tiles[t] = tiles[t] - product[0]
        new = rows[0]
        for p in range(1, 8):
            new = jnp.where(sub == p, rows[p], new)
        tiles[panel] = new
    last = tiles[12]
    factor_ref[96:97, :] = jnp.where(lane[:1] == 96, jnp.sqrt(last[0:1]), 0.0)[:, :97]
    step = jnp.zeros((1, 128), F32)
    for t in range(12):
        column = spread_lane(tiles[t], 96)
        step = step + jnp.sum(jnp.where(lane == 8 * t + sub, column, 0.0), axis=0, keepdims=True)
    step_ref[...] = step[:, :96] * (-1.0 / row_scale)


def solve_call(row_scale, first, second):
    return pl.pallas_call(
        functools.partial(solve_kernel, row_scale),
        out_shape=(jax.ShapeDtypeStruct((97, 97), F32), jax.ShapeDtypeStruct((1, 96), F32)),
        in_specs=vmem(2),
        out_specs=tuple(vmem(2)),
        scratch_shapes=[pltpu.VMEM((104, 128), F32)],
        compiler_params=pltpu.CompilerParams(vmem_limit_bytes=VMEM_LIMIT),
        name="solve",
    )(first, second)


def swap(x, axis, step):
    count = lax.axis_size(axis)
    return lax.ppermute(x, axis, [(i, i ^ step) for i in range(count)])


def swap_odd(x, axis):
    pairs = []
    for i in range(1, lax.axis_size(axis) - 1, 2):
        pairs += [(i, i + 1), (i + 1, i)]
    return lax.ppermute(x, axis, pairs)


def local(
    reduced_basis,
    cell_jacobian,
    face_cells,
    face_jacobian,
    limiter_flags,
    viscosity,
    ghost_cells,
    ghost_jacobian,
    ghost_counts,
    receive_cells,
    coordinates,
    base_residual,
):
    devices = lax.axis_size(ROW) * lax.axis_size(COL)
    row_scale = (F * C * devices) ** (-0.5)
    basis = reduced_basis.reshape(FK, C)
    jacobian = face_jacobian.transpose(1, 2, 0, 3)
    flags = limiter_flags.reshape(1, N)
    row_a, row_b, col_a, col_b = ghost_call(
        ghost_counts.reshape(1, 8), basis, ghost_cells.reshape(1, S), ghost_jacobian
    )
    row_a = swap(row_a, ROW, 1)
    row_b = swap_odd(row_b, ROW)
    image, hot, coef = early_call(
        viscosity, basis, face_cells, jacobian, flags, receive_cells.reshape(1, S), coordinates.reshape(1, K)
    )
    group = (lax.broadcasted_iota(jnp.int32, (HALF, 128), 1) % 64) // 8
    corner = row_a + row_b
    col_a = jnp.where((group == 4) | (group == 6), corner, col_a)
    col_b = jnp.where((group == 5) | (group == 7), corner, col_b)
    col_a = swap(col_a, COL, 1)
    col_b = swap_odd(col_b, COL)
    image = late_call(viscosity, basis, cell_jacobian, face_cells, jacobian, flags, image)
    test, gram = finish_call(row_scale, image, row_a, row_b, col_a, col_b, hot, coef, base_residual)
    gram = gram + swap(gram, "col_1", 1)
    for axis in ("col_0", "row_1", "row_0"):
        one, two, three = (swap(gram, axis, k) for k in (1, 2, 3))
        first, second = gram + one, two + three
        gram = first + second
    factor, step = solve_call(row_scale, first, second)
    return (test, factor, step.reshape(K))


def solution(mesh):
    torus = Mesh(mesh.devices.reshape(4, 4, 4, 2), ("row_0", "row_1", "col_0", "col_1"))
    in_specs = (
        P(None, None, ROW_COL),
        P(None, None, ROW_COL),
        P(None, ROW_COL),
        P(None, None, None, ROW_COL),
        P(ROW_COL),
        P(),
        P(ROW_COL),
        P(None, None, ROW_COL),
        P(ROW_COL),
        P(ROW_COL),
        P(),
        P(None, ROW_COL),
    )
    out_specs = (P(None, None, ROW_COL), P(), P())
    return jax.shard_map(local, mesh=torus, in_specs=in_specs, out_specs=out_specs, check_vma=False)
```

time: 62.7 us -> 56 us (0.89)
  starting transfers between devices: 29.2 us -> 22.6 us
  waiting for transfers between devices: 16.7 us -> 14.2 us
  Pallas kernels: 12.2 us -> 13.7 us
  local copies, waits for them, and re-layouts: 3.25 us -> 4.13 us
    ppermute x4 -> x2, starting transfers between devices: 8.56 us -> 1.32 us  [swap_odd(): return lax.ppermute(x, axis, pairs)]
    ppermute x4 -> x2, waiting for transfers between devices: 1.73 us -> 0.01 us  [swap_odd(): return lax.ppermute(x, axis, pairs)]
    pallas_call x2 -> x3, Pallas kernels: 5.57 us -> 7.13 us  [the longest x1 2.98 us: late_call(): pl.pallas_call(late_kernel, out_shape=jax.ShapeDtypeStruct((WIDE, C), F32...]
    unnamed x27 -> x26, local copies, waits for them, and re-layouts: 3.25 us -> 4.13 us
    ppermute x10 -> x12, waiting for transfers between devices: 15 us -> 14.2 us  [swap(): return lax.ppermute(x, axis, [(i, i ^ step) for i in range(count)])]
    ppermute x10 -> x12, starting transfers between devices: 20.7 us -> 21.3 us  [swap(): return lax.ppermute(x, axis, [(i, i ^ step) for i in range(count)])]
  transfers between devices with their start and end apart: 14 -> 14, of which waited for: 9 -> 7; matrix products, arithmetic and copies ran while one was open for 0% -> 0% of each run, Pallas kernels for 7% -> 10%
where the time goes in v2:
time: 56 us; the launch traced here: 55.7 us
  starting transfers between devices  22.6 us (40%)
  waiting for transfers between devices  14.2 us (25%)
  Pallas kernels  13.7 us (24%)
  local copies, waits for them, and re-layouts  4.13 us (7%)
  between operations  0.84 us (2%)
    ppermute x12, starting transfers between devices, swap(): return lax.ppermute(x, axis, [(i, i ^ step) for i in range(count)])  21.3 us
    ppermute x12, waiting for transfers between devices, swap(): return lax.ppermute(x, axis, [(i, i ^ step) for i in range(count)])  14.2 us
    pallas_call x1, Pallas kernels, solve_call(): pl.pallas_call(functools.partial(solve_kernel, row_scale), out_shape=(jax...  5.16 us
    unnamed x26, local copies, waits for them, and re-layouts  4.13 us
    pallas_call x1, Pallas kernels, late_call(): pl.pallas_call(late_kernel, out_shape=jax.ShapeDtypeStruct((WIDE, C), F32...  2.98 us
    pallas_call x1, Pallas kernels, early_call(): pl.pallas_call(early_kernel, out_shape=(jax.ShapeDtypeStruct((WIDE, C), F...  2.63 us
    pallas_call x1, Pallas kernels, ghost_call(): pl.pallas_call(ghost_kernel, out_shape=(message,) * 4, in_specs=[pl.Block...  1.52 us
    pallas_call x1, Pallas kernels, finish_call(): pl.pallas_call(functools.partial(finish_kernel, row_scale), out_shape=(ja...  1.44 us
  transfers between devices with their start and end apart: 14, of which 7 were waited for; matrix products, arithmetic and copies ran while one was open for 0% of the time, Pallas kernels for 10%

profile of v2, /device:TPU:0, one launch (start us, length us, event | category | flops | bytes accessed | tf_op | source)
XLA Modules:
  0.0 55.7 jit_solution(3567104086375508161)
XLA Ops:
  0.6 0.0 copy-start.4
  0.6 0.0 copy-start.5
  0.7 0.7 %copy-done.4 = s32[160]{0:T(256)S(1)} copy-done((s32[160]{0:T(256)S(1)}, s32[160]{0:T(256)}, u32[]{:S(2)}) %copy-start.4) | copy-done | bytes 664
  1.3 0.0 copy-done.5
  1.3 0.0 copy-start
  1.3 1.0 %copy-done = bf16[5,96,512]{2,1,0:T(8,128)(2,1)S(1)} copy-done((bf16[5,96,512]{2,1,0:T(8,128)(2,1)S(1)}, bf16[5,96,512]{2,1,0:T(8,128)(2,1)}, u32[]{:S(2)}) %copy-start) | copy-done | bytes 491544
  2.3 0.0 copy-start.2
  2.3 0.8 %copy-done.2 = f32[5,5,160]{2,1,0:T(8,128)S(1)} copy-done((f32[5,5,160]{2,1,0:T(8,128)S(1)}, f32[5,5,160]{2,1,0:T(8,128)}, u32[]{:S(2)}) %copy-start.2) | copy-done | bytes 16024
  3.1 0.0 copy-start.1
  3.1 0.0 copy-start.11
  3.1 0.0 copy-start.12
  3.1 1.5 %ghost.1 = (bf16[240,128]{1,0:T(8,128)(2,1)S(1)}, bf16[240,128]{1,0:T(8,128)(2,1)S(1)}, bf16[240,128]{1,0:T(8,128)(2,1)S(1)}, bf16[240,128]{1,0:T(8,128)(2,1)S(1)}) custom-call(s32[1,8]{1,0:T(1,128)S(1)} %bitcast.12, bf16[480,512]{1,0:T(8,128)(2,1)S(1)} %bitcast.8, s32[1,160]{1,0:T(1,128)S(1)} %bitcast.11, f32[5,5,160]{2,1,0:T(8,128)S(1)} %copy-done.2), custom_call_target="tpu_custom_call" | custom-call | tf_op jit(solution)/shard_map/ghost/pallas_call | solution.py:125
  4.7 0.0 copy-start.8
  4.7 1.7 %collective-permute-start = (bf16[240,128]{1,0:T(8,128)(2,1)S(1)}, bf16[240,128]{1,0:T(8,128)(2,1)S(1)}, u32[]{:S(2)}, u32[]{:S(2)}) collective-permute-start(bf16[240,128]{1,0:T(8,128)(2,1)S(1)} %get-tuple-element.15), channel_id=1, source_target_pairs={{0,8},{8,0},{16,24},{24,16},{32,40},{40,32},{48,56},{56,48},{64,72... | collective-permute-start | bytes 184328 | tf_op jit(solution)/shard_map/ppermute | solution.py:362
  6.4 0.7 %collective-permute-start.1 = (bf16[240,128]{1,0:T(8,128)(2,1)S(1)}, bf16[240,128]{1,0:T(8,128)(2,1)S(1)}, u32[]{:S(2)}, u32[]{:S(2)}) collective-permute-start(bf16[240,128]{1,0:T(8,128)(2,1)S(1)} %get-tuple-element.16), channel_id=1, source_target_pairs={{8,16},{16,8},{24,32},{32,24},{40,48},{48,40},{56,64},{64,56},{72,... | collective-permute-start | bytes 184328 | tf_op jit(solution)/shard_map/ppermute | solution.py:369
  7.1 0.0 copy-start.9
  7.1 0.0 copy-start.10
  7.1 0.0 copy-done.1
  7.1 0.0 copy-done.11
  7.1 0.0 copy-done.12
  7.1 0.0 copy-done.8
  7.2 0.6 %copy-done.9 = s32[1024]{0:T(1024)S(1)} copy-done((s32[1024]{0:T(1024)S(1)}, s32[1024]{0:T(1024)}, u32[]{:S(2)}) %copy-start.9) | copy-done | bytes 4120
  7.8 0.0 copy-done.10
  7.8 0.0 copy-start.6
  7.8 0.9 %copy-done.6 = f32[2,5,5,1024]{3,0,2,1:T(2,128)S(1)} copy-done((f32[2,5,5,1024]{3,0,2,1:T(2,128)S(1)}, f32[2,5,5,1024]{3,0,2,1:T(2,128)}, u32[]{:S(2)}) %copy-start.6) | copy-done | bytes 204824
  8.7 2.6 %early_faces.1 = (f32[496,512]{1,0:T(8,128)S(1)}, bf16[512,256]{1,0:T(8,128)(2,1)S(1)}, bf16[16,96]{1,0:T(8,128)(2,1)S(1)}) custom-call(f32[5]{0:T(128)S(1)} %copy-done.12, bf16[480,512]{1,0:T(8,128)(2,1)S(1)} %bitcast.9, s32[2,1024]{1,0:T(2,128)S(1)} %copy-done.8, f32[5,5,2,1024]{3,2,1,0:T(2,128)S(1)} %bitcast.13, s32[1,1024]{1,0:T(1,128)S(1)} %bitcast.15, ...), custom_call_target="tpu_custom_call" | custom-call | flops 2500000000 | bytes 2000000 | tf_op jit(solution)/shard_map/early_faces/pallas_call | solution.py:220
  11.4 0.0 collective-permute-done.row_a
  11.4 0.0 collective-permute-done.1.row_b
  11.4 0.0 copy-start.7
  11.4 0.1 collective-permute-start.2
  11.5 0.7 %collective-permute-start.3 = (bf16[240,128]{1,0:T(8,128)(2,1)S(1)}, bf16[240,128]{1,0:T(8,128)(2,1)S(1)}, u32[]{:S(2)}, u32[]{:S(2)}) collective-permute-start(bf16[240,128]{1,0:T(8,128)(2,1)S(1)} %get-tuple-element.25), channel_id=1, source_target_pairs={{1,2},{2,1},{3,4},{4,3},{5,6},{6,5},{9,10},{10,9},{11,12},{12,11},... | collective-permute-start | bytes 184328 | tf_op jit(solution)/shard_map/ppermute | solution.py:369
  12.2 0.1 copy-done.7
  12.3 0.0 copy-start.3
  12.3 3.0 %late_faces.1.image_ref = f32[496,512]{1,0:T(8,128)S(1)} custom-call(f32[5]{0:T(128)S(1)} %copy-done.12, bf16[480,512]{1,0:T(8,128)(2,1)S(1)} %bitcast.10, f32[5,5,512]{2,1,0:T(8,128)S(1)} %copy-done.7, s32[2,1024]{1,0:T(2,128)S(1)} %copy-done.8, f32[5,5,2,1024]{3,2,1,0:T(2,128)S(1)} %bitcast.14, s32[1,1024]{1,0:T(1,128)S(1)} %bitcast.16, ...), custom_call_target="tpu_custom_call" | custom-call | flops 2500000000 | bytes 2000000 | tf_op jit(solution)/shard_map/late_faces/pallas_call | solution.py:237
  15.3 0.0 collective-permute-done.2.col_a
  15.3 0.0 collective-permute-done.3.col_b
  15.3 0.0 copy-done.3
  15.3 1.4 %finish.1 = (bf16[5,96,512]{2,1,0:T(8,128)(2,1)}, f32[104,128]{1,0:T(8,128)S(1)}) custom-call(f32[496,512]{1,0:T(8,128)S(1)} %late_faces.1.image_ref, bf16[240,128]{1,0:T(8,128)(2,1)S(1)} %collective-permute-done.row_a, bf16[240,128]{1,0:T(8,128)(2,1)S(1)} %collective-permute-done.1.row_b, bf16[240,128]{1,0:T(8,128)(2,1)S(1)} %collective-permute-done.2.col_a, ...), custom_call_target="tpu_custom_call" | custom-call | tf_op jit(solution)/shard_map/finish/pallas_call | solution.py:277
  16.7 3.2 %collective-permute-start.4 = (f32[104,128]{1,0:T(8,128)S(1)}, f32[104,128]{1,0:T(8,128)S(1)}, u32[]{:S(2)}, u32[]{:S(2)}) collective-permute-start(f32[104,128]{1,0:T(8,128)S(1)} %get-tuple-element.22), channel_id=1, source_target_pairs={{0,1},{1,0},{2,3},{3,2},{4,5},{5,4},{6,7},{7,6},{8,9},{9,8},{10,11... | collective-permute-start | bytes 159752 | tf_op jit(solution)/shard_map/ppermute | solution.py:362
  20.0 0.9 %collective-permute-done.4 = f32[104,128]{1,0:T(8,128)S(1)} collective-permute-done((f32[104,128]{1,0:T(8,128)S(1)}, f32[104,128]{1,0:T(8,128)S(1)}, u32[]{:S(2)}, u32[]{:S(2)}) %collective-permute-start.4) | collective-permute-done | bytes 53280 | tf_op jit(solution)/shard_map/ppermute | solution.py:362
  20.9 3.6 %collective-permute-start.6 = (f32[104,128]{1,0:T(8,128)S(1)}, f32[104,128]{1,0:T(8,128)S(1)}, u32[]{:S(2)}, u32[]{:S(2)}) collective-permute-start(f32[104,128]{1,0:T(8,128)S(1)} %add.42), channel_id=1, source_target_pairs={{0,4},{2,6},{4,0},{6,2},{1,5},{3,7},{5,1},{7,3},{8,12},{10,14},{12... | collective-permute-start | bytes 159752 | tf_op jit(solution)/shard_map/ppermute | solution.py:362
  24.5 1.0 %collective-permute-start.7 = (f32[104,128]{1,0:T(8,128)S(1)}, f32[104,128]{1,0:T(8,128)S(1)}, u32[]{:S(2)}, u32[]{:S(2)}) collective-permute-start(f32[104,128]{1,0:T(8,128)S(1)} %add.42), channel_id=1, source_target_pairs={{0,6},{2,4},{4,2},{6,0},{1,7},{3,5},{5,3},{7,1},{8,14},{10,12},{12... | collective-permute-start | bytes 159752 | tf_op jit(solution)/shard_map/ppermute | solution.py:362
  25.5 0.0 collective-permute-start.5
  25.5 1.4 %collective-permute-done.6 = f32[104,128]{1,0:T(8,128)S(1)} collective-permute-done((f32[104,128]{1,0:T(8,128)S(1)}, f32[104,128]{1,0:T(8,128)S(1)}, u32[]{:S(2)}, u32[]{:S(2)}) %collective-permute-start.6) | collective-permute-done | bytes 53280 | tf_op jit(solution)/shard_map/ppermute | solution.py:362
  26.9 3.0 %collective-permute-done.7 = f32[104,128]{1,0:T(8,128)S(1)} collective-permute-done((f32[104,128]{1,0:T(8,128)S(1)}, f32[104,128]{1,0:T(8,128)S(1)}, u32[]{:S(2)}, u32[]{:S(2)}) %collective-permute-start.7) | collective-permute-done | bytes 53280 | tf_op jit(solution)/shard_map/ppermute | solution.py:362
  29.8 0.0 collective-permute-done.5
  29.9 4.2 %collective-permute-start.9 = (f32[104,128]{1,0:T(8,128)S(1)}, f32[104,128]{1,0:T(8,128)S(1)}, u32[]{:S(2)}, u32[]{:S(2)}) collective-permute-start(f32[104,128]{1,0:T(8,128)S(1)} %add_add_fusion.1), channel_id=1, source_target_pairs={{0,16},{8,24},{16,0},{24,8},{1,17},{9,25},{17,1},{25,9},{2,18},{10... | collective-permute-start | bytes 159752 | tf_op jit(solution)/shard_map/ppermute | solution.py:362
  34.1 2.6 %collective-permute-start.10 = (f32[104,128]{1,0:T(8,128)S(1)}, f32[104,128]{1,0:T(8,128)S(1)}, u32[]{:S(2)}, u32[]{:S(2)}) collective-permute-start(f32[104,128]{1,0:T(8,128)S(1)} %add_add_fusion.1), channel_id=1, source_target_pairs={{0,24},{8,16},{16,8},{24,0},{1,25},{9,17},{17,9},{25,1},{2,26},{10... | collective-permute-start | bytes 159752 | tf_op jit(solution)/shard_map/ppermute | solution.py:362
  36.7 0.0 collective-permute-start.8
  36.7 0.0 collective-permute-done.9
  36.7 2.7 %collective-permute-done.10 = f32[104,128]{1,0:T(8,128)S(1)} collective-permute-done((f32[104,128]{1,0:T(8,128)S(1)}, f32[104,128]{1,0:T(8,128)S(1)}, u32[]{:S(2)}, u32[]{:S(2)}) %collective-permute-start.10) | collective-permute-done | bytes 53280 | tf_op jit(solution)/shard_map/ppermute | solution.py:362
  39.4 1.4 %collective-permute-done.8 = f32[104,128]{1,0:T(8,128)S(1)} collective-permute-done((f32[104,128]{1,0:T(8,128)S(1)}, f32[104,128]{1,0:T(8,128)S(1)}, u32[]{:S(2)}, u32[]{:S(2)}) %collective-permute-start.8) | collective-permute-done | bytes 53280 | tf_op jit(solution)/shard_map/ppermute | solution.py:362
  40.9 1.6 %collective-permute-start.11 = (f32[104,128]{1,0:T(8,128)S(1)}, f32[104,128]{1,0:T(8,128)S(1)}, u32[]{:S(2)}, u32[]{:S(2)}) collective-permute-start(f32[104,128]{1,0:T(8,128)S(1)} %add_add_fusion), channel_id=1, source_target_pairs={{0,32},{32,0},{64,96},{96,64},{1,33},{33,1},{65,97},{97,65},{2,34}... | collective-permute-start | bytes 159752 | tf_op jit(solution)/shard_map/ppermute | solution.py:362
  42.4 2.7 %collective-permute-start.12 = (f32[104,128]{1,0:T(8,128)S(1)}, f32[104,128]{1,0:T(8,128)S(1)}, u32[]{:S(2)}, u32[]{:S(2)}) collective-permute-start(f32[104,128]{1,0:T(8,128)S(1)} %add_add_fusion), channel_id=1, source_target_pairs={{0,64},{32,96},{64,0},{96,32},{1,65},{33,97},{65,1},{97,33},{2,66}... | collective-permute-start | bytes 159752 | tf_op jit(solution)/shard_map/ppermute | solution.py:362
  45.2 0.5 collective-permute-start.13
  45.6 0.0 collective-permute-done.11
  45.7 2.4 %collective-permute-done.12 = f32[104,128]{1,0:T(8,128)S(1)} collective-permute-done((f32[104,128]{1,0:T(8,128)S(1)}, f32[104,128]{1,0:T(8,128)S(1)}, u32[]{:S(2)}, u32[]{:S(2)}) %collective-permute-start.12) | collective-permute-done | bytes 53280 | tf_op jit(solution)/shard_map/ppermute | solution.py:362
  48.1 2.4 %collective-permute-done.13 = f32[104,128]{1,0:T(8,128)S(1)} collective-permute-done((f32[104,128]{1,0:T(8,128)S(1)}, f32[104,128]{1,0:T(8,128)S(1)}, u32[]{:S(2)}, u32[]{:S(2)}) %collective-permute-start.13) | collective-permute-done | bytes 53280 | tf_op jit(solution)/shard_map/ppermute | solution.py:362
  50.5 5.2 %solve.1 = (f32[97,97]{1,0:T(8,128)}, f32[1,96]{1,0:T(1,128)}) custom-call(f32[104,128]{1,0:T(8,128)S(1)} %add.49.first_ref, f32[104,128]{1,0:T(8,128)S(1)} %add.50.second_ref), custom_call_target="tpu_custom_call" | custom-call | tf_op jit(solution)/shard_map/solve/pallas_call | solution.py:349
  (8 shorter events, 0.1 us)
Async XLA Ops:
  0.6 0.7 %copy-start.4 = (s32[160]{0:T(256)S(1)}, s32[160]{0:T(256)}, u32[]{:S(2)}) copy-start(s32[160]{0:T(256)} %param.18) | copy-start | bytes 1924
  0.6 0.7 %copy-start.5 = (s32[8]{0:T(128)S(1)}, s32[8]{0:T(128)}, u32[]{:S(2)}) copy-start(s32[8]{0:T(128)} %param.20) | copy-start | bytes 100
  1.3 1.0 %copy-start = (bf16[5,96,512]{2,1,0:T(8,128)(2,1)S(1)}, bf16[5,96,512]{2,1,0:T(8,128)(2,1)}, u32[]{:S(2)}) copy-start(bf16[5,96,512]{2,1,0:T(8,128)(2,1)} %param.12) | copy-start | bytes 1474564
  2.3 0.8 %copy-start.2 = (f32[5,5,160]{2,1,0:T(8,128)S(1)}, f32[5,5,160]{2,1,0:T(8,128)}, u32[]{:S(2)}) copy-start(f32[5,5,160]{2,1,0:T(8,128)} %jac_hbm.1) | copy-start | bytes 48004
  3.1 4.0 %copy-start.1 = (bf16[5,96,512]{2,1,0:T(8,128)(2,1)S(1)}, bf16[5,96,512]{2,1,0:T(8,128)(2,1)}, u32[]{:S(2)}) copy-start(bf16[5,96,512]{2,1,0:T(8,128)(2,1)} %param.12) | copy-start | bytes 1474564
  3.1 4.0 %copy-start.11 = (f32[96]{0:T(128)S(1)}, f32[96]{0:T(128)}, u32[]{:S(2)}) copy-start(f32[96]{0:T(128)} %param.22) | copy-start | bytes 1156
  3.1 4.0 %copy-start.12 = (f32[5]{0:T(128)S(1)}, f32[5]{0:T(128)}, u32[]{:S(2)}) copy-start(f32[5]{0:T(128)} %nu_ref.3) | copy-start | bytes 64
  4.7 2.5 %copy-start.8 = (s32[2,1024]{1,0:T(2,128)S(1)}, s32[2,1024]{1,0:T(2,128)}, u32[]{:S(2)}) copy-start(s32[2,1024]{1,0:T(2,128)} %pair_ref.3) | copy-start | bytes 24580
  4.7 6.7 %collective-permute-start = (bf16[240,128]{1,0:T(8,128)(2,1)S(1)}, bf16[240,128]{1,0:T(8,128)(2,1)S(1)}, u32[]{:S(2)}, u32[]{:S(2)}) collective-permute-start(bf16[240,128]{1,0:T(8,128)(2,1)S(1)} %get-tuple-element.15), channel_id=1, source_target_pairs={{0,8},{8,0},{16,24},{24,16},{32,40},{40,32},{48,56},{56,48},{64,72... | collective-permute-start | bytes 184328 | tf_op jit(solution)/shard_map/ppermute | solution.py:362
  6.4 5.0 %collective-permute-start.1 = (bf16[240,128]{1,0:T(8,128)(2,1)S(1)}, bf16[240,128]{1,0:T(8,128)(2,1)S(1)}, u32[]{:S(2)}, u32[]{:S(2)}) collective-permute-start(bf16[240,128]{1,0:T(8,128)(2,1)S(1)} %get-tuple-element.16), channel_id=1, source_target_pairs={{8,16},{16,8},{24,32},{32,24},{40,48},{48,40},{56,64},{64,56},{72,... | collective-permute-start | bytes 184328 | tf_op jit(solution)/shard_map/ppermute | solution.py:369
  7.1 0.7 %copy-start.9 = (s32[1024]{0:T(1024)S(1)}, s32[1024]{0:T(1024)}, u32[]{:S(2)}) copy-start(s32[1024]{0:T(1024)} %param.16) | copy-start | bytes 12292
  7.1 0.7 %copy-start.10 = (s32[160]{0:T(256)S(1)}, s32[160]{0:T(256)}, u32[]{:S(2)}) copy-start(s32[160]{0:T(256)} %param.21) | copy-start | bytes 1924
  7.8 0.9 %copy-start.6 = (f32[2,5,5,1024]{3,0,2,1:T(2,128)S(1)}, f32[2,5,5,1024]{3,0,2,1:T(2,128)}, u32[]{:S(2)}) copy-start(f32[2,5,5,1024]{3,0,2,1:T(2,128)} %param.15) | copy-start | bytes 614404
  11.4 0.9 %copy-start.7 = (f32[5,5,512]{2,1,0:T(8,128)S(1)}, f32[5,5,512]{2,1,0:T(8,128)}, u32[]{:S(2)}) copy-start(f32[5,5,512]{2,1,0:T(8,128)} %diag_ref.1) | copy-start | bytes 153604
  11.4 3.8 %collective-permute-start.2 = (bf16[240,128]{1,0:T(8,128)(2,1)S(1)}, bf16[240,128]{1,0:T(8,128)(2,1)S(1)}, u32[]{:S(2)}, u32[]{:S(2)}) collective-permute-start(bf16[240,128]{1,0:T(8,128)(2,1)S(1)} %get-tuple-element.26), channel_id=1, source_target_pairs={{0,1},{1,0},{2,3},{3,2},{4,5},{5,4},{6,7},{7,6},{8,9},{9,8},{10,11... | collective-permute-start | bytes 184328 | tf_op jit(solution)/shard_map/ppermute | solution.py:362
  11.5 3.7 %collective-permute-start.3 = (bf16[240,128]{1,0:T(8,128)(2,1)S(1)}, bf16[240,128]{1,0:T(8,128)(2,1)S(1)}, u32[]{:S(2)}, u32[]{:S(2)}) collective-permute-start(bf16[240,128]{1,0:T(8,128)(2,1)S(1)} %get-tuple-element.25), channel_id=1, source_target_pairs={{1,2},{2,1},{3,4},{4,3},{5,6},{6,5},{9,10},{10,9},{11,12},{12,11},... | collective-permute-start | bytes 184328 | tf_op jit(solution)/shard_map/ppermute | solution.py:369
  12.3 3.0 %copy-start.3 = (f32[5,512]{1,0:T(8,128)S(1)}, f32[5,512]{1,0:T(8,128)}, u32[]{:S(2)}) copy-start(f32[5,512]{1,0:T(8,128)} %base_ref.1) | copy-start | bytes 30724
  16.7 4.1 %collective-permute-start.4 = (f32[104,128]{1,0:T(8,128)S(1)}, f32[104,128]{1,0:T(8,128)S(1)}, u32[]{:S(2)}, u32[]{:S(2)}) collective-permute-start(f32[104,128]{1,0:T(8,128)S(1)} %get-tuple-element.22), channel_id=1, source_target_pairs={{0,1},{1,0},{2,3},{3,2},{4,5},{5,4},{6,7},{7,6},{8,9},{9,8},{10,11... | collective-permute-start | bytes 159752 | tf_op jit(solution)/shard_map/ppermute | solution.py:362
  20.9 6.0 %collective-permute-start.6 = (f32[104,128]{1,0:T(8,128)S(1)}, f32[104,128]{1,0:T(8,128)S(1)}, u32[]{:S(2)}, u32[]{:S(2)}) collective-permute-start(f32[104,128]{1,0:T(8,128)S(1)} %add.42), channel_id=1, source_target_pairs={{0,4},{2,6},{4,0},{6,2},{1,5},{3,7},{5,1},{7,3},{8,12},{10,14},{12... | collective-permute-start | bytes 159752 | tf_op jit(solution)/shard_map/ppermute | solution.py:362
  24.5 5.3 %collective-permute-start.7 = (f32[104,128]{1,0:T(8,128)S(1)}, f32[104,128]{1,0:T(8,128)S(1)}, u32[]{:S(2)}, u32[]{:S(2)}) collective-permute-start(f32[104,128]{1,0:T(8,128)S(1)} %add.42), channel_id=1, source_target_pairs={{0,6},{2,4},{4,2},{6,0},{1,7},{3,5},{5,3},{7,1},{8,14},{10,12},{12... | collective-permute-start | bytes 159752 | tf_op jit(solution)/shard_map/ppermute | solution.py:362
  25.5 4.3 %collective-permute-start.5 = (f32[104,128]{1,0:T(8,128)S(1)}, f32[104,128]{1,0:T(8,128)S(1)}, u32[]{:S(2)}, u32[]{:S(2)}) collective-permute-start(f32[104,128]{1,0:T(8,128)S(1)} %add.42), channel_id=1, source_target_pairs={{0,2},{2,0},{4,6},{6,4},{1,3},{3,1},{5,7},{7,5},{8,10},{10,8},{12,... | collective-permute-start | bytes 159752 | tf_op jit(solution)/shard_map/ppermute | solution.py:362
  29.9 6.9 %collective-permute-start.9 = (f32[104,128]{1,0:T(8,128)S(1)}, f32[104,128]{1,0:T(8,128)S(1)}, u32[]{:S(2)}, u32[]{:S(2)}) collective-permute-start(f32[104,128]{1,0:T(8,128)S(1)} %add_add_fusion.1), channel_id=1, source_target_pairs={{0,16},{8,24},{16,0},{24,8},{1,17},{9,25},{17,1},{25,9},{2,18},{10... | collective-permute-start | bytes 159752 | tf_op jit(solution)/shard_map/ppermute | solution.py:362
  34.1 5.3 %collective-permute-start.10 = (f32[104,128]{1,0:T(8,128)S(1)}, f32[104,128]{1,0:T(8,128)S(1)}, u32[]{:S(2)}, u32[]{:S(2)}) collective-permute-start(f32[104,128]{1,0:T(8,128)S(1)} %add_add_fusion.1), channel_id=1, source_target_pairs={{0,24},{8,16},{16,8},{24,0},{1,25},{9,17},{17,9},{25,1},{2,26},{10... | collective-permute-start | bytes 159752 | tf_op jit(solution)/shard_map/ppermute | solution.py:362
  36.7 4.1 %collective-permute-start.8 = (f32[104,128]{1,0:T(8,128)S(1)}, f32[104,128]{1,0:T(8,128)S(1)}, u32[]{:S(2)}, u32[]{:S(2)}) collective-permute-start(f32[104,128]{1,0:T(8,128)S(1)} %add_add_fusion.1), channel_id=1, source_target_pairs={{0,8},{8,0},{16,24},{24,16},{1,9},{9,1},{17,25},{25,17},{2,10},{10... | collective-permute-start | bytes 159752 | tf_op jit(solution)/shard_map/ppermute | solution.py:362
  40.9 4.8 %collective-permute-start.11 = (f32[104,128]{1,0:T(8,128)S(1)}, f32[104,128]{1,0:T(8,128)S(1)}, u32[]{:S(2)}, u32[]{:S(2)}) collective-permute-start(f32[104,128]{1,0:T(8,128)S(1)} %add_add_fusion), channel_id=1, source_target_pairs={{0,32},{32,0},{64,96},{96,64},{1,33},{33,1},{65,97},{97,65},{2,34}... | collective-permute-start | bytes 159752 | tf_op jit(solution)/shard_map/ppermute | solution.py:362
  42.4 5.6 %collective-permute-start.12 = (f32[104,128]{1,0:T(8,128)S(1)}, f32[104,128]{1,0:T(8,128)S(1)}, u32[]{:S(2)}, u32[]{:S(2)}) collective-permute-start(f32[104,128]{1,0:T(8,128)S(1)} %add_add_fusion), channel_id=1, source_target_pairs={{0,64},{32,96},{64,0},{96,32},{1,65},{33,97},{65,1},{97,33},{2,66}... | collective-permute-start | bytes 159752 | tf_op jit(solution)/shard_map/ppermute | solution.py:362
  45.2 5.3 %collective-permute-start.13 = (f32[104,128]{1,0:T(8,128)S(1)}, f32[104,128]{1,0:T(8,128)S(1)}, u32[]{:S(2)}, u32[]{:S(2)}) collective-permute-start(f32[104,128]{1,0:T(8,128)S(1)} %add_add_fusion), channel_id=1, source_target_pairs={{0,96},{32,64},{64,32},{96,0},{1,97},{33,65},{65,33},{97,1},{2,98}... | collective-permute-start | bytes 159752 | tf_op jit(solution)/shard_map/ppermute | solution.py:362

commit v3 on v2

--- a/solution.py
+++ b/solution.py
@@ -27,10 +27,6 @@
     return [pl.BlockSpec(memory_space=pltpu.VMEM)] * count
 
 
-def smem(count):
-    return [pl.BlockSpec(memory_space=pltpu.SMEM)] * count
-
-
 def one_hot(row):
     cells = lax.broadcasted_iota(jnp.int32, (C, row.shape[1]), 0)
     return jnp.where(cells == row, 1.0, 0.0).astype(BF)
@@ -84,12 +80,18 @@
     return lax.axis_index("row_1") % 2 == 1, lax.axis_index("col_1") % 2 == 1
 
 
-def ghost_kernel(count_hbm, basis_hbm, cell_hbm, jac_hbm, row_a, row_b, col_a, col_b,
-                 count_ref, basis_ref, cell_ref, jac_ref, val, sems):
-    pairs = ((basis_hbm, basis_ref), (cell_hbm, cell_ref), (count_hbm, count_ref), (jac_hbm, jac_ref))
+def ghost_kernel(count_hbm, cell_hbm, jac_hbm, basis_hbm, pair_hbm, flag_hbm, face_hbm, diag_hbm, arrive_hbm,
+                 coord_hbm, base_hbm, nu_hbm, row_a, row_b, col_a, col_b, basis_ref, pair_ref, flag_ref, face_ref,
+                 diag_ref, arrive_ref, coord_ref, base_ref, nu_ref, count_ref, cell_ref, jac_ref, val, sems):
+    pairs = (
+        (basis_hbm, basis_ref), (cell_hbm, cell_ref), (count_hbm, count_ref), (jac_hbm, jac_ref),
+        (face_hbm, face_ref), (pair_hbm, pair_ref), (flag_hbm, flag_ref), (diag_hbm, diag_ref),
+        (arrive_hbm, arrive_ref), (coord_hbm, coord_ref), (base_hbm, base_ref),
+        (nu_hbm, nu_ref),
+    )
     copies = [pltpu.make_async_copy(src, dst, sems.at[i]) for i, (src, dst) in enumerate(pairs)]
-    for copy in copies:
-        copy.start()
+    for i in (1, 2, 0, 3, 4, 5, 6, 7, 8, 9, 10, 11):
+        copies[i].start()
     odd_i, odd_j = parities()
     copies[1].wait()
     copies[2].wait()
@@ -118,26 +120,28 @@
         top, bottom = wide[:HALF], wide[HALF:]
         first[...] = jnp.where(low, top, pltpu.roll(bottom, 64, 1)).astype(BF)
         second[...] = jnp.where(low, pltpu.roll(top, 64, 1), bottom).astype(BF)
-
-
-def ghost_call(counts, basis, cells, jacobian):
+    for copy in copies[4:]:
+        copy.wait()
+
+
+def ghost_call(counts, cells, jacobian, *loaded):
     message = jax.ShapeDtypeStruct((HALF, 128), BF)
+    operands = [pltpu.with_memory_space_constraint(x, pltpu.MemorySpace.HBM) for x in (counts, cells, jacobian) + loaded]
     return pl.pallas_call(
         ghost_kernel,
-        out_shape=(message,) * 4,
-        in_specs=[pl.BlockSpec(memory_space=pltpu.MemorySpace.HBM)] * 4,
-        out_specs=tuple(vmem(4)),
+        out_shape=(message,) * 4 + tuple(jax.ShapeDtypeStruct(x.shape, x.dtype) for x in loaded),
+        in_specs=[pl.BlockSpec(memory_space=pltpu.MemorySpace.HBM)] * len(operands),
+        out_specs=tuple(vmem(4 + len(loaded))),
         scratch_shapes=[
             pltpu.VMEM((1, 8), jnp.int32),
-            pltpu.VMEM((FK, C), BF),
             pltpu.VMEM((1, S), jnp.int32),
             pltpu.VMEM((F, F, S), F32),
             pltpu.VMEM((F, K, 256), F32),
-            pltpu.SemaphoreType.DMA((4,)),
+            pltpu.SemaphoreType.DMA((12,)),
         ],
         compiler_params=pltpu.CompilerParams(vmem_limit_bytes=VMEM_LIMIT),
         name="ghost",
-    )(counts, basis, cells, jacobian)
+    )(*operands)
 
 
 BLOCK = 256
@@ -159,12 +163,12 @@
             here = slice(base + tile * 128, base + (tile + 1) * 128)
             at_a = slice(tile * 128, (tile + 1) * 128)
             at_b = slice(BLOCK + tile * 128, BLOCK + (tile + 1) * 128)
-            flag = flags[:, at_a]
+            damps = [nu_ref[0:1, g : g + 1] * flags[:, at_a] for g in range(F)]
             for start in range(0, K, CHUNK):
                 a = [got[block, f * K + start : f * K + start + CHUNK, at_a] for f in range(F)]
                 b = [got[block, f * K + start : f * K + start + CHUNK, at_b] for f in range(F)]
                 for g in range(F):
-                    damp = nu_ref[g] * flag
+                    damp = damps[g]
                     to_a = (jac_ref[g, g, 0:1, here] - damp) * b[g]
                     to_b = (jac_ref[g, g, 1:2, here] - damp) * a[g]
                     for f in range(F):
@@ -197,11 +201,12 @@
     for tile in range(C // 128):
         here = slice(tile * 128, (tile + 1) * 128)
         flagged = out_ref[FK : FK + 1, here]
+        own = [diag_ref[g, g : g + 1, here] + nu_ref[0:1, g : g + 1] * flagged for g in range(F)]
         for start in range(0, K, CHUNK):
             v = [basis_ref[f * K + start : f * K + start + CHUNK, here].astype(F32) for f in range(F)]
             for g in range(F):
                 rows = slice(g * K + start, g * K + start + CHUNK)
-                total = out_ref[rows, here] + (diag_ref[g, g : g + 1, here] + nu_ref[g] * flagged) * v[g]
+                total = out_ref[rows, here] + own[g] * v[g]
                 for f in range(F):
                     if f != g:
                         total = total + diag_ref[g, f : f + 1, here] * v[f]
@@ -224,7 +229,7 @@
             jax.ShapeDtypeStruct((C, 256), BF),
             jax.ShapeDtypeStruct((16, K), BF),
         ),
-        in_specs=smem(1) + vmem(6),
+        in_specs=vmem(7),
         out_specs=tuple(vmem(3)),
         scratch_shapes=[pltpu.VMEM(*scratch) for scratch in FACE_SCRATCH],
         compiler_params=pltpu.CompilerParams(vmem_limit_bytes=VMEM_LIMIT),
@@ -237,7 +242,7 @@
     return pl.pallas_call(
         late_kernel,
         out_shape=jax.ShapeDtypeStruct((WIDE, C), F32),
-        in_specs=smem(1) + vmem(6),
+        in_specs=vmem(7),
         out_specs=vmem(1)[0],
         scratch_shapes=[pltpu.VMEM(*scratch) for scratch in FACE_SCRATCH],
         compiler_params=pltpu.CompilerParams(vmem_limit_bytes=VMEM_LIMIT),
@@ -388,13 +393,15 @@
     basis = reduced_basis.reshape(FK, C)
     jacobian = face_jacobian.transpose(1, 2, 0, 3)
     flags = limiter_flags.reshape(1, N)
-    row_a, row_b, col_a, col_b = ghost_call(
-        ghost_counts.reshape(1, 8), basis, ghost_cells.reshape(1, S), ghost_jacobian
+    row_a, row_b, col_a, col_b, basis, pair, flags, jacobian, diag, arrive, coords, base, nu = ghost_call(
+        ghost_counts.reshape(1, 8), ghost_cells.reshape(1, S), ghost_jacobian,
+        basis, face_cells, flags, jacobian, cell_jacobian, receive_cells.reshape(1, S),
+        coordinates.reshape(1, K), base_residual, viscosity.reshape(1, F),
     )
     row_a = swap(row_a, ROW, 1)
     row_b = swap_odd(row_b, ROW)
     image, hot, coef = early_call(
-        viscosity, basis, face_cells, jacobian, flags, receive_cells.reshape(1, S), coordinates.reshape(1, K)
+        nu, basis, pair, jacobian, flags, arrive, coords
     )
     group = (lax.broadcasted_iota(jnp.int32, (HALF, 128), 1) % 64) // 8
     corner = row_a + row_b
@@ -402,8 +409,8 @@
     col_b = jnp.where((group == 5) | (group == 7), corner, col_b)
     col_a = swap(col_a, COL, 1)
     col_b = swap_odd(col_b, COL)
-    image = late_call(viscosity, basis, cell_jacobian, face_cells, jacobian, flags, image)
-    test, gram = finish_call(row_scale, image, row_a, row_b, col_a, col_b, hot, coef, base_residual)
+    image = late_call(nu, basis, diag, pair, jacobian, flags, image)
+    test, gram = finish_call(row_scale, image, row_a, row_b, col_a, col_b, hot, coef, base)
     gram = gram + swap(gram, "col_1", 1)
     for axis in ("col_0", "row_1", "row_0"):
         one, two, three = (swap(gram, axis, k) for k in (1, 2, 3))

time: 56 us -> 53.4 us (0.954)
  local copies, waits for them, and re-layouts: 4.13 us -> 0 us
  waiting for transfers between devices: 14.2 us -> 15.9 us
  starting transfers between devices: 22.6 us -> 23.4 us
  Pallas kernels: 13.7 us -> 13.1 us
    unnamed x26 -> x0, local copies, waits for them, and re-layouts: 4.13 us -> none
    ppermute x12, waiting for transfers between devices: 14.2 us -> 15.9 us  [swap(): return lax.ppermute(x, axis, [(i, i ^ step) for i in range(count)])]
    ppermute x12, starting transfers between devices: 21.3 us -> 22.1 us  [swap(): return lax.ppermute(x, axis, [(i, i ^ step) for i in range(count)])]
  transfers between devices with their start and end apart: 14 -> 14, of which waited for: 7 -> 7; matrix products, arithmetic and copies ran while one was open for 0% -> 0% of each run, Pallas kernels for 10% -> 9%
where the time goes in v3:
time: 53.4 us; the launch traced here: 53.3 us
  starting transfers between devices  23.4 us (44%)
  waiting for transfers between devices  15.9 us (30%)
  Pallas kernels  13.1 us (25%)
  between operations  0.75 us (1%)
    ppermute x12, starting transfers between devices, swap(): return lax.ppermute(x, axis, [(i, i ^ step) for i in range(count)])  22.1 us
    ppermute x12, waiting for transfers between devices, swap(): return lax.ppermute(x, axis, [(i, i ^ step) for i in range(count)])  15.9 us
    pallas_call x1, Pallas kernels, solve_call(): pl.pallas_call(functools.partial(solve_kernel, row_scale), out_shape=(jax...  5.16 us
    pallas_call x1, Pallas kernels, late_call(): pl.pallas_call(late_kernel, out_shape=jax.ShapeDtypeStruct((WIDE, C), F32...  2.52 us
    pallas_call x1, Pallas kernels, early_call(): pl.pallas_call(early_kernel, out_shape=(jax.ShapeDtypeStruct((WIDE, C), F...  2.1 us
    pallas_call x1, Pallas kernels, ghost_call(): pl.pallas_call(ghost_kernel, out_shape=(message,) * 4 + tuple((jax.ShapeD...  1.92 us
    pallas_call x1, Pallas kernels, finish_call(): pl.pallas_call(functools.partial(finish_kernel, row_scale), out_shape=(ja...  1.44 us
    ppermute x2, starting transfers between devices, swap_odd(): return lax.ppermute(x, axis, pairs)  1.32 us
  transfers between devices with their start and end apart: 14, of which 7 were waited for; matrix products, arithmetic and copies ran while one was open for 0% of the time, Pallas kernels for 9%

profile of v3, /device:TPU:0, one launch (start us, length us, event | category | flops | bytes accessed | tf_op | source)
XLA Modules:
  0.0 53.3 jit_solution(7383869448400318981)
XLA Ops:
  0.6 1.9 %ghost.1 = (bf16[240,128]{1,0:T(8,128)(2,1)S(1)}, bf16[240,128]{1,0:T(8,128)(2,1)S(1)}, bf16[240,128]{1,0:T(8,128)(2,1)S(1)}, bf16[240,128]{1,0:T(8,128)(2,1)S(1...) custom-call(s32[1,8]{1,0:T(1,128)} %bitcast.14, ...), custom_call_target="tpu_custom_call" | custom-call | tf_op jit(solution)/shard_map/ghost/pallas_call | solution.py:130
  2.6 1.7 %collective-permute-start = (bf16[240,128]{1,0:T(8,128)(2,1)S(1)}, bf16[240,128]{1,0:T(8,128)(2,1)S(1)}, u32[]{:S(2)}, u32[]{:S(2)}) collective-permute-start(bf16[240,128]{1,0:T(8,128)(2,1)S(1)} %get-tuple-element.32), channel_id=1, source_target_pairs={{0,8},{8,0},{16,24},{24,16},{32,40},{40,32},{48,56},{56,48},{64,72... | collective-permute-start | bytes 184328 | tf_op jit(solution)/shard_map/ppermute | solution.py:367
  4.3 0.7 %collective-permute-start.1 = (bf16[240,128]{1,0:T(8,128)(2,1)S(1)}, bf16[240,128]{1,0:T(8,128)(2,1)S(1)}, u32[]{:S(2)}, u32[]{:S(2)}) collective-permute-start(bf16[240,128]{1,0:T(8,128)(2,1)S(1)} %get-tuple-element.33), channel_id=1, source_target_pairs={{8,16},{16,8},{24,32},{32,24},{40,48},{48,40},{56,64},{64,56},{72,... | collective-permute-start | bytes 184328 | tf_op jit(solution)/shard_map/ppermute | solution.py:374
  5.0 2.1 %early_faces.1 = (f32[496,512]{1,0:T(8,128)S(1)}, bf16[512,256]{1,0:T(8,128)(2,1)S(1)}, bf16[16,96]{1,0:T(8,128)(2,1)S(1)}) custom-call(f32[1,5]{1,0:T(1,128)S(1)} %get-tuple-element.23.nu_ref, bf16[480,512]{1,0:T(8,128)(2,1)S(1)} %get-tuple-element.24.basis_ref, s32[2,1024]{1,0:T(2,128)S(1)} %get-tuple-element.26.pair_ref, ...), custom_call_target="tpu_custom_call" | custom-call | flops 2500000000 | bytes 2000000 | tf_op jit(solution)/shard_map/early_faces/pallas_call | solution.py:225
  7.1 0.0 collective-permute-done.row_a
  7.1 0.0 collective-permute-done.1.row_b
  7.2 0.7 %collective-permute-start.3 = (bf16[240,128]{1,0:T(8,128)(2,1)S(1)}, bf16[240,128]{1,0:T(8,128)(2,1)S(1)}, u32[]{:S(2)}, u32[]{:S(2)}) collective-permute-start(bf16[240,128]{1,0:T(8,128)(2,1)S(1)} %get-tuple-element.43), channel_id=1, source_target_pairs={{1,2},{2,1},{3,4},{4,3},{5,6},{6,5},{9,10},{10,9},{11,12},{12,11},... | collective-permute-start | bytes 184328 | tf_op jit(solution)/shard_map/ppermute | solution.py:374
  7.8 3.3 %collective-permute-start.2 = (bf16[240,128]{1,0:T(8,128)(2,1)S(1)}, bf16[240,128]{1,0:T(8,128)(2,1)S(1)}, u32[]{:S(2)}, u32[]{:S(2)}) collective-permute-start(bf16[240,128]{1,0:T(8,128)(2,1)S(1)} %get-tuple-element.44), channel_id=1, source_target_pairs={{0,1},{1,0},{2,3},{3,2},{4,5},{5,4},{6,7},{7,6},{8,9},{9,8},{10,11... | collective-permute-start | bytes 184328 | tf_op jit(solution)/shard_map/ppermute | solution.py:367
  11.2 2.5 %late_faces.1.image_ref = f32[496,512]{1,0:T(8,128)S(1)} custom-call(f32[1,5]{1,0:T(1,128)S(1)} %get-tuple-element.23.nu_ref, bf16[480,512]{1,0:T(8,128)(2,1)S(1)} %get-tuple-element.24.basis_ref, f32[5,5,512]{2,1,0:T(8,128)S(1)} %get-tuple-element.25.diag_ref, s32[2,1024]{1,0:T(2,128)S(1)} %get-tuple-element.26.pair_ref, ...), custom_call_target="tpu_custom_call" | custom-call | flops 2500000000 | bytes 2000000 | tf_op jit(solution)/shard_map/late_faces/pallas_call | solution.py:242
  13.7 0.0 collective-permute-done.3.col_b
  13.7 0.0 collective-permute-done.2.col_a
  13.7 1.4 %finish.1 = (bf16[5,96,512]{2,1,0:T(8,128)(2,1)}, f32[104,128]{1,0:T(8,128)S(1)}) custom-call(f32[496,512]{1,0:T(8,128)S(1)} %late_faces.1.image_ref, bf16[240,128]{1,0:T(8,128)(2,1)S(1)} %collective-permute-done.row_a, bf16[240,128]{1,0:T(8,128)(2,1)S(1)} %collective-permute-done.1.row_b, bf16[240,128]{1,0:T(8,128)(2,1)S(1)} %collective-permute-done.2.col_a, ...), custom_call_target="tpu_custom_call" | custom-call | tf_op jit(solution)/shard_map/finish/pallas_call | solution.py:282
  15.2 0.0 collective-permute-start.4
  15.2 1.2 %collective-permute-done.4 = f32[104,128]{1,0:T(8,128)S(1)} collective-permute-done((f32[104,128]{1,0:T(8,128)S(1)}, f32[104,128]{1,0:T(8,128)S(1)}, u32[]{:S(2)}, u32[]{:S(2)}) %collective-permute-start.4) | collective-permute-done | bytes 53280 | tf_op jit(solution)/shard_map/ppermute | solution.py:367
  16.4 3.1 %collective-permute-start.7 = (f32[104,128]{1,0:T(8,128)S(1)}, f32[104,128]{1,0:T(8,128)S(1)}, u32[]{:S(2)}, u32[]{:S(2)}) collective-permute-start(f32[104,128]{1,0:T(8,128)S(1)} %add.42), channel_id=1, source_target_pairs={{0,6},{2,4},{4,2},{6,0},{1,7},{3,5},{5,3},{7,1},{8,14},{10,12},{12... | collective-permute-start | bytes 159752 | tf_op jit(solution)/shard_map/ppermute | solution.py:367
  19.5 1.0 %collective-permute-start.6 = (f32[104,128]{1,0:T(8,128)S(1)}, f32[104,128]{1,0:T(8,128)S(1)}, u32[]{:S(2)}, u32[]{:S(2)}) collective-permute-start(f32[104,128]{1,0:T(8,128)S(1)} %add.42), channel_id=1, source_target_pairs={{0,4},{2,6},{4,0},{6,2},{1,5},{3,7},{5,1},{7,3},{8,12},{10,14},{12... | collective-permute-start | bytes 159752 | tf_op jit(solution)/shard_map/ppermute | solution.py:367
  20.5 0.1 collective-permute-start.5
  20.6 1.5 %collective-permute-done.7 = f32[104,128]{1,0:T(8,128)S(1)} collective-permute-done((f32[104,128]{1,0:T(8,128)S(1)}, f32[104,128]{1,0:T(8,128)S(1)}, u32[]{:S(2)}, u32[]{:S(2)}) %collective-permute-start.7) | collective-permute-done | bytes 53280 | tf_op jit(solution)/shard_map/ppermute | solution.py:367
  22.0 3.4 %collective-permute-done.6 = f32[104,128]{1,0:T(8,128)S(1)} collective-permute-done((f32[104,128]{1,0:T(8,128)S(1)}, f32[104,128]{1,0:T(8,128)S(1)}, u32[]{:S(2)}, u32[]{:S(2)}) %collective-permute-start.6) | collective-permute-done | bytes 53280 | tf_op jit(solution)/shard_map/ppermute | solution.py:367
  25.4 0.0 collective-permute-done.5
  25.5 7.7 %collective-permute-start.10 = (f32[104,128]{1,0:T(8,128)S(1)}, f32[104,128]{1,0:T(8,128)S(1)}, u32[]{:S(2)}, u32[]{:S(2)}) collective-permute-start(f32[104,128]{1,0:T(8,128)S(1)} %add_add_fusion.1), channel_id=1, source_target_pairs={{0,24},{8,16},{16,8},{24,0},{1,25},{9,17},{17,9},{25,1},{2,26},{10... | collective-permute-start | bytes 159752 | tf_op jit(solution)/shard_map/ppermute | solution.py:367
  33.1 0.0 collective-permute-start.9
  33.1 0.9 %collective-permute-start.8 = (f32[104,128]{1,0:T(8,128)S(1)}, f32[104,128]{1,0:T(8,128)S(1)}, u32[]{:S(2)}, u32[]{:S(2)}) collective-permute-start(f32[104,128]{1,0:T(8,128)S(1)} %add_add_fusion.1), channel_id=1, source_target_pairs={{0,8},{8,0},{16,24},{24,16},{1,9},{9,1},{17,25},{25,17},{2,10},{10... | collective-permute-start | bytes 159752 | tf_op jit(solution)/shard_map/ppermute | solution.py:367
  34.1 1.2 %collective-permute-done.10 = f32[104,128]{1,0:T(8,128)S(1)} collective-permute-done((f32[104,128]{1,0:T(8,128)S(1)}, f32[104,128]{1,0:T(8,128)S(1)}, u32[]{:S(2)}, u32[]{:S(2)}) %collective-permute-start.10) | collective-permute-done | bytes 53280 | tf_op jit(solution)/shard_map/ppermute | solution.py:367
  35.2 3.5 %collective-permute-done.9 = f32[104,128]{1,0:T(8,128)S(1)} collective-permute-done((f32[104,128]{1,0:T(8,128)S(1)}, f32[104,128]{1,0:T(8,128)S(1)}, u32[]{:S(2)}, u32[]{:S(2)}) %collective-permute-start.9) | collective-permute-done | bytes 53280 | tf_op jit(solution)/shard_map/ppermute | solution.py:367
  38.8 0.0 collective-permute-done.8
  38.8 1.6 %collective-permute-start.11 = (f32[104,128]{1,0:T(8,128)S(1)}, f32[104,128]{1,0:T(8,128)S(1)}, u32[]{:S(2)}, u32[]{:S(2)}) collective-permute-start(f32[104,128]{1,0:T(8,128)S(1)} %add_add_fusion), channel_id=1, source_target_pairs={{0,32},{32,0},{64,96},{96,64},{1,33},{33,1},{65,97},{97,65},{2,34}... | collective-permute-start | bytes 159752 | tf_op jit(solution)/shard_map/ppermute | solution.py:367
  40.4 2.1 %collective-permute-start.13 = (f32[104,128]{1,0:T(8,128)S(1)}, f32[104,128]{1,0:T(8,128)S(1)}, u32[]{:S(2)}, u32[]{:S(2)}) collective-permute-start(f32[104,128]{1,0:T(8,128)S(1)} %add_add_fusion), channel_id=1, source_target_pairs={{0,96},{32,64},{64,32},{96,0},{1,97},{33,65},{65,33},{97,1},{2,98}... | collective-permute-start | bytes 159752 | tf_op jit(solution)/shard_map/ppermute | solution.py:367
  42.5 0.5 collective-permute-start.12
  43.0 0.0 collective-permute-done.11
  43.0 2.7 %collective-permute-done.13 = f32[104,128]{1,0:T(8,128)S(1)} collective-permute-done((f32[104,128]{1,0:T(8,128)S(1)}, f32[104,128]{1,0:T(8,128)S(1)}, u32[]{:S(2)}, u32[]{:S(2)}) %collective-permute-start.13) | collective-permute-done | bytes 53280 | tf_op jit(solution)/shard_map/ppermute | solution.py:367
  45.7 2.4 %collective-permute-done.12 = f32[104,128]{1,0:T(8,128)S(1)} collective-permute-done((f32[104,128]{1,0:T(8,128)S(1)}, f32[104,128]{1,0:T(8,128)S(1)}, u32[]{:S(2)}, u32[]{:S(2)}) %collective-permute-start.12) | collective-permute-done | bytes 53280 | tf_op jit(solution)/shard_map/ppermute | solution.py:367
  48.1 5.2 %solve.1 = (f32[97,97]{1,0:T(8,128)}, f32[1,96]{1,0:T(1,128)}) custom-call(f32[104,128]{1,0:T(8,128)S(1)} %add.49.first_ref, f32[104,128]{1,0:T(8,128)S(1)} %add.50.second_ref), custom_call_target="tpu_custom_call" | custom-call | tf_op jit(solution)/shard_map/solve/pallas_call | solution.py:354
  (8 shorter events, 0.1 us)
Async XLA Ops:
  2.6 4.5 %collective-permute-start = (bf16[240,128]{1,0:T(8,128)(2,1)S(1)}, bf16[240,128]{1,0:T(8,128)(2,1)S(1)}, u32[]{:S(2)}, u32[]{:S(2)}) collective-permute-start(bf16[240,128]{1,0:T(8,128)(2,1)S(1)} %get-tuple-element.32), channel_id=1, source_target_pairs={{0,8},{8,0},{16,24},{24,16},{32,40},{40,32},{48,56},{56,48},{64,72... | collective-permute-start | bytes 184328 | tf_op jit(solution)/shard_map/ppermute | solution.py:367
  4.3 2.8 %collective-permute-start.1 = (bf16[240,128]{1,0:T(8,128)(2,1)S(1)}, bf16[240,128]{1,0:T(8,128)(2,1)S(1)}, u32[]{:S(2)}, u32[]{:S(2)}) collective-permute-start(bf16[240,128]{1,0:T(8,128)(2,1)S(1)} %get-tuple-element.33), channel_id=1, source_target_pairs={{8,16},{16,8},{24,32},{32,24},{40,48},{48,40},{56,64},{64,56},{72,... | collective-permute-start | bytes 184328 | tf_op jit(solution)/shard_map/ppermute | solution.py:374
  7.2 6.5 %collective-permute-start.3 = (bf16[240,128]{1,0:T(8,128)(2,1)S(1)}, bf16[240,128]{1,0:T(8,128)(2,1)S(1)}, u32[]{:S(2)}, u32[]{:S(2)}) collective-permute-start(bf16[240,128]{1,0:T(8,128)(2,1)S(1)} %get-tuple-element.43), channel_id=1, source_target_pairs={{1,2},{2,1},{3,4},{4,3},{5,6},{6,5},{9,10},{10,9},{11,12},{12,11},... | collective-permute-start | bytes 184328 | tf_op jit(solution)/shard_map/ppermute | solution.py:374
  7.8 5.9 %collective-permute-start.2 = (bf16[240,128]{1,0:T(8,128)(2,1)S(1)}, bf16[240,128]{1,0:T(8,128)(2,1)S(1)}, u32[]{:S(2)}, u32[]{:S(2)}) collective-permute-start(bf16[240,128]{1,0:T(8,128)(2,1)S(1)} %get-tuple-element.44), channel_id=1, source_target_pairs={{0,1},{1,0},{2,3},{3,2},{4,5},{5,4},{6,7},{7,6},{8,9},{9,8},{10,11... | collective-permute-start | bytes 184328 | tf_op jit(solution)/shard_map/ppermute | solution.py:367
  15.2 1.2 %collective-permute-start.4 = (f32[104,128]{1,0:T(8,128)S(1)}, f32[104,128]{1,0:T(8,128)S(1)}, u32[]{:S(2)}, u32[]{:S(2)}) collective-permute-start(f32[104,128]{1,0:T(8,128)S(1)} %get-tuple-element.40), channel_id=1, source_target_pairs={{0,1},{1,0},{2,3},{3,2},{4,5},{5,4},{6,7},{7,6},{8,9},{9,8},{10,11... | collective-permute-start | bytes 159752 | tf_op jit(solution)/shard_map/ppermute | solution.py:367
  16.4 5.6 %collective-permute-start.7 = (f32[104,128]{1,0:T(8,128)S(1)}, f32[104,128]{1,0:T(8,128)S(1)}, u32[]{:S(2)}, u32[]{:S(2)}) collective-permute-start(f32[104,128]{1,0:T(8,128)S(1)} %add.42), channel_id=1, source_target_pairs={{0,6},{2,4},{4,2},{6,0},{1,7},{3,5},{5,3},{7,1},{8,14},{10,12},{12... | collective-permute-start | bytes 159752 | tf_op jit(solution)/shard_map/ppermute | solution.py:367
  19.5 5.9 %collective-permute-start.6 = (f32[104,128]{1,0:T(8,128)S(1)}, f32[104,128]{1,0:T(8,128)S(1)}, u32[]{:S(2)}, u32[]{:S(2)}) collective-permute-start(f32[104,128]{1,0:T(8,128)S(1)} %add.42), channel_id=1, source_target_pairs={{0,4},{2,6},{4,0},{6,2},{1,5},{3,7},{5,1},{7,3},{8,12},{10,14},{12... | collective-permute-start | bytes 159752 | tf_op jit(solution)/shard_map/ppermute | solution.py:367
  20.5 5.0 %collective-permute-start.5 = (f32[104,128]{1,0:T(8,128)S(1)}, f32[104,128]{1,0:T(8,128)S(1)}, u32[]{:S(2)}, u32[]{:S(2)}) collective-permute-start(f32[104,128]{1,0:T(8,128)S(1)} %add.42), channel_id=1, source_target_pairs={{0,2},{2,0},{4,6},{6,4},{1,3},{3,1},{5,7},{7,5},{8,10},{10,8},{12,... | collective-permute-start | bytes 159752 | tf_op jit(solution)/shard_map/ppermute | solution.py:367
  25.5 9.8 %collective-permute-start.10 = (f32[104,128]{1,0:T(8,128)S(1)}, f32[104,128]{1,0:T(8,128)S(1)}, u32[]{:S(2)}, u32[]{:S(2)}) collective-permute-start(f32[104,128]{1,0:T(8,128)S(1)} %add_add_fusion.1), channel_id=1, source_target_pairs={{0,24},{8,16},{16,8},{24,0},{1,25},{9,17},{17,9},{25,1},{2,26},{10... | collective-permute-start | bytes 159752 | tf_op jit(solution)/shard_map/ppermute | solution.py:367
  33.1 5.6 %collective-permute-start.9 = (f32[104,128]{1,0:T(8,128)S(1)}, f32[104,128]{1,0:T(8,128)S(1)}, u32[]{:S(2)}, u32[]{:S(2)}) collective-permute-start(f32[104,128]{1,0:T(8,128)S(1)} %add_add_fusion.1), channel_id=1, source_target_pairs={{0,16},{8,24},{16,0},{24,8},{1,17},{9,25},{17,1},{25,9},{2,18},{10... | collective-permute-start | bytes 159752 | tf_op jit(solution)/shard_map/ppermute | solution.py:367
  33.1 5.6 %collective-permute-start.8 = (f32[104,128]{1,0:T(8,128)S(1)}, f32[104,128]{1,0:T(8,128)S(1)}, u32[]{:S(2)}, u32[]{:S(2)}) collective-permute-start(f32[104,128]{1,0:T(8,128)S(1)} %add_add_fusion.1), channel_id=1, source_target_pairs={{0,8},{8,0},{16,24},{24,16},{1,9},{9,1},{17,25},{25,17},{2,10},{10... | collective-permute-start | bytes 159752 | tf_op jit(solution)/shard_map/ppermute | solution.py:367
  38.8 4.2 %collective-permute-start.11 = (f32[104,128]{1,0:T(8,128)S(1)}, f32[104,128]{1,0:T(8,128)S(1)}, u32[]{:S(2)}, u32[]{:S(2)}) collective-permute-start(f32[104,128]{1,0:T(8,128)S(1)} %add_add_fusion), channel_id=1, source_target_pairs={{0,32},{32,0},{64,96},{96,64},{1,33},{33,1},{65,97},{97,65},{2,34}... | collective-permute-start | bytes 159752 | tf_op jit(solution)/shard_map/ppermute | solution.py:367
  40.4 5.3 %collective-permute-start.13 = (f32[104,128]{1,0:T(8,128)S(1)}, f32[104,128]{1,0:T(8,128)S(1)}, u32[]{:S(2)}, u32[]{:S(2)}) collective-permute-start(f32[104,128]{1,0:T(8,128)S(1)} %add_add_fusion), channel_id=1, source_target_pairs={{0,96},{32,64},{64,32},{96,0},{1,97},{33,65},{65,33},{97,1},{2,98}... | collective-permute-start | bytes 159752 | tf_op jit(solution)/shard_map/ppermute | solution.py:367
  42.5 5.6 %collective-permute-start.12 = (f32[104,128]{1,0:T(8,128)S(1)}, f32[104,128]{1,0:T(8,128)S(1)}, u32[]{:S(2)}, u32[]{:S(2)}) collective-permute-start(f32[104,128]{1,0:T(8,128)S(1)} %add_add_fusion), channel_id=1, source_target_pairs={{0,64},{32,96},{64,0},{96,32},{1,65},{33,97},{65,1},{97,33},{2,66}... | collective-permute-start | bytes 159752 | tf_op jit(solution)/shard_map/ppermute | solution.py:367

commit v4 on v3

--- a/solution.py
+++ b/solution.py
@@ -293,8 +293,8 @@
 TILES = 13
 
 
-def solve_kernel(row_scale, first_ref, second_ref, factor_ref, step_ref, work):
-    work[...] = first_ref[...] + second_ref[...]
+def solve_kernel(row_scale, one_ref, three_ref, two_ref, own_ref, factor_ref, step_ref, work):
+    work[...] = (one_ref[...] + three_ref[...]) + (two_ref[...] + own_ref[...])
     lane = lax.broadcasted_iota(jnp.int32, (8, 128), 1)
     sub = lax.broadcasted_iota(jnp.int32, (8, 128), 0)
 
@@ -302,7 +302,8 @@
         return jnp.broadcast_to(tile[p : p + 1], (8, 128))
 
     def spread_lane(tile, j):
-        return jnp.broadcast_to(tile[:, j : j + 1], (8, 128))
+        place = jnp.full((8, 128), j, jnp.int32)
+        return jnp.take_along_axis(tile, place, axis=1, mode="promise_in_bounds")
 
     tiles = [work[8 * t : 8 * t + 8] for t in range(TILES)]
     for panel in range(12):
@@ -350,21 +351,26 @@
     step_ref[...] = step[:, :96] * (-1.0 / row_scale)
 
 
-def solve_call(row_scale, first, second):
+def solve_call(row_scale, *terms):
     return pl.pallas_call(
         functools.partial(solve_kernel, row_scale),
         out_shape=(jax.ShapeDtypeStruct((97, 97), F32), jax.ShapeDtypeStruct((1, 96), F32)),
-        in_specs=vmem(2),
+        in_specs=vmem(4),
         out_specs=tuple(vmem(2)),
         scratch_shapes=[pltpu.VMEM((104, 128), F32)],
         compiler_params=pltpu.CompilerParams(vmem_limit_bytes=VMEM_LIMIT),
         name="solve",
-    )(first, second)
+    )(*terms)
 
 
 def swap(x, axis, step):
     count = lax.axis_size(axis)
     return lax.ppermute(x, axis, [(i, i ^ step) for i in range(count)])
+
+
+def cross(x, axis, step):
+    pairs = [(2 * i + c, 2 * (i ^ step) + 1 - c) for i in range(lax.axis_size(axis)) for c in range(2)]
+    return lax.ppermute(x, (axis, "col_1"), pairs)
 
 
 def swap_odd(x, axis):
@@ -413,10 +419,10 @@
     test, gram = finish_call(row_scale, image, row_a, row_b, col_a, col_b, hot, coef, base)
     gram = gram + swap(gram, "col_1", 1)
     for axis in ("col_0", "row_1", "row_0"):
-        one, two, three = (swap(gram, axis, k) for k in (1, 2, 3))
-        first, second = gram + one, two + three
-        gram = first + second
-    factor, step = solve_call(row_scale, first, second)
+        one, three, two = (cross(gram, axis, k) for k in (1, 3, 2))
+        terms = (one, three, two, gram)
+        gram = (one + three) + (two + gram)
+    factor, step = solve_call(row_scale, *terms)
     return (test, factor, step.reshape(K))
 
 

time: 53.4 us -> 49.7 us (0.931)
  the two profiles are of different devices: /device:TPU:0 before, /device:TPU:1 now
where the time goes in v4:
time: 49.7 us; the launch traced here: 49.5 us
  starting transfers between devices  25.1 us (51%)
  waiting for transfers between devices  12 us (24%)
  Pallas kernels  11.6 us (23%)
  between operations  0.75 us (2%)
    ppermute x9, starting transfers between devices, cross(): return lax.ppermute(x, (axis, 'col_1'), pairs)  17.2 us
    ppermute x9, waiting for transfers between devices, cross(): return lax.ppermute(x, (axis, 'col_1'), pairs)  11.1 us
    ppermute x2, starting transfers between devices, swap_odd(): return lax.ppermute(x, axis, pairs)  5.04 us
    pallas_call x1, Pallas kernels, solve_call(): pl.pallas_call(functools.partial(solve_kernel, row_scale), out_shape=(jax...  3.64 us
    ppermute x3, starting transfers between devices, swap(): return lax.ppermute(x, axis, [(i, i ^ step) for i in range(count)])  2.78 us
    pallas_call x1, Pallas kernels, late_call(): pl.pallas_call(late_kernel, out_shape=jax.ShapeDtypeStruct((WIDE, C), F32...  2.52 us
    pallas_call x1, Pallas kernels, early_call(): pl.pallas_call(early_kernel, out_shape=(jax.ShapeDtypeStruct((WIDE, C), F...  2.1 us
    pallas_call x1, Pallas kernels, ghost_call(): pl.pallas_call(ghost_kernel, out_shape=(message,) * 4 + tuple((jax.ShapeD...  1.92 us
  transfers between devices with their start and end apart: 14, of which 8 were waited for; matrix products, arithmetic and copies ran while one was open for 0% of the time, Pallas kernels for 9%

profile of v4, /device:TPU:1, one launch (start us, length us, event | category | flops | bytes accessed | tf_op | source)
XLA Modules:
  0.0 49.5 jit_solution(6019542312364513394)
XLA Ops:
  0.6 1.9 %ghost.1 = (bf16[240,128]{1,0:T(8,128)(2,1)S(1)}, bf16[240,128]{1,0:T(8,128)(2,1)S(1)}, bf16[240,128]{1,0:T(8,128)(2,1)S(1)}, bf16[240,128]{1,0:T(8,128)(2,1)S(1...) custom-call(s32[1,8]{1,0:T(1,128)} %bitcast.14, ...), custom_call_target="tpu_custom_call" | custom-call | tf_op jit(solution)/shard_map/ghost/pallas_call | solution.py:130
  2.6 2.2 %collective-permute-start = (bf16[240,128]{1,0:T(8,128)(2,1)S(1)}, bf16[240,128]{1,0:T(8,128)(2,1)S(1)}, u32[]{:S(2)}, u32[]{:S(2)}) collective-permute-start(bf16[240,128]{1,0:T(8,128)(2,1)S(1)} %get-tuple-element.32), channel_id=1, source_target_pairs={{0,8},{8,0},{16,24},{24,16},{32,40},{40,32},{48,56},{56,48},{64,72... | collective-permute-start | bytes 184328 | tf_op jit(solution)/shard_map/ppermute | solution.py:368
  4.8 0.7 %collective-permute-start.1 = (bf16[240,128]{1,0:T(8,128)(2,1)S(1)}, bf16[240,128]{1,0:T(8,128)(2,1)S(1)}, u32[]{:S(2)}, u32[]{:S(2)}) collective-permute-start(bf16[240,128]{1,0:T(8,128)(2,1)S(1)} %get-tuple-element.33), channel_id=1, source_target_pairs={{8,16},{16,8},{24,32},{32,24},{40,48},{48,40},{56,64},{64,56},{72,... | collective-permute-start | bytes 184328 | tf_op jit(solution)/shard_map/ppermute | solution.py:380
  5.4 2.1 %early_faces.1 = (f32[496,512]{1,0:T(8,128)S(1)}, bf16[512,256]{1,0:T(8,128)(2,1)S(1)}, bf16[16,96]{1,0:T(8,128)(2,1)S(1)}) custom-call(f32[1,5]{1,0:T(1,128)S(1)} %get-tuple-element.23.nu_ref, bf16[480,512]{1,0:T(8,128)(2,1)S(1)} %get-tuple-element.24.basis_ref, s32[2,1024]{1,0:T(2,128)S(1)} %get-tuple-element.26.pair_ref, ...), custom_call_target="tpu_custom_call" | custom-call | flops 2500000000 | bytes 2000000 | tf_op jit(solution)/shard_map/early_faces/pallas_call | solution.py:225
  7.6 0.0 collective-permute-done.row_a
  7.6 0.0 collective-permute-done.1.row_b
  7.6 4.4 %collective-permute-start.3 = (bf16[240,128]{1,0:T(8,128)(2,1)S(1)}, bf16[240,128]{1,0:T(8,128)(2,1)S(1)}, u32[]{:S(2)}, u32[]{:S(2)}) collective-permute-start(bf16[240,128]{1,0:T(8,128)(2,1)S(1)} %get-tuple-element.43), channel_id=1, source_target_pairs={{1,2},{2,1},{3,4},{4,3},{5,6},{6,5},{9,10},{10,9},{11,12},{12,11},... | collective-permute-start | bytes 184328 | tf_op jit(solution)/shard_map/ppermute | solution.py:380
  12.0 0.1 collective-permute-start.2
  12.1 2.5 %late_faces.1.image_ref = f32[496,512]{1,0:T(8,128)S(1)} custom-call(f32[1,5]{1,0:T(1,128)S(1)} %get-tuple-element.23.nu_ref, bf16[480,512]{1,0:T(8,128)(2,1)S(1)} %get-tuple-element.24.basis_ref, f32[5,5,512]{2,1,0:T(8,128)S(1)} %get-tuple-element.25.diag_ref, s32[2,1024]{1,0:T(2,128)S(1)} %get-tuple-element.26.pair_ref, ...), custom_call_target="tpu_custom_call" | custom-call | flops 2500000000 | bytes 2000000 | tf_op jit(solution)/shard_map/late_faces/pallas_call | solution.py:242
  14.6 0.0 collective-permute-done.3.col_b
  14.7 0.0 collective-permute-done.2.col_a
  14.7 1.4 %finish.1 = (bf16[5,96,512]{2,1,0:T(8,128)(2,1)}, f32[104,128]{1,0:T(8,128)S(1)}) custom-call(f32[496,512]{1,0:T(8,128)S(1)} %late_faces.1.image_ref, bf16[240,128]{1,0:T(8,128)(2,1)S(1)} %collective-permute-done.row_a, bf16[240,128]{1,0:T(8,128)(2,1)S(1)} %collective-permute-done.1.row_b, bf16[240,128]{1,0:T(8,128)(2,1)S(1)} %collective-permute-done.2.col_a, ...), custom_call_target="tpu_custom_call" | custom-call | tf_op jit(solution)/shard_map/finish/pallas_call | solution.py:282
  16.1 0.5 collective-permute-start.4
  16.6 0.9 %collective-permute-done.4 = f32[104,128]{1,0:T(8,128)S(1)} collective-permute-done((f32[104,128]{1,0:T(8,128)S(1)}, f32[104,128]{1,0:T(8,128)S(1)}, u32[]{:S(2)}, u32[]{:S(2)}) %collective-permute-start.4) | collective-permute-done | bytes 53280 | tf_op jit(solution)/shard_map/ppermute | solution.py:368
  17.5 3.6 %collective-permute-start.7 = (f32[104,128]{1,0:T(8,128)S(1)}, f32[104,128]{1,0:T(8,128)S(1)}, u32[]{:S(2)}, u32[]{:S(2)}) collective-permute-start(f32[104,128]{1,0:T(8,128)S(1)} %add.36), channel_id=1, source_target_pairs={{0,5},{1,4},{2,7},{3,6},{4,1},{5,0},{6,3},{7,2},{8,13},{9,12},{10,... | collective-permute-start | bytes 159752 | tf_op jit(solution)/shard_map/ppermute | solution.py:373
  21.1 0.7 %collective-permute-start.6 = (f32[104,128]{1,0:T(8,128)S(1)}, f32[104,128]{1,0:T(8,128)S(1)}, u32[]{:S(2)}, u32[]{:S(2)}) collective-permute-start(f32[104,128]{1,0:T(8,128)S(1)} %add.36), channel_id=1, source_target_pairs={{0,7},{1,6},{2,5},{3,4},{4,3},{5,2},{6,1},{7,0},{8,15},{9,14},{10,... | collective-permute-start | bytes 159752 | tf_op jit(solution)/shard_map/ppermute | solution.py:373
  21.8 0.0 collective-permute-start.5
  21.8 1.1 %collective-permute-done.7 = f32[104,128]{1,0:T(8,128)S(1)} collective-permute-done((f32[104,128]{1,0:T(8,128)S(1)}, f32[104,128]{1,0:T(8,128)S(1)}, u32[]{:S(2)}, u32[]{:S(2)}) %collective-permute-start.7) | collective-permute-done | bytes 53280 | tf_op jit(solution)/shard_map/ppermute | solution.py:373
  22.9 3.0 %collective-permute-done.6 = f32[104,128]{1,0:T(8,128)S(1)} collective-permute-done((f32[104,128]{1,0:T(8,128)S(1)}, f32[104,128]{1,0:T(8,128)S(1)}, u32[]{:S(2)}, u32[]{:S(2)}) %collective-permute-start.6) | collective-permute-done | bytes 53280 | tf_op jit(solution)/shard_map/ppermute | solution.py:373
  25.9 0.0 collective-permute-done.5
  25.9 6.1 %collective-permute-start.10 = (f32[104,128]{1,0:T(8,128)S(1)}, f32[104,128]{1,0:T(8,128)S(1)}, u32[]{:S(2)}, u32[]{:S(2)}) collective-permute-start(f32[104,128]{1,0:T(8,128)S(1)} %add_add_fusion.1), channel_id=1, source_target_pairs={{0,17},{1,16},{8,25},{9,24},{16,1},{17,0},{24,9},{25,8},{2,19},{3,... | collective-permute-start | bytes 159752 | tf_op jit(solution)/shard_map/ppermute | solution.py:373
  32.0 1.5 %collective-permute-start.9 = (f32[104,128]{1,0:T(8,128)S(1)}, f32[104,128]{1,0:T(8,128)S(1)}, u32[]{:S(2)}, u32[]{:S(2)}) collective-permute-start(f32[104,128]{1,0:T(8,128)S(1)} %add_add_fusion.1), channel_id=1, source_target_pairs={{0,25},{1,24},{8,17},{9,16},{16,9},{17,8},{24,1},{25,0},{2,27},{3,... | collective-permute-start | bytes 159752 | tf_op jit(solution)/shard_map/ppermute | solution.py:373
  33.5 0.7 %collective-permute-start.8 = (f32[104,128]{1,0:T(8,128)S(1)}, f32[104,128]{1,0:T(8,128)S(1)}, u32[]{:S(2)}, u32[]{:S(2)}) collective-permute-start(f32[104,128]{1,0:T(8,128)S(1)} %add_add_fusion.1), channel_id=1, source_target_pairs={{0,9},{1,8},{8,1},{9,0},{16,25},{17,24},{24,17},{25,16},{2,11},{3,... | collective-permute-start | bytes 159752 | tf_op jit(solution)/shard_map/ppermute | solution.py:373
  34.2 0.0 collective-permute-done.10
  34.2 2.8 %collective-permute-done.9 = f32[104,128]{1,0:T(8,128)S(1)} collective-permute-done((f32[104,128]{1,0:T(8,128)S(1)}, f32[104,128]{1,0:T(8,128)S(1)}, u32[]{:S(2)}, u32[]{:S(2)}) %collective-permute-start.9) | collective-permute-done | bytes 53280 | tf_op jit(solution)/shard_map/ppermute | solution.py:373
  37.0 0.3 collective-permute-done.8
  37.3 3.7 %collective-permute-start.13 = (f32[104,128]{1,0:T(8,128)S(1)}, f32[104,128]{1,0:T(8,128)S(1)}, u32[]{:S(2)}, u32[]{:S(2)}) collective-permute-start(f32[104,128]{1,0:T(8,128)S(1)} %add_add_fusion.own_ref), channel_id=1, source_target_pairs={{0,65},{1,64},{32,97},{33,96},{64,1},{65,0},{96,33},{97,32},{2,67}... | collective-permute-start | bytes 159752 | tf_op jit(solution)/shard_map/ppermute | solution.py:373
  41.0 1.0 %collective-permute-start.12 = (f32[104,128]{1,0:T(8,128)S(1)}, f32[104,128]{1,0:T(8,128)S(1)}, u32[]{:S(2)}, u32[]{:S(2)}) collective-permute-start(f32[104,128]{1,0:T(8,128)S(1)} %add_add_fusion.own_ref), channel_id=1, source_target_pairs={{0,97},{1,96},{32,65},{33,64},{64,33},{65,32},{96,1},{97,0},{2,99}... | collective-permute-start | bytes 159752 | tf_op jit(solution)/shard_map/ppermute | solution.py:373
  42.0 0.0 collective-permute-start.11
  42.0 0.8 %collective-permute-done.13.two_ref = f32[104,128]{1,0:T(8,128)S(1)} collective-permute-done((f32[104,128]{1,0:T(8,128)S(1)}, f32[104,128]{1,0:T(8,128)S(1)}, u32[]{:S(2)}, u32[]{:S(2)}) %collective-permute-start.13) | collective-permute-done | bytes 53280 | tf_op jit(solution)/shard_map/ppermute | solution.py:373
  42.8 3.0 %collective-permute-done.12.three_ref = f32[104,128]{1,0:T(8,128)S(1)} collective-permute-done((f32[104,128]{1,0:T(8,128)S(1)}, f32[104,128]{1,0:T(8,128)S(1)}, u32[]{:S(2)}, u32[]{:S(2)}) %collective-permute-start.12) | collective-permute-done | bytes 53280 | tf_op jit(solution)/shard_map/ppermute | solution.py:373
  45.8 0.1 collective-permute-done.11.one_ref
  45.9 3.6 %solve.1 = (f32[97,97]{1,0:T(8,128)}, f32[1,96]{1,0:T(1,128)}) custom-call(f32[104,128]{1,0:T(8,128)S(1)} %collective-permute-done.11.one_ref, f32[104,128]{1,0:T(8,128)S(1)} %collective-permute-done.12.three_ref, f32[104,128]{1,0:T(8,128)S(1)} %collective-permute-done.13.two_ref, f32[104,128]{1,0:T(8,128)S(1)} %add_add_fusion.own_ref), custom_call_target="tpu_custom_call" | custom-call | tf_op jit(solution)/shard_map/solve/pallas_call | solution.py:355
  (6 shorter events, 0.1 us)
Async XLA Ops:
  2.6 5.0 %collective-permute-start = (bf16[240,128]{1,0:T(8,128)(2,1)S(1)}, bf16[240,128]{1,0:T(8,128)(2,1)S(1)}, u32[]{:S(2)}, u32[]{:S(2)}) collective-permute-start(bf16[240,128]{1,0:T(8,128)(2,1)S(1)} %get-tuple-element.32), channel_id=1, source_target_pairs={{0,8},{8,0},{16,24},{24,16},{32,40},{40,32},{48,56},{56,48},{64,72... | collective-permute-start | bytes 184328 | tf_op jit(solution)/shard_map/ppermute | solution.py:368
  4.8 2.8 %collective-permute-start.1 = (bf16[240,128]{1,0:T(8,128)(2,1)S(1)}, bf16[240,128]{1,0:T(8,128)(2,1)S(1)}, u32[]{:S(2)}, u32[]{:S(2)}) collective-permute-start(bf16[240,128]{1,0:T(8,128)(2,1)S(1)} %get-tuple-element.33), channel_id=1, source_target_pairs={{8,16},{16,8},{24,32},{32,24},{40,48},{48,40},{56,64},{64,56},{72,... | collective-permute-start | bytes 184328 | tf_op jit(solution)/shard_map/ppermute | solution.py:380
  7.6 7.0 %collective-permute-start.3 = (bf16[240,128]{1,0:T(8,128)(2,1)S(1)}, bf16[240,128]{1,0:T(8,128)(2,1)S(1)}, u32[]{:S(2)}, u32[]{:S(2)}) collective-permute-start(bf16[240,128]{1,0:T(8,128)(2,1)S(1)} %get-tuple-element.43), channel_id=1, source_target_pairs={{1,2},{2,1},{3,4},{4,3},{5,6},{6,5},{9,10},{10,9},{11,12},{12,11},... | collective-permute-start | bytes 184328 | tf_op jit(solution)/shard_map/ppermute | solution.py:380
  12.0 2.6 %collective-permute-start.2 = (bf16[240,128]{1,0:T(8,128)(2,1)S(1)}, bf16[240,128]{1,0:T(8,128)(2,1)S(1)}, u32[]{:S(2)}, u32[]{:S(2)}) collective-permute-start(bf16[240,128]{1,0:T(8,128)(2,1)S(1)} %get-tuple-element.44), channel_id=1, source_target_pairs={{0,1},{1,0},{2,3},{3,2},{4,5},{5,4},{6,7},{7,6},{8,9},{9,8},{10,11... | collective-permute-start | bytes 184328 | tf_op jit(solution)/shard_map/ppermute | solution.py:368
  16.1 1.4 %collective-permute-start.4 = (f32[104,128]{1,0:T(8,128)S(1)}, f32[104,128]{1,0:T(8,128)S(1)}, u32[]{:S(2)}, u32[]{:S(2)}) collective-permute-start(f32[104,128]{1,0:T(8,128)S(1)} %get-tuple-element.40), channel_id=1, source_target_pairs={{0,1},{1,0},{2,3},{3,2},{4,5},{5,4},{6,7},{7,6},{8,9},{9,8},{10,11... | collective-permute-start | bytes 159752 | tf_op jit(solution)/shard_map/ppermute | solution.py:368
  17.5 5.4 %collective-permute-start.7 = (f32[104,128]{1,0:T(8,128)S(1)}, f32[104,128]{1,0:T(8,128)S(1)}, u32[]{:S(2)}, u32[]{:S(2)}) collective-permute-start(f32[104,128]{1,0:T(8,128)S(1)} %add.36), channel_id=1, source_target_pairs={{0,5},{1,4},{2,7},{3,6},{4,1},{5,0},{6,3},{7,2},{8,13},{9,12},{10,... | collective-permute-start | bytes 159752 | tf_op jit(solution)/shard_map/ppermute | solution.py:373
  21.1 4.8 %collective-permute-start.6 = (f32[104,128]{1,0:T(8,128)S(1)}, f32[104,128]{1,0:T(8,128)S(1)}, u32[]{:S(2)}, u32[]{:S(2)}) collective-permute-start(f32[104,128]{1,0:T(8,128)S(1)} %add.36), channel_id=1, source_target_pairs={{0,7},{1,6},{2,5},{3,4},{4,3},{5,2},{6,1},{7,0},{8,15},{9,14},{10,... | collective-permute-start | bytes 159752 | tf_op jit(solution)/shard_map/ppermute | solution.py:373
  21.8 4.1 %collective-permute-start.5 = (f32[104,128]{1,0:T(8,128)S(1)}, f32[104,128]{1,0:T(8,128)S(1)}, u32[]{:S(2)}, u32[]{:S(2)}) collective-permute-start(f32[104,128]{1,0:T(8,128)S(1)} %add.36), channel_id=1, source_target_pairs={{0,3},{1,2},{2,1},{3,0},{4,7},{5,6},{6,5},{7,4},{8,11},{9,10},{10,... | collective-permute-start | bytes 159752 | tf_op jit(solution)/shard_map/ppermute | solution.py:373
  25.9 8.2 %collective-permute-start.10 = (f32[104,128]{1,0:T(8,128)S(1)}, f32[104,128]{1,0:T(8,128)S(1)}, u32[]{:S(2)}, u32[]{:S(2)}) collective-permute-start(f32[104,128]{1,0:T(8,128)S(1)} %add_add_fusion.1), channel_id=1, source_target_pairs={{0,17},{1,16},{8,25},{9,24},{16,1},{17,0},{24,9},{25,8},{2,19},{3,... | collective-permute-start | bytes 159752 | tf_op jit(solution)/shard_map/ppermute | solution.py:373
  32.0 4.9 %collective-permute-start.9 = (f32[104,128]{1,0:T(8,128)S(1)}, f32[104,128]{1,0:T(8,128)S(1)}, u32[]{:S(2)}, u32[]{:S(2)}) collective-permute-start(f32[104,128]{1,0:T(8,128)S(1)} %add_add_fusion.1), channel_id=1, source_target_pairs={{0,25},{1,24},{8,17},{9,16},{16,9},{17,8},{24,1},{25,0},{2,27},{3,... | collective-permute-start | bytes 159752 | tf_op jit(solution)/shard_map/ppermute | solution.py:373
  33.5 3.8 %collective-permute-start.8 = (f32[104,128]{1,0:T(8,128)S(1)}, f32[104,128]{1,0:T(8,128)S(1)}, u32[]{:S(2)}, u32[]{:S(2)}) collective-permute-start(f32[104,128]{1,0:T(8,128)S(1)} %add_add_fusion.1), channel_id=1, source_target_pairs={{0,9},{1,8},{8,1},{9,0},{16,25},{17,24},{24,17},{25,16},{2,11},{3,... | collective-permute-start | bytes 159752 | tf_op jit(solution)/shard_map/ppermute | solution.py:373
  37.3 5.5 %collective-permute-start.13 = (f32[104,128]{1,0:T(8,128)S(1)}, f32[104,128]{1,0:T(8,128)S(1)}, u32[]{:S(2)}, u32[]{:S(2)}) collective-permute-start(f32[104,128]{1,0:T(8,128)S(1)} %add_add_fusion.own_ref), channel_id=1, source_target_pairs={{0,65},{1,64},{32,97},{33,96},{64,1},{65,0},{96,33},{97,32},{2,67}... | collective-permute-start | bytes 159752 | tf_op jit(solution)/shard_map/ppermute | solution.py:373
  41.0 4.8 %collective-permute-start.12 = (f32[104,128]{1,0:T(8,128)S(1)}, f32[104,128]{1,0:T(8,128)S(1)}, u32[]{:S(2)}, u32[]{:S(2)}) collective-permute-start(f32[104,128]{1,0:T(8,128)S(1)} %add_add_fusion.own_ref), channel_id=1, source_target_pairs={{0,97},{1,96},{32,65},{33,64},{64,33},{65,32},{96,1},{97,0},{2,99}... | collective-permute-start | bytes 159752 | tf_op jit(solution)/shard_map/ppermute | solution.py:373
  42.0 3.9 %collective-permute-start.11 = (f32[104,128]{1,0:T(8,128)S(1)}, f32[104,128]{1,0:T(8,128)S(1)}, u32[]{:S(2)}, u32[]{:S(2)}) collective-permute-start(f32[104,128]{1,0:T(8,128)S(1)} %add_add_fusion.own_ref), channel_id=1, source_target_pairs={{0,33},{1,32},{32,1},{33,0},{64,97},{65,96},{96,65},{97,64},{2,35}... | collective-permute-start | bytes 159752 | tf_op jit(solution)/shard_map/ppermute | solution.py:373

commit v5 on v4

--- a/solution.py
+++ b/solution.py
@@ -76,6 +76,12 @@
     return row, jnp.where(odd_j, odd, even)
 
 
+BLOCK_AIMS = (
+    (0, -1, 0), (32, 1, 0), (64, 0, -1), (96, 0, 1),
+    (128, -1, -1), (136, -1, 1), (144, 1, -1), (152, 1, 1),
+)
+
+
 def parities():
     return lax.axis_index("row_1") % 2 == 1, lax.axis_index("col_1") % 2 == 1
 
@@ -96,9 +102,18 @@
     copies[1].wait()
     copies[2].wait()
     lane = lax.broadcasted_iota(jnp.int32, (1, S), 1)
+    at_i = lax.axis_index("row_0") * lax.axis_size("row_1") + lax.axis_index("row_1")
+    at_j = lax.axis_index("col_0") * lax.axis_size("col_1") + lax.axis_index("col_1")
+    end_i = lax.axis_size("row_0") * lax.axis_size("row_1") - 1
+    end_j = lax.axis_size("col_0") * lax.axis_size("col_1") - 1
     limit = jnp.zeros((1, S), jnp.int32)
-    for block, start in enumerate((0, 32, 64, 96, 128, 136, 144, 152)):
-        limit = jnp.where(lane >= start, count_ref[0:1, block : block + 1] + start, limit)
+    for block, (start, dr, dc) in enumerate(BLOCK_AIMS):
+        count = count_ref[0:1, block : block + 1]
+        if dr:
+            count = jnp.where(at_i == (0 if dr < 0 else end_i), 0, count)
+        if dc:
+            count = jnp.where(at_j == (0 if dc < 0 else end_j), 0, count)
+        limit = jnp.where(lane >= start, count + start, limit)
     index = jnp.where(lane < limit, cell_ref[...], -1)
     hot = one_hot(jnp.concatenate(send_order(index, -1, odd_i, odd_j), axis=-1))
     copies[3].wait()
@@ -374,10 +389,8 @@
 
 
 def swap_odd(x, axis):
-    pairs = []
-    for i in range(1, lax.axis_size(axis) - 1, 2):
-        pairs += [(i, i + 1), (i + 1, i)]
-    return lax.ppermute(x, axis, pairs)
+    count = lax.axis_size(axis)
+    return lax.ppermute(x, axis, [(i, (i + 1) % count if i % 2 else (i - 1) % count) for i in range(count)])
 
 
 def local(

time: 49.7 us -> 45.9 us (0.924)
  starting transfers between devices: 25.1 us -> 21.2 us
    ppermute x9, starting transfers between devices: 17.2 us -> 10.4 us  [cross(): return lax.ppermute(x, (axis, 'col_1'), pairs)]
    ppermute x2, starting transfers between devices: 5.04 us -> 7.79 us  [swap_odd(): lax.ppermute(x, axis, [(i, (i + 1) % count if i % 2 else (i - 1) % count)...]
  transfers between devices with their start and end apart: 14 -> 14, of which waited for: 8 -> 8; matrix products, arithmetic and copies ran while one was open for 0% -> 0% of each run, Pallas kernels for 9% -> 10%
where the time goes in v5:
time: 45.9 us; the launch traced here: 45.8 us
  starting transfers between devices  21.2 us (46%)
  waiting for transfers between devices  12.2 us (27%)
  Pallas kernels  11.6 us (25%)
  between operations  0.72 us (2%)
    ppermute x9, waiting for transfers between devices, cross(): return lax.ppermute(x, (axis, 'col_1'), pairs)  11 us
    ppermute x9, starting transfers between devices, cross(): return lax.ppermute(x, (axis, 'col_1'), pairs)  10.4 us
    ppermute x2, starting transfers between devices, swap_odd(): lax.ppermute(x, axis, [(i, (i + 1) % count if i % 2 else (i - 1) % count)...  7.79 us
    pallas_call x1, Pallas kernels, solve_call(): pl.pallas_call(functools.partial(solve_kernel, row_scale), out_shape=(jax...  3.65 us
    ppermute x3, starting transfers between devices, swap(): return lax.ppermute(x, axis, [(i, i ^ step) for i in range(count)])  3.01 us
    pallas_call x1, Pallas kernels, late_call(): pl.pallas_call(late_kernel, out_shape=jax.ShapeDtypeStruct((WIDE, C), F32...  2.51 us
    pallas_call x1, Pallas kernels, early_call(): pl.pallas_call(early_kernel, out_shape=(jax.ShapeDtypeStruct((WIDE, C), F...  2.09 us
    pallas_call x1, Pallas kernels, ghost_call(): pl.pallas_call(ghost_kernel, out_shape=(message,) * 4 + tuple((jax.ShapeD...  1.92 us
  transfers between devices with their start and end apart: 14, of which 8 were waited for; matrix products, arithmetic and copies ran while one was open for 0% of the time, Pallas kernels for 10%

profile of v5, /device:TPU:1, one launch (start us, length us, event | category | flops | bytes accessed | tf_op | source)
XLA Modules:
  0.0 45.8 jit_solution(6243514302929508697)
XLA Ops:
  0.6 1.9 %ghost.1 = (bf16[240,128]{1,0:T(8,128)(2,1)S(1)}, bf16[240,128]{1,0:T(8,128)(2,1)S(1)}, bf16[240,128]{1,0:T(8,128)(2,1)S(1)}, bf16[240,128]{1,0:T(8,128)(2,1)S(1...) custom-call(s32[1,8]{1,0:T(1,128)} %bitcast.14, ...), custom_call_target="tpu_custom_call" | custom-call | tf_op jit(solution)/shard_map/ghost/pallas_call | solution.py:145
  2.6 2.2 %collective-permute-start = (bf16[240,128]{1,0:T(8,128)(2,1)S(1)}, bf16[240,128]{1,0:T(8,128)(2,1)S(1)}, u32[]{:S(2)}, u32[]{:S(2)}) collective-permute-start(bf16[240,128]{1,0:T(8,128)(2,1)S(1)} %get-tuple-element.32), channel_id=1, source_target_pairs={{0,8},{8,0},{16,24},{24,16},{32,40},{40,32},{48,56},{56,48},{64,72... | collective-permute-start | bytes 184328 | tf_op jit(solution)/shard_map/ppermute | solution.py:383
  4.8 4.1 %collective-permute-start.1 = (bf16[240,128]{1,0:T(8,128)(2,1)S(1)}, bf16[240,128]{1,0:T(8,128)(2,1)S(1)}, u32[]{:S(2)}, u32[]{:S(2)}) collective-permute-start(bf16[240,128]{1,0:T(8,128)(2,1)S(1)} %get-tuple-element.33), channel_id=1, source_target_pairs={{0,120},{8,16},{16,8},{24,32},{32,24},{40,48},{48,40},{56,64},{64,... | collective-permute-start | bytes 184328 | tf_op jit(solution)/shard_map/ppermute | solution.py:393
  8.9 2.1 %early_faces.1 = (f32[496,512]{1,0:T(8,128)S(1)}, bf16[512,256]{1,0:T(8,128)(2,1)S(1)}, bf16[16,96]{1,0:T(8,128)(2,1)S(1)}) custom-call(f32[1,5]{1,0:T(1,128)S(1)} %get-tuple-element.23.nu_ref, bf16[480,512]{1,0:T(8,128)(2,1)S(1)} %get-tuple-element.24.basis_ref, s32[2,1024]{1,0:T(2,128)S(1)} %get-tuple-element.26.pair_ref, ...), custom_call_target="tpu_custom_call" | custom-call | flops 2500000000 | bytes 2000000 | tf_op jit(solution)/shard_map/early_faces/pallas_call | solution.py:240
  11.0 0.0 collective-permute-done.row_a
  11.0 0.2 collective-permute-done.1.row_b
  11.2 3.7 %collective-permute-start.3 = (bf16[240,128]{1,0:T(8,128)(2,1)S(1)}, bf16[240,128]{1,0:T(8,128)(2,1)S(1)}, u32[]{:S(2)}, u32[]{:S(2)}) collective-permute-start(bf16[240,128]{1,0:T(8,128)(2,1)S(1)} %get-tuple-element.43), channel_id=1, source_target_pairs={{0,7},{1,2},{2,1},{3,4},{4,3},{5,6},{6,5},{7,0},{8,15},{9,10},{10,... | collective-permute-start | bytes 184328 | tf_op jit(solution)/shard_map/ppermute | solution.py:393
  14.9 0.5 %collective-permute-start.2 = (bf16[240,128]{1,0:T(8,128)(2,1)S(1)}, bf16[240,128]{1,0:T(8,128)(2,1)S(1)}, u32[]{:S(2)}, u32[]{:S(2)}) collective-permute-start(bf16[240,128]{1,0:T(8,128)(2,1)S(1)} %get-tuple-element.44), channel_id=1, source_target_pairs={{0,1},{1,0},{2,3},{3,2},{4,5},{5,4},{6,7},{7,6},{8,9},{9,8},{10,11... | collective-permute-start | bytes 184328 | tf_op jit(solution)/shard_map/ppermute | solution.py:383
  15.4 2.5 %late_faces.1.image_ref = f32[496,512]{1,0:T(8,128)S(1)} custom-call(f32[1,5]{1,0:T(1,128)S(1)} %get-tuple-element.23.nu_ref, bf16[480,512]{1,0:T(8,128)(2,1)S(1)} %get-tuple-element.24.basis_ref, f32[5,5,512]{2,1,0:T(8,128)S(1)} %get-tuple-element.25.diag_ref, s32[2,1024]{1,0:T(2,128)S(1)} %get-tuple-element.26.pair_ref, ...), custom_call_target="tpu_custom_call" | custom-call | flops 2500000000 | bytes 2000000 | tf_op jit(solution)/shard_map/late_faces/pallas_call | solution.py:257
  18.0 0.0 collective-permute-done.3.col_b
  18.0 0.0 collective-permute-done.2.col_a
  18.0 1.4 %finish.1 = (bf16[5,96,512]{2,1,0:T(8,128)(2,1)}, f32[104,128]{1,0:T(8,128)S(1)}) custom-call(f32[496,512]{1,0:T(8,128)S(1)} %late_faces.1.image_ref, bf16[240,128]{1,0:T(8,128)(2,1)S(1)} %collective-permute-done.row_a, bf16[240,128]{1,0:T(8,128)(2,1)S(1)} %collective-permute-done.1.row_b, bf16[240,128]{1,0:T(8,128)(2,1)S(1)} %collective-permute-done.2.col_a, ...), custom_call_target="tpu_custom_call" | custom-call | tf_op jit(solution)/shard_map/finish/pallas_call | solution.py:297
  19.4 0.3 collective-permute-start.4
  19.7 1.0 %collective-permute-done.4 = f32[104,128]{1,0:T(8,128)S(1)} collective-permute-done((f32[104,128]{1,0:T(8,128)S(1)}, f32[104,128]{1,0:T(8,128)S(1)}, u32[]{:S(2)}, u32[]{:S(2)}) %collective-permute-start.4) | collective-permute-done | bytes 53280 | tf_op jit(solution)/shard_map/ppermute | solution.py:383
  20.7 3.2 %collective-permute-start.7 = (f32[104,128]{1,0:T(8,128)S(1)}, f32[104,128]{1,0:T(8,128)S(1)}, u32[]{:S(2)}, u32[]{:S(2)}) collective-permute-start(f32[104,128]{1,0:T(8,128)S(1)} %add.36), channel_id=1, source_target_pairs={{0,5},{1,4},{2,7},{3,6},{4,1},{5,0},{6,3},{7,2},{8,13},{9,12},{10,... | collective-permute-start | bytes 159752 | tf_op jit(solution)/shard_map/ppermute | solution.py:388
  23.9 0.7 %collective-permute-start.6 = (f32[104,128]{1,0:T(8,128)S(1)}, f32[104,128]{1,0:T(8,128)S(1)}, u32[]{:S(2)}, u32[]{:S(2)}) collective-permute-start(f32[104,128]{1,0:T(8,128)S(1)} %add.36), channel_id=1, source_target_pairs={{0,7},{1,6},{2,5},{3,4},{4,3},{5,2},{6,1},{7,0},{8,15},{9,14},{10,... | collective-permute-start | bytes 159752 | tf_op jit(solution)/shard_map/ppermute | solution.py:388
  24.7 0.0 collective-permute-start.5
  24.7 1.3 %collective-permute-done.7 = f32[104,128]{1,0:T(8,128)S(1)} collective-permute-done((f32[104,128]{1,0:T(8,128)S(1)}, f32[104,128]{1,0:T(8,128)S(1)}, u32[]{:S(2)}, u32[]{:S(2)}) %collective-permute-start.7) | collective-permute-done | bytes 53280 | tf_op jit(solution)/shard_map/ppermute | solution.py:388
  26.0 2.8 %collective-permute-done.6 = f32[104,128]{1,0:T(8,128)S(1)} collective-permute-done((f32[104,128]{1,0:T(8,128)S(1)}, f32[104,128]{1,0:T(8,128)S(1)}, u32[]{:S(2)}, u32[]{:S(2)}) %collective-permute-start.6) | collective-permute-done | bytes 53280 | tf_op jit(solution)/shard_map/ppermute | solution.py:388
  28.7 0.0 collective-permute-done.5
  28.7 0.1 collective-permute-start.10
  28.8 0.9 %collective-permute-start.9 = (f32[104,128]{1,0:T(8,128)S(1)}, f32[104,128]{1,0:T(8,128)S(1)}, u32[]{:S(2)}, u32[]{:S(2)}) collective-permute-start(f32[104,128]{1,0:T(8,128)S(1)} %add_add_fusion.1), channel_id=1, source_target_pairs={{0,25},{1,24},{8,17},{9,16},{16,9},{17,8},{24,1},{25,0},{2,27},{3,... | collective-permute-start | bytes 159752 | tf_op jit(solution)/shard_map/ppermute | solution.py:388
  29.7 2.1 %collective-permute-start.8 = (f32[104,128]{1,0:T(8,128)S(1)}, f32[104,128]{1,0:T(8,128)S(1)}, u32[]{:S(2)}, u32[]{:S(2)}) collective-permute-start(f32[104,128]{1,0:T(8,128)S(1)} %add_add_fusion.1), channel_id=1, source_target_pairs={{0,9},{1,8},{8,1},{9,0},{16,25},{17,24},{24,17},{25,16},{2,11},{3,... | collective-permute-start | bytes 159752 | tf_op jit(solution)/shard_map/ppermute | solution.py:388
  31.9 2.2 %collective-permute-done.10 = f32[104,128]{1,0:T(8,128)S(1)} collective-permute-done((f32[104,128]{1,0:T(8,128)S(1)}, f32[104,128]{1,0:T(8,128)S(1)}, u32[]{:S(2)}, u32[]{:S(2)}) %collective-permute-start.10) | collective-permute-done | bytes 53280 | tf_op jit(solution)/shard_map/ppermute | solution.py:388
  34.1 0.8 %collective-permute-done.9 = f32[104,128]{1,0:T(8,128)S(1)} collective-permute-done((f32[104,128]{1,0:T(8,128)S(1)}, f32[104,128]{1,0:T(8,128)S(1)}, u32[]{:S(2)}, u32[]{:S(2)}) %collective-permute-start.9) | collective-permute-done | bytes 53280 | tf_op jit(solution)/shard_map/ppermute | solution.py:388
  34.9 0.0 collective-permute-done.8
  35.0 2.4 %collective-permute-start.13 = (f32[104,128]{1,0:T(8,128)S(1)}, f32[104,128]{1,0:T(8,128)S(1)}, u32[]{:S(2)}, u32[]{:S(2)}) collective-permute-start(f32[104,128]{1,0:T(8,128)S(1)} %add_add_fusion.own_ref), channel_id=1, source_target_pairs={{0,65},{1,64},{32,97},{33,96},{64,1},{65,0},{96,33},{97,32},{2,67}... | collective-permute-start | bytes 159752 | tf_op jit(solution)/shard_map/ppermute | solution.py:388
  37.3 0.9 %collective-permute-start.12 = (f32[104,128]{1,0:T(8,128)S(1)}, f32[104,128]{1,0:T(8,128)S(1)}, u32[]{:S(2)}, u32[]{:S(2)}) collective-permute-start(f32[104,128]{1,0:T(8,128)S(1)} %add_add_fusion.own_ref), channel_id=1, source_target_pairs={{0,97},{1,96},{32,65},{33,64},{64,33},{65,32},{96,1},{97,0},{2,99}... | collective-permute-start | bytes 159752 | tf_op jit(solution)/shard_map/ppermute | solution.py:388
  38.2 0.1 collective-permute-start.11
  38.2 2.1 %collective-permute-done.13.two_ref = f32[104,128]{1,0:T(8,128)S(1)} collective-permute-done((f32[104,128]{1,0:T(8,128)S(1)}, f32[104,128]{1,0:T(8,128)S(1)}, u32[]{:S(2)}, u32[]{:S(2)}) %collective-permute-start.13) | collective-permute-done | bytes 53280 | tf_op jit(solution)/shard_map/ppermute | solution.py:388
  40.4 1.7 %collective-permute-done.12.three_ref = f32[104,128]{1,0:T(8,128)S(1)} collective-permute-done((f32[104,128]{1,0:T(8,128)S(1)}, f32[104,128]{1,0:T(8,128)S(1)}, u32[]{:S(2)}, u32[]{:S(2)}) %collective-permute-start.12) | collective-permute-done | bytes 53280 | tf_op jit(solution)/shard_map/ppermute | solution.py:388
  42.1 0.0 collective-permute-done.11.one_ref
  42.1 3.6 %solve.1 = (f32[97,97]{1,0:T(8,128)}, f32[1,96]{1,0:T(1,128)}) custom-call(f32[104,128]{1,0:T(8,128)S(1)} %collective-permute-done.11.one_ref, f32[104,128]{1,0:T(8,128)S(1)} %collective-permute-done.12.three_ref, f32[104,128]{1,0:T(8,128)S(1)} %collective-permute-done.13.two_ref, f32[104,128]{1,0:T(8,128)S(1)} %add_add_fusion.own_ref), custom_call_target="tpu_custom_call" | custom-call | tf_op jit(solution)/shard_map/solve/pallas_call | solution.py:370
  (6 shorter events, 0.1 us)
Async XLA Ops:
  2.6 8.4 %collective-permute-start = (bf16[240,128]{1,0:T(8,128)(2,1)S(1)}, bf16[240,128]{1,0:T(8,128)(2,1)S(1)}, u32[]{:S(2)}, u32[]{:S(2)}) collective-permute-start(bf16[240,128]{1,0:T(8,128)(2,1)S(1)} %get-tuple-element.32), channel_id=1, source_target_pairs={{0,8},{8,0},{16,24},{24,16},{32,40},{40,32},{48,56},{56,48},{64,72... | collective-permute-start | bytes 184328 | tf_op jit(solution)/shard_map/ppermute | solution.py:383
  4.8 6.4 %collective-permute-start.1 = (bf16[240,128]{1,0:T(8,128)(2,1)S(1)}, bf16[240,128]{1,0:T(8,128)(2,1)S(1)}, u32[]{:S(2)}, u32[]{:S(2)}) collective-permute-start(bf16[240,128]{1,0:T(8,128)(2,1)S(1)} %get-tuple-element.33), channel_id=1, source_target_pairs={{0,120},{8,16},{16,8},{24,32},{32,24},{40,48},{48,40},{56,64},{64,... | collective-permute-start | bytes 184328 | tf_op jit(solution)/shard_map/ppermute | solution.py:393
  11.2 6.8 %collective-permute-start.3 = (bf16[240,128]{1,0:T(8,128)(2,1)S(1)}, bf16[240,128]{1,0:T(8,128)(2,1)S(1)}, u32[]{:S(2)}, u32[]{:S(2)}) collective-permute-start(bf16[240,128]{1,0:T(8,128)(2,1)S(1)} %get-tuple-element.43), channel_id=1, source_target_pairs={{0,7},{1,2},{2,1},{3,4},{4,3},{5,6},{6,5},{7,0},{8,15},{9,10},{10,... | collective-permute-start | bytes 184328 | tf_op jit(solution)/shard_map/ppermute | solution.py:393
  14.9 3.1 %collective-permute-start.2 = (bf16[240,128]{1,0:T(8,128)(2,1)S(1)}, bf16[240,128]{1,0:T(8,128)(2,1)S(1)}, u32[]{:S(2)}, u32[]{:S(2)}) collective-permute-start(bf16[240,128]{1,0:T(8,128)(2,1)S(1)} %get-tuple-element.44), channel_id=1, source_target_pairs={{0,1},{1,0},{2,3},{3,2},{4,5},{5,4},{6,7},{7,6},{8,9},{9,8},{10,11... | collective-permute-start | bytes 184328 | tf_op jit(solution)/shard_map/ppermute | solution.py:383
  19.4 1.2 %collective-permute-start.4 = (f32[104,128]{1,0:T(8,128)S(1)}, f32[104,128]{1,0:T(8,128)S(1)}, u32[]{:S(2)}, u32[]{:S(2)}) collective-permute-start(f32[104,128]{1,0:T(8,128)S(1)} %get-tuple-element.40), channel_id=1, source_target_pairs={{0,1},{1,0},{2,3},{3,2},{4,5},{5,4},{6,7},{7,6},{8,9},{9,8},{10,11... | collective-permute-start | bytes 159752 | tf_op jit(solution)/shard_map/ppermute | solution.py:383
  20.7 5.3 %collective-permute-start.7 = (f32[104,128]{1,0:T(8,128)S(1)}, f32[104,128]{1,0:T(8,128)S(1)}, u32[]{:S(2)}, u32[]{:S(2)}) collective-permute-start(f32[104,128]{1,0:T(8,128)S(1)} %add.36), channel_id=1, source_target_pairs={{0,5},{1,4},{2,7},{3,6},{4,1},{5,0},{6,3},{7,2},{8,13},{9,12},{10,... | collective-permute-start | bytes 159752 | tf_op jit(solution)/shard_map/ppermute | solution.py:388
  23.9 4.8 %collective-permute-start.6 = (f32[104,128]{1,0:T(8,128)S(1)}, f32[104,128]{1,0:T(8,128)S(1)}, u32[]{:S(2)}, u32[]{:S(2)}) collective-permute-start(f32[104,128]{1,0:T(8,128)S(1)} %add.36), channel_id=1, source_target_pairs={{0,7},{1,6},{2,5},{3,4},{4,3},{5,2},{6,1},{7,0},{8,15},{9,14},{10,... | collective-permute-start | bytes 159752 | tf_op jit(solution)/shard_map/ppermute | solution.py:388
  24.7 4.1 %collective-permute-start.5 = (f32[104,128]{1,0:T(8,128)S(1)}, f32[104,128]{1,0:T(8,128)S(1)}, u32[]{:S(2)}, u32[]{:S(2)}) collective-permute-start(f32[104,128]{1,0:T(8,128)S(1)} %add.36), channel_id=1, source_target_pairs={{0,3},{1,2},{2,1},{3,0},{4,7},{5,6},{6,5},{7,4},{8,11},{9,10},{10,... | collective-permute-start | bytes 159752 | tf_op jit(solution)/shard_map/ppermute | solution.py:388
  28.7 5.4 %collective-permute-start.10 = (f32[104,128]{1,0:T(8,128)S(1)}, f32[104,128]{1,0:T(8,128)S(1)}, u32[]{:S(2)}, u32[]{:S(2)}) collective-permute-start(f32[104,128]{1,0:T(8,128)S(1)} %add_add_fusion.1), channel_id=1, source_target_pairs={{0,17},{1,16},{8,25},{9,24},{16,1},{17,0},{24,9},{25,8},{2,19},{3,... | collective-permute-start | bytes 159752 | tf_op jit(solution)/shard_map/ppermute | solution.py:388
  28.8 6.1 %collective-permute-start.9 = (f32[104,128]{1,0:T(8,128)S(1)}, f32[104,128]{1,0:T(8,128)S(1)}, u32[]{:S(2)}, u32[]{:S(2)}) collective-permute-start(f32[104,128]{1,0:T(8,128)S(1)} %add_add_fusion.1), channel_id=1, source_target_pairs={{0,25},{1,24},{8,17},{9,16},{16,9},{17,8},{24,1},{25,0},{2,27},{3,... | collective-permute-start | bytes 159752 | tf_op jit(solution)/shard_map/ppermute | solution.py:388
  29.7 5.2 %collective-permute-start.8 = (f32[104,128]{1,0:T(8,128)S(1)}, f32[104,128]{1,0:T(8,128)S(1)}, u32[]{:S(2)}, u32[]{:S(2)}) collective-permute-start(f32[104,128]{1,0:T(8,128)S(1)} %add_add_fusion.1), channel_id=1, source_target_pairs={{0,9},{1,8},{8,1},{9,0},{16,25},{17,24},{24,17},{25,16},{2,11},{3,... | collective-permute-start | bytes 159752 | tf_op jit(solution)/shard_map/ppermute | solution.py:388
  35.0 5.4 %collective-permute-start.13 = (f32[104,128]{1,0:T(8,128)S(1)}, f32[104,128]{1,0:T(8,128)S(1)}, u32[]{:S(2)}, u32[]{:S(2)}) collective-permute-start(f32[104,128]{1,0:T(8,128)S(1)} %add_add_fusion.own_ref), channel_id=1, source_target_pairs={{0,65},{1,64},{32,97},{33,96},{64,1},{65,0},{96,33},{97,32},{2,67}... | collective-permute-start | bytes 159752 | tf_op jit(solution)/shard_map/ppermute | solution.py:388
  37.3 4.8 %collective-permute-start.12 = (f32[104,128]{1,0:T(8,128)S(1)}, f32[104,128]{1,0:T(8,128)S(1)}, u32[]{:S(2)}, u32[]{:S(2)}) collective-permute-start(f32[104,128]{1,0:T(8,128)S(1)} %add_add_fusion.own_ref), channel_id=1, source_target_pairs={{0,97},{1,96},{32,65},{33,64},{64,33},{65,32},{96,1},{97,0},{2,99}... | collective-permute-start | bytes 159752 | tf_op jit(solution)/shard_map/ppermute | solution.py:388
  38.2 3.9 %collective-permute-start.11 = (f32[104,128]{1,0:T(8,128)S(1)}, f32[104,128]{1,0:T(8,128)S(1)}, u32[]{:S(2)}, u32[]{:S(2)}) collective-permute-start(f32[104,128]{1,0:T(8,128)S(1)} %add_add_fusion.own_ref), channel_id=1, source_target_pairs={{0,33},{1,32},{32,1},{33,0},{64,97},{65,96},{96,65},{97,64},{2,35}... | collective-permute-start | bytes 159752 | tf_op jit(solution)/shard_map/ppermute | solution.py:388

commit v6 on v5

--- a/solution.py
+++ b/solution.py
@@ -266,7 +266,39 @@
     )(nu, basis, diag, pair, jacobian, flags, image)
 
 
-ROWS = 112
+ROWS = 128
+PACK = 56
+MID = K // 2
+
+
+def grids(rows, first=0):
+    row = lax.broadcasted_iota(jnp.int32, (rows, 128), 0) + first
+    return row, lax.broadcasted_iota(jnp.int32, (rows, 128), 1)
+
+
+def pack_gram(gram):
+    row, lane = grids(MID)
+    lower = pltpu.roll(gram[MID:K], 128 - MID, 1)
+    upper = jnp.where((lane < MID) & (lane < row), lower, gram[:MID])
+    row, lane = grids(MID, MID)
+    diagonal = jnp.sum(jnp.where(row == lane, gram[MID:K], 0.0), axis=0, keepdims=True)
+    row, lane = grids(8)
+    tail = jnp.where(row == 0, gram[K : K + 1], jnp.where(row == 1, diagonal, 0.0))
+    return jnp.concatenate([upper, tail], axis=0)
+
+
+def unpack_gram(packed, work):
+    flipped = packed.T
+    row, lane = grids(MID)
+    first = packed[:MID]
+    turned = jnp.concatenate([flipped, jnp.zeros((128, 128 - PACK), F32)], axis=1)
+    work[:MID] = jnp.where((lane < MID) & (lane < row), turned[:MID], first)
+    half = jnp.where(lane < row, first, turned[:MID])
+    half = pltpu.roll(jnp.where(lane < MID, half, turned[MID:K]), MID, 1)
+    half = jnp.where(lane < MID, turned[MID:K], half)
+    work[MID:K] = jnp.where(lane == row + MID, packed[MID + 1 : MID + 2], half)
+    row, lane = grids(8)
+    work[K : K + 8] = jnp.where(row == 0, packed[MID : MID + 1], 0.0)
 
 
 def finish_kernel(row_scale, image_ref, row_a, row_b, col_a, col_b, hot_ref, coef_ref, base_ref,
@@ -279,7 +311,7 @@
         arrive[HALF:, here] = jnp.where(low, pltpu.roll(one, 64, 1), two).astype(BF)
     test = (image_ref[:FK] + dot_nt(arrive[...], hot_ref[...])).astype(BF)
     coef = coef_ref[...]
-    first_row = lax.broadcasted_iota(jnp.int32, (16, C), 0) == 0
+    first_row = lax.broadcasted_iota(jnp.int32, (ROWS - K, C), 0) == 0
     for f in range(F):
         part = test[f * K : (f + 1) * K]
         here = slice(f * C, (f + 1) * C)
@@ -290,13 +322,13 @@
         stack[K:ROWS, here] = jnp.where(first_row, value, 0.0).astype(BF)
     whole = stack[...]
     gram = dot_nt(whole, whole) * (row_scale * row_scale)
-    gram_ref[...] = jnp.concatenate([gram[:104], jnp.zeros((104, 128 - ROWS), F32)], axis=1)
+    gram_ref[...] = pack_gram(gram)
 
 
 def finish_call(row_scale, image, row_a, row_b, col_a, col_b, hot, coef, base):
     return pl.pallas_call(
         functools.partial(finish_kernel, row_scale),
-        out_shape=(jax.ShapeDtypeStruct((F, K, C), BF), jax.ShapeDtypeStruct((104, 128), F32)),
+        out_shape=(jax.ShapeDtypeStruct((F, K, C), BF), jax.ShapeDtypeStruct((PACK, 128), F32)),
         in_specs=vmem(8),
         out_specs=tuple(vmem(2)),
         scratch_shapes=[pltpu.VMEM((FK, 256), BF), pltpu.VMEM((ROWS, F * C), BF)],
@@ -309,7 +341,7 @@
 
 
 def solve_kernel(row_scale, one_ref, three_ref, two_ref, own_ref, factor_ref, step_ref, work):
-    work[...] = (one_ref[...] + three_ref[...]) + (two_ref[...] + own_ref[...])
+    unpack_gram((one_ref[...] + three_ref[...]) + (two_ref[...] + own_ref[...]), work)
     lane = lax.broadcasted_iota(jnp.int32, (8, 128), 1)
     sub = lax.broadcasted_iota(jnp.int32, (8, 128), 0)
 

time: 45.9 us -> 44 us (0.959)
  waiting for transfers between devices: 12.2 us -> 10 us
    ppermute x9, waiting for transfers between devices: 11 us -> 8.89 us  [cross(): return lax.ppermute(x, (axis, 'col_1'), pairs)]
where the time goes in v6:
time: 44 us; the launch traced here: 43.9 us
  starting transfers between devices  21.6 us (49%)
  Pallas kernels  11.5 us (26%)
  waiting for transfers between devices  10 us (23%)
  between operations  0.72 us (2%)
    ppermute x9, starting transfers between devices, cross(): return lax.ppermute(x, (axis, 'col_1'), pairs)  10.8 us
    ppermute x9, waiting for transfers between devices, cross(): return lax.ppermute(x, (axis, 'col_1'), pairs)  8.89 us
    ppermute x2, starting transfers between devices, swap_odd(): lax.ppermute(x, axis, [(i, (i + 1) % count if i % 2 else (i - 1) % count)...  7.79 us
    pallas_call x1, Pallas kernels, solve_call(): pl.pallas_call(functools.partial(solve_kernel, row_scale), out_shape=(jax...  3.77 us
    ppermute x3, starting transfers between devices, swap(): return lax.ppermute(x, axis, [(i, i ^ step) for i in range(count)])  3.01 us
    pallas_call x1, Pallas kernels, late_call(): pl.pallas_call(late_kernel, out_shape=jax.ShapeDtypeStruct((WIDE, C), F32...  2.51 us
    pallas_call x1, Pallas kernels, early_call(): pl.pallas_call(early_kernel, out_shape=(jax.ShapeDtypeStruct((WIDE, C), F...  2.09 us
    pallas_call x1, Pallas kernels, ghost_call(): pl.pallas_call(ghost_kernel, out_shape=(message,) * 4 + tuple((jax.ShapeD...  1.92 us
  transfers between devices with their start and end apart: 14, of which 8 were waited for; matrix products, arithmetic and copies ran while one was open for 0% of the time, Pallas kernels for 10%

profile of v6, /device:TPU:1, one launch (start us, length us, event | category | flops | bytes accessed | tf_op | source)
XLA Modules:
  0.0 43.9 jit_solution(9600592351416984152)
XLA Ops:
  0.6 1.9 %ghost.1 = (bf16[240,128]{1,0:T(8,128)(2,1)S(1)}, bf16[240,128]{1,0:T(8,128)(2,1)S(1)}, bf16[240,128]{1,0:T(8,128)(2,1)S(1)}, bf16[240,128]{1,0:T(8,128)(2,1)S(1...) custom-call(s32[1,8]{1,0:T(1,128)} %bitcast.14, ...), custom_call_target="tpu_custom_call" | custom-call | tf_op jit(solution)/shard_map/ghost/pallas_call | solution.py:145
  2.6 2.2 %collective-permute-start = (bf16[240,128]{1,0:T(8,128)(2,1)S(1)}, bf16[240,128]{1,0:T(8,128)(2,1)S(1)}, u32[]{:S(2)}, u32[]{:S(2)}) collective-permute-start(bf16[240,128]{1,0:T(8,128)(2,1)S(1)} %get-tuple-element.32), channel_id=1, source_target_pairs={{0,8},{8,0},{16,24},{24,16},{32,40},{40,32},{48,56},{56,48},{64,72... | collective-permute-start | bytes 184328 | tf_op jit(solution)/shard_map/ppermute | solution.py:415
  4.8 4.1 %collective-permute-start.1 = (bf16[240,128]{1,0:T(8,128)(2,1)S(1)}, bf16[240,128]{1,0:T(8,128)(2,1)S(1)}, u32[]{:S(2)}, u32[]{:S(2)}) collective-permute-start(bf16[240,128]{1,0:T(8,128)(2,1)S(1)} %get-tuple-element.33), channel_id=1, source_target_pairs={{0,120},{8,16},{16,8},{24,32},{32,24},{40,48},{48,40},{56,64},{64,... | collective-permute-start | bytes 184328 | tf_op jit(solution)/shard_map/ppermute | solution.py:425
  8.9 2.1 %early_faces.1 = (f32[496,512]{1,0:T(8,128)S(1)}, bf16[512,256]{1,0:T(8,128)(2,1)S(1)}, bf16[16,96]{1,0:T(8,128)(2,1)S(1)}) custom-call(f32[1,5]{1,0:T(1,128)S(1)} %get-tuple-element.23.nu_ref, bf16[480,512]{1,0:T(8,128)(2,1)S(1)} %get-tuple-element.24.basis_ref, s32[2,1024]{1,0:T(2,128)S(1)} %get-tuple-element.26.pair_ref, ...), custom_call_target="tpu_custom_call" | custom-call | flops 2500000000 | bytes 2000000 | tf_op jit(solution)/shard_map/early_faces/pallas_call | solution.py:240
  11.0 0.0 collective-permute-done.row_a
  11.0 0.2 collective-permute-done.1.row_b
  11.2 3.7 %collective-permute-start.3 = (bf16[240,128]{1,0:T(8,128)(2,1)S(1)}, bf16[240,128]{1,0:T(8,128)(2,1)S(1)}, u32[]{:S(2)}, u32[]{:S(2)}) collective-permute-start(bf16[240,128]{1,0:T(8,128)(2,1)S(1)} %get-tuple-element.43), channel_id=1, source_target_pairs={{0,7},{1,2},{2,1},{3,4},{4,3},{5,6},{6,5},{7,0},{8,15},{9,10},{10,... | collective-permute-start | bytes 184328 | tf_op jit(solution)/shard_map/ppermute | solution.py:425
  14.9 0.5 %collective-permute-start.2 = (bf16[240,128]{1,0:T(8,128)(2,1)S(1)}, bf16[240,128]{1,0:T(8,128)(2,1)S(1)}, u32[]{:S(2)}, u32[]{:S(2)}) collective-permute-start(bf16[240,128]{1,0:T(8,128)(2,1)S(1)} %get-tuple-element.44), channel_id=1, source_target_pairs={{0,1},{1,0},{2,3},{3,2},{4,5},{5,4},{6,7},{7,6},{8,9},{9,8},{10,11... | collective-permute-start | bytes 184328 | tf_op jit(solution)/shard_map/ppermute | solution.py:415
  15.4 2.5 %late_faces.1.image_ref = f32[496,512]{1,0:T(8,128)S(1)} custom-call(f32[1,5]{1,0:T(1,128)S(1)} %get-tuple-element.23.nu_ref, bf16[480,512]{1,0:T(8,128)(2,1)S(1)} %get-tuple-element.24.basis_ref, f32[5,5,512]{2,1,0:T(8,128)S(1)} %get-tuple-element.25.diag_ref, s32[2,1024]{1,0:T(2,128)S(1)} %get-tuple-element.26.pair_ref, ...), custom_call_target="tpu_custom_call" | custom-call | flops 2500000000 | bytes 2000000 | tf_op jit(solution)/shard_map/late_faces/pallas_call | solution.py:257
  18.0 0.0 collective-permute-done.3.col_b
  18.0 0.0 collective-permute-done.2.col_a
  18.0 1.2 %finish.1 = (bf16[5,96,512]{2,1,0:T(8,128)(2,1)}, f32[56,128]{1,0:T(8,128)S(1)}) custom-call(f32[496,512]{1,0:T(8,128)S(1)} %late_faces.1.image_ref, bf16[240,128]{1,0:T(8,128)(2,1)S(1)} %collective-permute-done.row_a, bf16[240,128]{1,0:T(8,128)(2,1)S(1)} %collective-permute-done.1.row_b, bf16[240,128]{1,0:T(8,128)(2,1)S(1)} %collective-permute-done.2.col_a, ...), custom_call_target="tpu_custom_call" | custom-call | tf_op jit(solution)/shard_map/finish/pallas_call | solution.py:329
  19.2 0.3 collective-permute-start.4
  19.5 0.9 %collective-permute-done.4 = f32[56,128]{1,0:T(8,128)S(1)} collective-permute-done((f32[56,128]{1,0:T(8,128)S(1)}, f32[56,128]{1,0:T(8,128)S(1)}, u32[]{:S(2)}, u32[]{:S(2)}) %collective-permute-start.4) | collective-permute-done | bytes 28704 | tf_op jit(solution)/shard_map/ppermute | solution.py:415
  20.4 3.2 %collective-permute-start.7 = (f32[56,128]{1,0:T(8,128)S(1)}, f32[56,128]{1,0:T(8,128)S(1)}, u32[]{:S(2)}, u32[]{:S(2)}) collective-permute-start(f32[56,128]{1,0:T(8,128)S(1)} %add.36), channel_id=1, source_target_pairs={{0,5},{1,4},{2,7},{3,6},{4,1},{5,0},{6,3},{7,2},{8,13},{9,12},{10,... | collective-permute-start | bytes 86024 | tf_op jit(solution)/shard_map/ppermute | solution.py:420
  23.6 0.8 %collective-permute-start.6 = (f32[56,128]{1,0:T(8,128)S(1)}, f32[56,128]{1,0:T(8,128)S(1)}, u32[]{:S(2)}, u32[]{:S(2)}) collective-permute-start(f32[56,128]{1,0:T(8,128)S(1)} %add.36), channel_id=1, source_target_pairs={{0,7},{1,6},{2,5},{3,4},{4,3},{5,2},{6,1},{7,0},{8,15},{9,14},{10,... | collective-permute-start | bytes 86024 | tf_op jit(solution)/shard_map/ppermute | solution.py:420
  24.4 0.0 collective-permute-start.5
  24.4 0.8 %collective-permute-done.7 = f32[56,128]{1,0:T(8,128)S(1)} collective-permute-done((f32[56,128]{1,0:T(8,128)S(1)}, f32[56,128]{1,0:T(8,128)S(1)}, u32[]{:S(2)}, u32[]{:S(2)}) %collective-permute-start.7) | collective-permute-done | bytes 28704 | tf_op jit(solution)/shard_map/ppermute | solution.py:420
  25.2 2.9 %collective-permute-done.6 = f32[56,128]{1,0:T(8,128)S(1)} collective-permute-done((f32[56,128]{1,0:T(8,128)S(1)}, f32[56,128]{1,0:T(8,128)S(1)}, u32[]{:S(2)}, u32[]{:S(2)}) %collective-permute-start.6) | collective-permute-done | bytes 28704 | tf_op jit(solution)/shard_map/ppermute | solution.py:420
  28.1 0.0 collective-permute-done.5
  28.1 0.1 collective-permute-start.10
  28.2 0.8 %collective-permute-start.9 = (f32[56,128]{1,0:T(8,128)S(1)}, f32[56,128]{1,0:T(8,128)S(1)}, u32[]{:S(2)}, u32[]{:S(2)}) collective-permute-start(f32[56,128]{1,0:T(8,128)S(1)} %add_add_fusion.1), channel_id=1, source_target_pairs={{0,25},{1,24},{8,17},{9,16},{16,9},{17,8},{24,1},{25,0},{2,27},{3,... | collective-permute-start | bytes 86024 | tf_op jit(solution)/shard_map/ppermute | solution.py:420
  29.1 2.1 %collective-permute-start.8 = (f32[56,128]{1,0:T(8,128)S(1)}, f32[56,128]{1,0:T(8,128)S(1)}, u32[]{:S(2)}, u32[]{:S(2)}) collective-permute-start(f32[56,128]{1,0:T(8,128)S(1)} %add_add_fusion.1), channel_id=1, source_target_pairs={{0,9},{1,8},{8,1},{9,0},{16,25},{17,24},{24,17},{25,16},{2,11},{3,... | collective-permute-start | bytes 86024 | tf_op jit(solution)/shard_map/ppermute | solution.py:420
  31.2 1.9 %collective-permute-done.10 = f32[56,128]{1,0:T(8,128)S(1)} collective-permute-done((f32[56,128]{1,0:T(8,128)S(1)}, f32[56,128]{1,0:T(8,128)S(1)}, u32[]{:S(2)}, u32[]{:S(2)}) %collective-permute-start.10) | collective-permute-done | bytes 28704 | tf_op jit(solution)/shard_map/ppermute | solution.py:420
  33.0 0.2 collective-permute-done.9
  33.2 0.0 collective-permute-done.8
  33.2 2.4 %collective-permute-start.13 = (f32[56,128]{1,0:T(8,128)S(1)}, f32[56,128]{1,0:T(8,128)S(1)}, u32[]{:S(2)}, u32[]{:S(2)}) collective-permute-start(f32[56,128]{1,0:T(8,128)S(1)} %add_add_fusion.own_ref), channel_id=1, source_target_pairs={{0,65},{1,64},{32,97},{33,96},{64,1},{65,0},{96,33},{97,32},{2,67}... | collective-permute-start | bytes 86024 | tf_op jit(solution)/shard_map/ppermute | solution.py:420
  35.6 0.9 %collective-permute-start.12 = (f32[56,128]{1,0:T(8,128)S(1)}, f32[56,128]{1,0:T(8,128)S(1)}, u32[]{:S(2)}, u32[]{:S(2)}) collective-permute-start(f32[56,128]{1,0:T(8,128)S(1)} %add_add_fusion.own_ref), channel_id=1, source_target_pairs={{0,97},{1,96},{32,65},{33,64},{64,33},{65,32},{96,1},{97,0},{2,99}... | collective-permute-start | bytes 86024 | tf_op jit(solution)/shard_map/ppermute | solution.py:420
  36.5 0.5 %collective-permute-start.11 = (f32[56,128]{1,0:T(8,128)S(1)}, f32[56,128]{1,0:T(8,128)S(1)}, u32[]{:S(2)}, u32[]{:S(2)}) collective-permute-start(f32[56,128]{1,0:T(8,128)S(1)} %add_add_fusion.own_ref), channel_id=1, source_target_pairs={{0,33},{1,32},{32,1},{33,0},{64,97},{65,96},{96,65},{97,64},{2,35}... | collective-permute-start | bytes 86024 | tf_op jit(solution)/shard_map/ppermute | solution.py:420
  37.0 1.1 %collective-permute-done.13.two_ref = f32[56,128]{1,0:T(8,128)S(1)} collective-permute-done((f32[56,128]{1,0:T(8,128)S(1)}, f32[56,128]{1,0:T(8,128)S(1)}, u32[]{:S(2)}, u32[]{:S(2)}) %collective-permute-start.13) | collective-permute-done | bytes 28704 | tf_op jit(solution)/shard_map/ppermute | solution.py:420
  38.1 2.0 %collective-permute-done.12.three_ref = f32[56,128]{1,0:T(8,128)S(1)} collective-permute-done((f32[56,128]{1,0:T(8,128)S(1)}, f32[56,128]{1,0:T(8,128)S(1)}, u32[]{:S(2)}, u32[]{:S(2)}) %collective-permute-start.12) | collective-permute-done | bytes 28704 | tf_op jit(solution)/shard_map/ppermute | solution.py:420
  40.1 0.0 collective-permute-done.11.one_ref
  40.1 3.8 %solve.1 = (f32[97,97]{1,0:T(8,128)}, f32[1,96]{1,0:T(1,128)}) custom-call(f32[56,128]{1,0:T(8,128)S(1)} %collective-permute-done.11.one_ref, f32[56,128]{1,0:T(8,128)S(1)} %collective-permute-done.12.three_ref, f32[56,128]{1,0:T(8,128)S(1)} %collective-permute-done.13.two_ref, f32[56,128]{1,0:T(8,128)S(1)} %add_add_fusion.own_ref), custom_call_target="tpu_custom_call" | custom-call | tf_op jit(solution)/shard_map/solve/pallas_call | solution.py:402
  (6 shorter events, 0.1 us)
Async XLA Ops:
  2.6 8.4 %collective-permute-start = (bf16[240,128]{1,0:T(8,128)(2,1)S(1)}, bf16[240,128]{1,0:T(8,128)(2,1)S(1)}, u32[]{:S(2)}, u32[]{:S(2)}) collective-permute-start(bf16[240,128]{1,0:T(8,128)(2,1)S(1)} %get-tuple-element.32), channel_id=1, source_target_pairs={{0,8},{8,0},{16,24},{24,16},{32,40},{40,32},{48,56},{56,48},{64,72... | collective-permute-start | bytes 184328 | tf_op jit(solution)/shard_map/ppermute | solution.py:415
  4.8 6.4 %collective-permute-start.1 = (bf16[240,128]{1,0:T(8,128)(2,1)S(1)}, bf16[240,128]{1,0:T(8,128)(2,1)S(1)}, u32[]{:S(2)}, u32[]{:S(2)}) collective-permute-start(bf16[240,128]{1,0:T(8,128)(2,1)S(1)} %get-tuple-element.33), channel_id=1, source_target_pairs={{0,120},{8,16},{16,8},{24,32},{32,24},{40,48},{48,40},{56,64},{64,... | collective-permute-start | bytes 184328 | tf_op jit(solution)/shard_map/ppermute | solution.py:425
  11.2 6.8 %collective-permute-start.3 = (bf16[240,128]{1,0:T(8,128)(2,1)S(1)}, bf16[240,128]{1,0:T(8,128)(2,1)S(1)}, u32[]{:S(2)}, u32[]{:S(2)}) collective-permute-start(bf16[240,128]{1,0:T(8,128)(2,1)S(1)} %get-tuple-element.43), channel_id=1, source_target_pairs={{0,7},{1,2},{2,1},{3,4},{4,3},{5,6},{6,5},{7,0},{8,15},{9,10},{10,... | collective-permute-start | bytes 184328 | tf_op jit(solution)/shard_map/ppermute | solution.py:425
  14.9 3.1 %collective-permute-start.2 = (bf16[240,128]{1,0:T(8,128)(2,1)S(1)}, bf16[240,128]{1,0:T(8,128)(2,1)S(1)}, u32[]{:S(2)}, u32[]{:S(2)}) collective-permute-start(bf16[240,128]{1,0:T(8,128)(2,1)S(1)} %get-tuple-element.44), channel_id=1, source_target_pairs={{0,1},{1,0},{2,3},{3,2},{4,5},{5,4},{6,7},{7,6},{8,9},{9,8},{10,11... | collective-permute-start | bytes 184328 | tf_op jit(solution)/shard_map/ppermute | solution.py:415
  19.2 1.2 %collective-permute-start.4 = (f32[56,128]{1,0:T(8,128)S(1)}, f32[56,128]{1,0:T(8,128)S(1)}, u32[]{:S(2)}, u32[]{:S(2)}) collective-permute-start(f32[56,128]{1,0:T(8,128)S(1)} %get-tuple-element.40), channel_id=1, source_target_pairs={{0,1},{1,0},{2,3},{3,2},{4,5},{5,4},{6,7},{7,6},{8,9},{9,8},{10,11... | collective-permute-start | bytes 86024 | tf_op jit(solution)/shard_map/ppermute | solution.py:415
  20.4 4.8 %collective-permute-start.7 = (f32[56,128]{1,0:T(8,128)S(1)}, f32[56,128]{1,0:T(8,128)S(1)}, u32[]{:S(2)}, u32[]{:S(2)}) collective-permute-start(f32[56,128]{1,0:T(8,128)S(1)} %add.36), channel_id=1, source_target_pairs={{0,5},{1,4},{2,7},{3,6},{4,1},{5,0},{6,3},{7,2},{8,13},{9,12},{10,... | collective-permute-start | bytes 86024 | tf_op jit(solution)/shard_map/ppermute | solution.py:420
  23.6 4.5 %collective-permute-start.6 = (f32[56,128]{1,0:T(8,128)S(1)}, f32[56,128]{1,0:T(8,128)S(1)}, u32[]{:S(2)}, u32[]{:S(2)}) collective-permute-start(f32[56,128]{1,0:T(8,128)S(1)} %add.36), channel_id=1, source_target_pairs={{0,7},{1,6},{2,5},{3,4},{4,3},{5,2},{6,1},{7,0},{8,15},{9,14},{10,... | collective-permute-start | bytes 86024 | tf_op jit(solution)/shard_map/ppermute | solution.py:420
  24.4 3.7 %collective-permute-start.5 = (f32[56,128]{1,0:T(8,128)S(1)}, f32[56,128]{1,0:T(8,128)S(1)}, u32[]{:S(2)}, u32[]{:S(2)}) collective-permute-start(f32[56,128]{1,0:T(8,128)S(1)} %add.36), channel_id=1, source_target_pairs={{0,3},{1,2},{2,1},{3,0},{4,7},{5,6},{6,5},{7,4},{8,11},{9,10},{10,... | collective-permute-start | bytes 86024 | tf_op jit(solution)/shard_map/ppermute | solution.py:420
  28.1 4.9 %collective-permute-start.10 = (f32[56,128]{1,0:T(8,128)S(1)}, f32[56,128]{1,0:T(8,128)S(1)}, u32[]{:S(2)}, u32[]{:S(2)}) collective-permute-start(f32[56,128]{1,0:T(8,128)S(1)} %add_add_fusion.1), channel_id=1, source_target_pairs={{0,17},{1,16},{8,25},{9,24},{16,1},{17,0},{24,9},{25,8},{2,19},{3,... | collective-permute-start | bytes 86024 | tf_op jit(solution)/shard_map/ppermute | solution.py:420
  28.2 5.0 %collective-permute-start.9 = (f32[56,128]{1,0:T(8,128)S(1)}, f32[56,128]{1,0:T(8,128)S(1)}, u32[]{:S(2)}, u32[]{:S(2)}) collective-permute-start(f32[56,128]{1,0:T(8,128)S(1)} %add_add_fusion.1), channel_id=1, source_target_pairs={{0,25},{1,24},{8,17},{9,16},{16,9},{17,8},{24,1},{25,0},{2,27},{3,... | collective-permute-start | bytes 86024 | tf_op jit(solution)/shard_map/ppermute | solution.py:420
  29.1 4.2 %collective-permute-start.8 = (f32[56,128]{1,0:T(8,128)S(1)}, f32[56,128]{1,0:T(8,128)S(1)}, u32[]{:S(2)}, u32[]{:S(2)}) collective-permute-start(f32[56,128]{1,0:T(8,128)S(1)} %add_add_fusion.1), channel_id=1, source_target_pairs={{0,9},{1,8},{8,1},{9,0},{16,25},{17,24},{24,17},{25,16},{2,11},{3,... | collective-permute-start | bytes 86024 | tf_op jit(solution)/shard_map/ppermute | solution.py:420
  33.2 4.9 %collective-permute-start.13 = (f32[56,128]{1,0:T(8,128)S(1)}, f32[56,128]{1,0:T(8,128)S(1)}, u32[]{:S(2)}, u32[]{:S(2)}) collective-permute-start(f32[56,128]{1,0:T(8,128)S(1)} %add_add_fusion.own_ref), channel_id=1, source_target_pairs={{0,65},{1,64},{32,97},{33,96},{64,1},{65,0},{96,33},{97,32},{2,67}... | collective-permute-start | bytes 86024 | tf_op jit(solution)/shard_map/ppermute | solution.py:420
  35.6 4.5 %collective-permute-start.12 = (f32[56,128]{1,0:T(8,128)S(1)}, f32[56,128]{1,0:T(8,128)S(1)}, u32[]{:S(2)}, u32[]{:S(2)}) collective-permute-start(f32[56,128]{1,0:T(8,128)S(1)} %add_add_fusion.own_ref), channel_id=1, source_target_pairs={{0,97},{1,96},{32,65},{33,64},{64,33},{65,32},{96,1},{97,0},{2,99}... | collective-permute-start | bytes 86024 | tf_op jit(solution)/shard_map/ppermute | solution.py:420
  36.5 3.7 %collective-permute-start.11 = (f32[56,128]{1,0:T(8,128)S(1)}, f32[56,128]{1,0:T(8,128)S(1)}, u32[]{:S(2)}, u32[]{:S(2)}) collective-permute-start(f32[56,128]{1,0:T(8,128)S(1)} %add_add_fusion.own_ref), channel_id=1, source_target_pairs={{0,33},{1,32},{32,1},{33,0},{64,97},{65,96},{96,65},{97,64},{2,35}... | collective-permute-start | bytes 86024 | tf_op jit(solution)/shard_map/ppermute | solution.py:420

commit v7 on v6

--- a/solution.py
+++ b/solution.py
@@ -160,13 +160,14 @@
 
 
 BLOCK = 256
-HALF_BLOCKS = 2
+EARLY = 3
+LATE = 1
 CHUNK = 32
 WIDE = FK + 16
 
 
-def face_blocks(first_block, nu_ref, basis, pair_ref, jac_ref, flag_ref, hot, got, add, image):
-    for block in range(HALF_BLOCKS):
+def face_blocks(first_block, count, nu_ref, basis, pair_ref, jac_ref, flag_ref, hot, got, add, image):
+    for block in range(count):
         base = (first_block + block) * BLOCK
         lanes = slice(base, base + BLOCK)
         hot[block, :, :BLOCK] = one_hot(pair_ref[0:1, lanes])
@@ -193,12 +194,28 @@
                     rows = slice(g * K + start, g * K + start + CHUNK)
                     add[block, rows, at_a] = to_a.astype(BF)
                     add[block, rows, at_b] = to_b.astype(BF)
-    for block in range(HALF_BLOCKS):
+    for block in range(count):
         image = dot_nt(add[block], hot[block]) if image is None else image + dot_nt(add[block], hot[block])
     return image
 
 
-def early_kernel(nu_ref, basis_ref, pair_ref, jac_ref, flag_ref, cell_ref, coord_ref,
+def add_diagonal(image_ref, basis_ref, nu_ref, diag_ref):
+    for tile in range(C // 128):
+        here = slice(tile * 128, (tile + 1) * 128)
+        flagged = image_ref[FK : FK + 1, here]
+        own = [diag_ref[g, g : g + 1, here] + nu_ref[0:1, g : g + 1] * flagged for g in range(F)]
+        for start in range(0, K, CHUNK):
+            v = [basis_ref[f * K + start : f * K + start + CHUNK, here].astype(F32) for f in range(F)]
+            for g in range(F):
+                rows = slice(g * K + start, g * K + start + CHUNK)
+                total = image_ref[rows, here] + own[g] * v[g]
+                for f in range(F):
+                    if f != g:
+                        total = total + diag_ref[g, f : f + 1, here] * v[f]
+                image_ref[rows, here] = total
+
+
+def early_kernel(nu_ref, basis_ref, diag_ref, pair_ref, jac_ref, flag_ref, cell_ref, coord_ref,
                  image_ref, hot_ref, coef_ref, hot, got, add):
     odd_i, odd_j = parities()
     hot_ref[...] = one_hot(jnp.concatenate(receive_order(cell_ref[...], odd_i, odd_j), axis=-1))
@@ -206,37 +223,32 @@
     high = coord.astype(BF).astype(F32)
     row = lax.broadcasted_iota(jnp.int32, (16, K), 0)
     coef_ref[...] = jnp.where(row == 0, high, jnp.where(row == 1, coord - high, 0.0)).astype(BF)
-    image_ref[...] = face_blocks(0, nu_ref, basis_ref[...], pair_ref, jac_ref, flag_ref, hot, got, add, None)
-
-
-def late_kernel(nu_ref, basis_ref, diag_ref, pair_ref, jac_ref, flag_ref, image_ref, out_ref, hot, got, add):
-    out_ref[...] = face_blocks(
-        HALF_BLOCKS, nu_ref, basis_ref[...], pair_ref, jac_ref, flag_ref, hot, got, add, image_ref[...]
-    )
-    for tile in range(C // 128):
-        here = slice(tile * 128, (tile + 1) * 128)
-        flagged = out_ref[FK : FK + 1, here]
-        own = [diag_ref[g, g : g + 1, here] + nu_ref[0:1, g : g + 1] * flagged for g in range(F)]
-        for start in range(0, K, CHUNK):
-            v = [basis_ref[f * K + start : f * K + start + CHUNK, here].astype(F32) for f in range(F)]
-            for g in range(F):
-                rows = slice(g * K + start, g * K + start + CHUNK)
-                total = out_ref[rows, here] + own[g] * v[g]
-                for f in range(F):
-                    if f != g:
-                        total = total + diag_ref[g, f : f + 1, here] * v[f]
-                out_ref[rows, here] = total
-
-
-FACE_SCRATCH = (
-    ((HALF_BLOCKS, C, 2 * BLOCK), BF),
-    ((HALF_BLOCKS, FK, 2 * BLOCK), F32),
-    ((HALF_BLOCKS, WIDE, 2 * BLOCK), BF),
-)
-FACE_COST = pl.CostEstimate(flops=2_500_000_000, bytes_accessed=2_000_000, transcendentals=0)
-
-
-def early_call(nu, basis, pair, jacobian, flags, cells, coords):
+    image_ref[...] = face_blocks(0, EARLY, nu_ref, basis_ref[...], pair_ref, jac_ref, flag_ref, hot, got, add, None)
+    add_diagonal(image_ref, basis_ref, nu_ref, diag_ref)
+
+
+def late_kernel(nu_ref, basis_ref, pair_ref, jac_ref, flag_ref, image_ref, out_ref, hot, got, add):
+    image = face_blocks(EARLY, LATE, nu_ref, basis_ref[...], pair_ref, jac_ref, flag_ref, hot, got, add, None)
+    flagged = image[FK : FK + 1]
+    for g in range(F):
+        rows = slice(g * K, (g + 1) * K)
+        damp = (nu_ref[0:1, g : g + 1] * flagged) * basis_ref[rows].astype(F32)
+        out_ref[rows] = (image_ref[rows] + image[rows]) + damp
+
+
+def face_scratch(count):
+    return [
+        pltpu.VMEM((count, C, 2 * BLOCK), BF),
+        pltpu.VMEM((count, FK, 2 * BLOCK), F32),
+        pltpu.VMEM((count, WIDE, 2 * BLOCK), BF),
+    ]
+
+
+def face_cost(count):
+    return pl.CostEstimate(flops=count * 1_250_000_000, bytes_accessed=2_000_000, transcendentals=0)
+
+
+def early_call(nu, basis, diag, pair, jacobian, flags, cells, coords):
     return pl.pallas_call(
         early_kernel,
         out_shape=(
@@ -244,26 +256,26 @@
             jax.ShapeDtypeStruct((C, 256), BF),
             jax.ShapeDtypeStruct((16, K), BF),
         ),
-        in_specs=vmem(7),
+        in_specs=vmem(8),
         out_specs=tuple(vmem(3)),
-        scratch_shapes=[pltpu.VMEM(*scratch) for scratch in FACE_SCRATCH],
+        scratch_shapes=face_scratch(EARLY),
         compiler_params=pltpu.CompilerParams(vmem_limit_bytes=VMEM_LIMIT),
-        cost_estimate=FACE_COST,
+        cost_estimate=face_cost(EARLY),
         name="early_faces",
-    )(nu, basis, pair, jacobian, flags, cells, coords)
-
-
-def late_call(nu, basis, diag, pair, jacobian, flags, image):
+    )(nu, basis, diag, pair, jacobian, flags, cells, coords)
+
+
+def late_call(nu, basis, pair, jacobian, flags, image):
     return pl.pallas_call(
         late_kernel,
-        out_shape=jax.ShapeDtypeStruct((WIDE, C), F32),
-        in_specs=vmem(7),
+        out_shape=jax.ShapeDtypeStruct((FK, C), F32),
+        in_specs=vmem(6),
         out_specs=vmem(1)[0],
-        scratch_shapes=[pltpu.VMEM(*scratch) for scratch in FACE_SCRATCH],
+        scratch_shapes=face_scratch(LATE),
         compiler_params=pltpu.CompilerParams(vmem_limit_bytes=VMEM_LIMIT),
-        cost_estimate=FACE_COST,
+        cost_estimate=face_cost(LATE),
         name="late_faces",
-    )(nu, basis, diag, pair, jacobian, flags, image)
+    )(nu, basis, pair, jacobian, flags, image)
 
 
 ROWS = 128
@@ -309,7 +321,7 @@
         one, two = first[...].astype(F32), second[...].astype(F32)
         arrive[:HALF, here] = jnp.where(low, one, pltpu.roll(two, 64, 1)).astype(BF)
         arrive[HALF:, here] = jnp.where(low, pltpu.roll(one, 64, 1), two).astype(BF)
-    test = (image_ref[:FK] + dot_nt(arrive[...], hot_ref[...])).astype(BF)
+    test = (image_ref[...] + dot_nt(arrive[...], hot_ref[...])).astype(BF)
     coef = coef_ref[...]
     first_row = lax.broadcasted_iota(jnp.int32, (ROWS - K, C), 0) == 0
     for f in range(F):
@@ -340,7 +352,9 @@
 TILES = 13
 
 
-def solve_kernel(row_scale, one_ref, three_ref, two_ref, own_ref, factor_ref, step_ref, work):
+def solve_kernel(row_scale, one_ref, three_ref, two_ref, own_ref, test_ref, factor_ref, step_ref, out_hbm, work, sem):
+    copy = pltpu.make_async_copy(test_ref, out_hbm, sem.at[0])
+    copy.start()
     unpack_gram((one_ref[...] + three_ref[...]) + (two_ref[...] + own_ref[...]), work)
     lane = lax.broadcasted_iota(jnp.int32, (8, 128), 1)
     sub = lax.broadcasted_iota(jnp.int32, (8, 128), 0)
@@ -396,15 +410,20 @@
         column = spread_lane(tiles[t], 96)
         step = step + jnp.sum(jnp.where(lane == 8 * t + sub, column, 0.0), axis=0, keepdims=True)
     step_ref[...] = step[:, :96] * (-1.0 / row_scale)
+    copy.wait()
 
 
 def solve_call(row_scale, *terms):
     return pl.pallas_call(
         functools.partial(solve_kernel, row_scale),
-        out_shape=(jax.ShapeDtypeStruct((97, 97), F32), jax.ShapeDtypeStruct((1, 96), F32)),
-        in_specs=vmem(4),
-        out_specs=tuple(vmem(2)),
-        scratch_shapes=[pltpu.VMEM((104, 128), F32)],
+        out_shape=(
+            jax.ShapeDtypeStruct((97, 97), F32),
+            jax.ShapeDtypeStruct((1, 96), F32),
+            jax.ShapeDtypeStruct((F, K, C), BF),
+        ),
+        in_specs=vmem(5),
+        out_specs=tuple(vmem(2)) + (pl.BlockSpec(memory_space=pltpu.MemorySpace.HBM),),
+        scratch_shapes=[pltpu.VMEM((104, 128), F32), pltpu.SemaphoreType.DMA((1,))],
         compiler_params=pltpu.CompilerParams(vmem_limit_bytes=VMEM_LIMIT),
         name="solve",
     )(*terms)
@@ -452,7 +471,7 @@
     row_a = swap(row_a, ROW, 1)
     row_b = swap_odd(row_b, ROW)
     image, hot, coef = early_call(
-        nu, basis, pair, jacobian, flags, arrive, coords
+        nu, basis, diag, pair, jacobian, flags, arrive, coords
     )
     group = (lax.broadcasted_iota(jnp.int32, (HALF, 128), 1) % 64) // 8
     corner = row_a + row_b
@@ -460,14 +479,14 @@
     col_b = jnp.where((group == 5) | (group == 7), corner, col_b)
     col_a = swap(col_a, COL, 1)
     col_b = swap_odd(col_b, COL)
-    image = late_call(nu, basis, diag, pair, jacobian, flags, image)
+    image = late_call(nu, basis, pair, jacobian, flags, image)
     test, gram = finish_call(row_scale, image, row_a, row_b, col_a, col_b, hot, coef, base)
     gram = gram + swap(gram, "col_1", 1)
     for axis in ("col_0", "row_1", "row_0"):
         one, three, two = (cross(gram, axis, k) for k in (1, 3, 2))
         terms = (one, three, two, gram)
         gram = (one + three) + (two + gram)
-    factor, step = solve_call(row_scale, *terms)
+    factor, step, test = solve_call(row_scale, *terms, test)
     return (test, factor, step.reshape(K))
 
 

time: 44 us -> 43.4 us (0.986)
  waiting for transfers between devices: 10 us -> 9.38 us
    ppermute x3, starting transfers between devices: 3.01 us -> 4.26 us  [swap(): return lax.ppermute(x, axis, [(i, i ^ step) for i in range(count)])]
    pallas_call x1, Pallas kernels: 2.09 us -> 3.33 us  [early_call(): pl.pallas_call(early_kernel, out_shape=(jax.ShapeDtypeStruct((WIDE, C), F...]
    pallas_call x1, Pallas kernels: 2.51 us -> 1.34 us  [late_call(): pl.pallas_call(late_kernel, out_shape=jax.ShapeDtypeStruct((FK, C), F32),...]
    ppermute x2, starting transfers between devices: 7.79 us -> 6.93 us  [swap_odd(): lax.ppermute(x, axis, [(i, (i + 1) % count if i % 2 else (i - 1) % count)...]
    ppermute x9, starting transfers between devices: 10.8 us -> 10.3 us  [cross(): return lax.ppermute(x, (axis, 'col_1'), pairs)]
  transfers between devices with their start and end apart: 14 -> 14, of which waited for: 8 -> 7; matrix products, arithmetic and copies ran while one was open for 0% -> 0% of each run, Pallas kernels for 10% -> 11%
where the time goes in v7:
time: 43.4 us; the launch traced here: 43.2 us
  starting transfers between devices  21.5 us (50%)
  Pallas kernels  11.4 us (26%)
  waiting for transfers between devices  9.38 us (22%)
  between operations  0.89 us (2%)
    ppermute x9, starting transfers between devices, cross(): return lax.ppermute(x, (axis, 'col_1'), pairs)  10.3 us
    ppermute x9, waiting for transfers between devices, cross(): return lax.ppermute(x, (axis, 'col_1'), pairs)  8.52 us
    ppermute x2, starting transfers between devices, swap_odd(): lax.ppermute(x, axis, [(i, (i + 1) % count if i % 2 else (i - 1) % count)...  6.93 us
    ppermute x3, starting transfers between devices, swap(): return lax.ppermute(x, axis, [(i, i ^ step) for i in range(count)])  4.26 us
    pallas_call x1, Pallas kernels, solve_call(): pl.pallas_call(functools.partial(solve_kernel, row_scale), out_shape=(jax...  3.79 us
    pallas_call x1, Pallas kernels, early_call(): pl.pallas_call(early_kernel, out_shape=(jax.ShapeDtypeStruct((WIDE, C), F...  3.33 us
    pallas_call x1, Pallas kernels, ghost_call(): pl.pallas_call(ghost_kernel, out_shape=(message,) * 4 + tuple((jax.ShapeD...  1.93 us
    pallas_call x1, Pallas kernels, late_call(): pl.pallas_call(late_kernel, out_shape=jax.ShapeDtypeStruct((FK, C), F32),...  1.34 us
  transfers between devices with their start and end apart: 14, of which 7 were waited for; matrix products, arithmetic and copies ran while one was open for 0% of the time, Pallas kernels for 11%

profile of v7, /device:TPU:1, one launch (start us, length us, event | category | flops | bytes accessed | tf_op | source)
XLA Modules:
  0.0 43.2 jit_solution(12454418052714995285)
XLA Ops:
  0.6 1.9 %ghost.1 = (bf16[240,128]{1,0:T(8,128)(2,1)S(1)}, bf16[240,128]{1,0:T(8,128)(2,1)S(1)}, bf16[240,128]{1,0:T(8,128)(2,1)S(1)}, bf16[240,128]{1,0:T(8,128)(2,1)S(1...) custom-call(s32[1,8]{1,0:T(1,128)} %bitcast.14, ...), custom_call_target="tpu_custom_call" | custom-call | tf_op jit(solution)/shard_map/ghost/pallas_call | solution.py:145
  2.6 2.2 %collective-permute-start = (bf16[240,128]{1,0:T(8,128)(2,1)S(1)}, bf16[240,128]{1,0:T(8,128)(2,1)S(1)}, u32[]{:S(2)}, u32[]{:S(2)}) collective-permute-start(bf16[240,128]{1,0:T(8,128)(2,1)S(1)} %get-tuple-element.33), channel_id=1, source_target_pairs={{0,8},{8,0},{16,24},{24,16},{32,40},{40,32},{48,56},{56,48},{64,72... | collective-permute-start | bytes 184328 | tf_op jit(solution)/shard_map/ppermute | solution.py:434
  4.8 4.1 %collective-permute-start.1 = (bf16[240,128]{1,0:T(8,128)(2,1)S(1)}, bf16[240,128]{1,0:T(8,128)(2,1)S(1)}, u32[]{:S(2)}, u32[]{:S(2)}) collective-permute-start(bf16[240,128]{1,0:T(8,128)(2,1)S(1)} %get-tuple-element.34), channel_id=1, source_target_pairs={{0,120},{8,16},{16,8},{24,32},{32,24},{40,48},{48,40},{56,64},{64,... | collective-permute-start | bytes 184328 | tf_op jit(solution)/shard_map/ppermute | solution.py:444
  8.9 3.3 %early_faces.1 = (f32[496,512]{1,0:T(8,128)S(1)}, bf16[512,256]{1,0:T(8,128)(2,1)S(1)}, bf16[16,96]{1,0:T(8,128)(2,1)S(1)}) custom-call(f32[1,5]{1,0:T(1,128)S(1)} %get-tuple-element.24.nu_ref, bf16[480,512]{1,0:T(8,128)(2,1)S(1)} %get-tuple-element.25.basis_ref, f32[5,5,512]{2,1,0:T(8,128)S(1)} %get-tuple-element.29.diag_ref, ...), custom_call_target="tpu_custom_call" | custom-call | flops 3750000128 | bytes 2000000 | tf_op jit(solution)/shard_map/early_faces/pallas_call | solution.py:252
  12.2 0.0 collective-permute-done.row_a
  12.2 0.0 collective-permute-done.1.row_b
  12.3 2.8 %collective-permute-start.3 = (bf16[240,128]{1,0:T(8,128)(2,1)S(1)}, bf16[240,128]{1,0:T(8,128)(2,1)S(1)}, u32[]{:S(2)}, u32[]{:S(2)}) collective-permute-start(bf16[240,128]{1,0:T(8,128)(2,1)S(1)} %get-tuple-element.45), channel_id=1, source_target_pairs={{0,7},{1,2},{2,1},{3,4},{4,3},{5,6},{6,5},{7,0},{8,15},{9,10},{10,... | collective-permute-start | bytes 184328 | tf_op jit(solution)/shard_map/ppermute | solution.py:444
  15.1 1.4 %collective-permute-start.2 = (bf16[240,128]{1,0:T(8,128)(2,1)S(1)}, bf16[240,128]{1,0:T(8,128)(2,1)S(1)}, u32[]{:S(2)}, u32[]{:S(2)}) collective-permute-start(bf16[240,128]{1,0:T(8,128)(2,1)S(1)} %get-tuple-element.46), channel_id=1, source_target_pairs={{0,1},{1,0},{2,3},{3,2},{4,5},{5,4},{6,7},{7,6},{8,9},{9,8},{10,11... | collective-permute-start | bytes 184328 | tf_op jit(solution)/shard_map/ppermute | solution.py:434
  16.5 1.3 %late_faces.1.image_ref = f32[480,512]{1,0:T(8,128)S(1)} custom-call(f32[1,5]{1,0:T(1,128)S(1)} %get-tuple-element.24.nu_ref, bf16[480,512]{1,0:T(8,128)(2,1)S(1)} %get-tuple-element.25.basis_ref, s32[2,1024]{1,0:T(2,128)S(1)} %get-tuple-element.26.pair_ref, f32[5,5,2,1024]{3,2,1,0:T(2,128)S(1)} %get-tuple-element.27.jac_ref, ...), custom_call_target="tpu_custom_call" | custom-call | flops 1250000000 | bytes 2000000 | tf_op jit(solution)/shard_map/late_faces/pallas_call | solution.py:269
  17.9 0.0 collective-permute-done.3.col_b
  17.9 0.0 collective-permute-done.2.col_a
  17.9 1.0 %finish.1 = (bf16[5,96,512]{2,1,0:T(8,128)(2,1)S(1)}, f32[56,128]{1,0:T(8,128)S(1)}) custom-call(f32[480,512]{1,0:T(8,128)S(1)} %late_faces.1.image_ref, bf16[240,128]{1,0:T(8,128)(2,1)S(1)} %collective-permute-done.row_a, bf16[240,128]{1,0:T(8,128)(2,1)S(1)} %collective-permute-done.1.row_b, bf16[240,128]{1,0:T(8,128)(2,1)S(1)} %collective-permute-done.2.col_a, ...), custom_call_target="tpu_custom_call" | custom-call | tf_op jit(solution)/shard_map/finish/pallas_call | solution.py:341
  18.9 0.7 %collective-permute-start.4 = (f32[56,128]{1,0:T(8,128)S(1)}, f32[56,128]{1,0:T(8,128)S(1)}, u32[]{:S(2)}, u32[]{:S(2)}) collective-permute-start(f32[56,128]{1,0:T(8,128)S(1)} %get-tuple-element.40), channel_id=1, source_target_pairs={{0,1},{1,0},{2,3},{3,2},{4,5},{5,4},{6,7},{7,6},{8,9},{9,8},{10,11... | collective-permute-start | bytes 86024 | tf_op jit(solution)/shard_map/ppermute | solution.py:434
  19.6 0.9 %collective-permute-done.4 = f32[56,128]{1,0:T(8,128)S(1)} collective-permute-done((f32[56,128]{1,0:T(8,128)S(1)}, f32[56,128]{1,0:T(8,128)S(1)}, u32[]{:S(2)}, u32[]{:S(2)}) %collective-permute-start.4) | collective-permute-done | bytes 28704 | tf_op jit(solution)/shard_map/ppermute | solution.py:434
  20.4 2.6 %collective-permute-start.7 = (f32[56,128]{1,0:T(8,128)S(1)}, f32[56,128]{1,0:T(8,128)S(1)}, u32[]{:S(2)}, u32[]{:S(2)}) collective-permute-start(f32[56,128]{1,0:T(8,128)S(1)} %add.36), channel_id=1, source_target_pairs={{0,5},{1,4},{2,7},{3,6},{4,1},{5,0},{6,3},{7,2},{8,13},{9,12},{10,... | collective-permute-start | bytes 86024 | tf_op jit(solution)/shard_map/ppermute | solution.py:439
  23.0 0.6 %collective-permute-start.6 = (f32[56,128]{1,0:T(8,128)S(1)}, f32[56,128]{1,0:T(8,128)S(1)}, u32[]{:S(2)}, u32[]{:S(2)}) collective-permute-start(f32[56,128]{1,0:T(8,128)S(1)} %add.36), channel_id=1, source_target_pairs={{0,7},{1,6},{2,5},{3,4},{4,3},{5,2},{6,1},{7,0},{8,15},{9,14},{10,... | collective-permute-start | bytes 86024 | tf_op jit(solution)/shard_map/ppermute | solution.py:439
  23.6 0.5 %collective-permute-start.5 = (f32[56,128]{1,0:T(8,128)S(1)}, f32[56,128]{1,0:T(8,128)S(1)}, u32[]{:S(2)}, u32[]{:S(2)}) collective-permute-start(f32[56,128]{1,0:T(8,128)S(1)} %add.36), channel_id=1, source_target_pairs={{0,3},{1,2},{2,1},{3,0},{4,7},{5,6},{6,5},{7,4},{8,11},{9,10},{10,... | collective-permute-start | bytes 86024 | tf_op jit(solution)/shard_map/ppermute | solution.py:439
  24.1 1.1 %collective-permute-done.7 = f32[56,128]{1,0:T(8,128)S(1)} collective-permute-done((f32[56,128]{1,0:T(8,128)S(1)}, f32[56,128]{1,0:T(8,128)S(1)}, u32[]{:S(2)}, u32[]{:S(2)}) %collective-permute-start.7) | collective-permute-done | bytes 28704 | tf_op jit(solution)/shard_map/ppermute | solution.py:439
  25.2 2.3 %collective-permute-done.6 = f32[56,128]{1,0:T(8,128)S(1)} collective-permute-done((f32[56,128]{1,0:T(8,128)S(1)}, f32[56,128]{1,0:T(8,128)S(1)}, u32[]{:S(2)}, u32[]{:S(2)}) %collective-permute-start.6) | collective-permute-done | bytes 28704 | tf_op jit(solution)/shard_map/ppermute | solution.py:439
  27.5 0.0 collective-permute-done.5
  27.6 0.1 collective-permute-start.10
  27.6 0.9 %collective-permute-start.9 = (f32[56,128]{1,0:T(8,128)S(1)}, f32[56,128]{1,0:T(8,128)S(1)}, u32[]{:S(2)}, u32[]{:S(2)}) collective-permute-start(f32[56,128]{1,0:T(8,128)S(1)} %add_add_fusion.1), channel_id=1, source_target_pairs={{0,25},{1,24},{8,17},{9,16},{16,9},{17,8},{24,1},{25,0},{2,27},{3,... | collective-permute-start | bytes 86024 | tf_op jit(solution)/shard_map/ppermute | solution.py:439
  28.5 2.1 %collective-permute-start.8 = (f32[56,128]{1,0:T(8,128)S(1)}, f32[56,128]{1,0:T(8,128)S(1)}, u32[]{:S(2)}, u32[]{:S(2)}) collective-permute-start(f32[56,128]{1,0:T(8,128)S(1)} %add_add_fusion.1), channel_id=1, source_target_pairs={{0,9},{1,8},{8,1},{9,0},{16,25},{17,24},{24,17},{25,16},{2,11},{3,... | collective-permute-start | bytes 86024 | tf_op jit(solution)/shard_map/ppermute | solution.py:439
  30.6 1.9 %collective-permute-done.10 = f32[56,128]{1,0:T(8,128)S(1)} collective-permute-done((f32[56,128]{1,0:T(8,128)S(1)}, f32[56,128]{1,0:T(8,128)S(1)}, u32[]{:S(2)}, u32[]{:S(2)}) %collective-permute-start.10) | collective-permute-done | bytes 28704 | tf_op jit(solution)/shard_map/ppermute | solution.py:439
  32.5 0.2 collective-permute-done.9
  32.6 0.0 collective-permute-done.8
  32.6 2.1 %collective-permute-start.13 = (f32[56,128]{1,0:T(8,128)S(1)}, f32[56,128]{1,0:T(8,128)S(1)}, u32[]{:S(2)}, u32[]{:S(2)}) collective-permute-start(f32[56,128]{1,0:T(8,128)S(1)} %add_add_fusion.own_ref), channel_id=1, source_target_pairs={{0,65},{1,64},{32,97},{33,96},{64,1},{65,0},{96,33},{97,32},{2,67}... | collective-permute-start | bytes 86024 | tf_op jit(solution)/shard_map/ppermute | solution.py:439
  34.8 1.0 %collective-permute-start.12 = (f32[56,128]{1,0:T(8,128)S(1)}, f32[56,128]{1,0:T(8,128)S(1)}, u32[]{:S(2)}, u32[]{:S(2)}) collective-permute-start(f32[56,128]{1,0:T(8,128)S(1)} %add_add_fusion.own_ref), channel_id=1, source_target_pairs={{0,97},{1,96},{32,65},{33,64},{64,33},{65,32},{96,1},{97,0},{2,99}... | collective-permute-start | bytes 86024 | tf_op jit(solution)/shard_map/ppermute | solution.py:439
  35.8 0.4 collective-permute-start.11
  36.2 1.4 %collective-permute-done.13.two_ref = f32[56,128]{1,0:T(8,128)S(1)} collective-permute-done((f32[56,128]{1,0:T(8,128)S(1)}, f32[56,128]{1,0:T(8,128)S(1)}, u32[]{:S(2)}, u32[]{:S(2)}) %collective-permute-start.13) | collective-permute-done | bytes 28704 | tf_op jit(solution)/shard_map/ppermute | solution.py:439
  37.5 1.7 %collective-permute-done.12.three_ref = f32[56,128]{1,0:T(8,128)S(1)} collective-permute-done((f32[56,128]{1,0:T(8,128)S(1)}, f32[56,128]{1,0:T(8,128)S(1)}, u32[]{:S(2)}, u32[]{:S(2)}) %collective-permute-start.12) | collective-permute-done | bytes 28704 | tf_op jit(solution)/shard_map/ppermute | solution.py:439
  39.3 0.0 collective-permute-done.11.one_ref
  39.3 3.8 %solve.1 = (f32[97,97]{1,0:T(8,128)}, f32[1,96]{1,0:T(1,128)}, bf16[5,96,512]{2,1,0:T(8,128)(2,1)}) custom-call(f32[56,128]{1,0:T(8,128)S(1)} %collective-permute-done.11.one_ref, f32[56,128]{1,0:T(8,128)S(1)} %collective-permute-done.12.three_ref, f32[56,128]{1,0:T(8,128)S(1)} %collective-permute-done.13.two_ref, f32[56,128]{1,0:T(8,128)S(1)} %add_add_fusion.own_ref, ...), custom_call_target="tpu_custom_call" | custom-call | tf_op jit(solution)/shard_map/solve/pallas_call | solution.py:417
  (6 shorter events, 0.1 us)
Async XLA Ops:
  2.6 9.7 %collective-permute-start = (bf16[240,128]{1,0:T(8,128)(2,1)S(1)}, bf16[240,128]{1,0:T(8,128)(2,1)S(1)}, u32[]{:S(2)}, u32[]{:S(2)}) collective-permute-start(bf16[240,128]{1,0:T(8,128)(2,1)S(1)} %get-tuple-element.33), channel_id=1, source_target_pairs={{0,8},{8,0},{16,24},{24,16},{32,40},{40,32},{48,56},{56,48},{64,72... | collective-permute-start | bytes 184328 | tf_op jit(solution)/shard_map/ppermute | solution.py:434
  4.8 7.5 %collective-permute-start.1 = (bf16[240,128]{1,0:T(8,128)(2,1)S(1)}, bf16[240,128]{1,0:T(8,128)(2,1)S(1)}, u32[]{:S(2)}, u32[]{:S(2)}) collective-permute-start(bf16[240,128]{1,0:T(8,128)(2,1)S(1)} %get-tuple-element.34), channel_id=1, source_target_pairs={{0,120},{8,16},{16,8},{24,32},{32,24},{40,48},{48,40},{56,64},{64,... | collective-permute-start | bytes 184328 | tf_op jit(solution)/shard_map/ppermute | solution.py:444
  12.3 5.6 %collective-permute-start.3 = (bf16[240,128]{1,0:T(8,128)(2,1)S(1)}, bf16[240,128]{1,0:T(8,128)(2,1)S(1)}, u32[]{:S(2)}, u32[]{:S(2)}) collective-permute-start(bf16[240,128]{1,0:T(8,128)(2,1)S(1)} %get-tuple-element.45), channel_id=1, source_target_pairs={{0,7},{1,2},{2,1},{3,4},{4,3},{5,6},{6,5},{7,0},{8,15},{9,10},{10,... | collective-permute-start | bytes 184328 | tf_op jit(solution)/shard_map/ppermute | solution.py:444
  15.1 2.8 %collective-permute-start.2 = (bf16[240,128]{1,0:T(8,128)(2,1)S(1)}, bf16[240,128]{1,0:T(8,128)(2,1)S(1)}, u32[]{:S(2)}, u32[]{:S(2)}) collective-permute-start(bf16[240,128]{1,0:T(8,128)(2,1)S(1)} %get-tuple-element.46), channel_id=1, source_target_pairs={{0,1},{1,0},{2,3},{3,2},{4,5},{5,4},{6,7},{7,6},{8,9},{9,8},{10,11... | collective-permute-start | bytes 184328 | tf_op jit(solution)/shard_map/ppermute | solution.py:434
  18.9 1.5 %collective-permute-start.4 = (f32[56,128]{1,0:T(8,128)S(1)}, f32[56,128]{1,0:T(8,128)S(1)}, u32[]{:S(2)}, u32[]{:S(2)}) collective-permute-start(f32[56,128]{1,0:T(8,128)S(1)} %get-tuple-element.40), channel_id=1, source_target_pairs={{0,1},{1,0},{2,3},{3,2},{4,5},{5,4},{6,7},{7,6},{8,9},{9,8},{10,11... | collective-permute-start | bytes 86024 | tf_op jit(solution)/shard_map/ppermute | solution.py:434
  20.4 4.8 %collective-permute-start.7 = (f32[56,128]{1,0:T(8,128)S(1)}, f32[56,128]{1,0:T(8,128)S(1)}, u32[]{:S(2)}, u32[]{:S(2)}) collective-permute-start(f32[56,128]{1,0:T(8,128)S(1)} %add.36), channel_id=1, source_target_pairs={{0,5},{1,4},{2,7},{3,6},{4,1},{5,0},{6,3},{7,2},{8,13},{9,12},{10,... | collective-permute-start | bytes 86024 | tf_op jit(solution)/shard_map/ppermute | solution.py:439
  23.0 4.5 %collective-permute-start.6 = (f32[56,128]{1,0:T(8,128)S(1)}, f32[56,128]{1,0:T(8,128)S(1)}, u32[]{:S(2)}, u32[]{:S(2)}) collective-permute-start(f32[56,128]{1,0:T(8,128)S(1)} %add.36), channel_id=1, source_target_pairs={{0,7},{1,6},{2,5},{3,4},{4,3},{5,2},{6,1},{7,0},{8,15},{9,14},{10,... | collective-permute-start | bytes 86024 | tf_op jit(solution)/shard_map/ppermute | solution.py:439
  23.6 3.9 %collective-permute-start.5 = (f32[56,128]{1,0:T(8,128)S(1)}, f32[56,128]{1,0:T(8,128)S(1)}, u32[]{:S(2)}, u32[]{:S(2)}) collective-permute-start(f32[56,128]{1,0:T(8,128)S(1)} %add.36), channel_id=1, source_target_pairs={{0,3},{1,2},{2,1},{3,0},{4,7},{5,6},{6,5},{7,4},{8,11},{9,10},{10,... | collective-permute-start | bytes 86024 | tf_op jit(solution)/shard_map/ppermute | solution.py:439
  27.6 4.9 %collective-permute-start.10 = (f32[56,128]{1,0:T(8,128)S(1)}, f32[56,128]{1,0:T(8,128)S(1)}, u32[]{:S(2)}, u32[]{:S(2)}) collective-permute-start(f32[56,128]{1,0:T(8,128)S(1)} %add_add_fusion.1), channel_id=1, source_target_pairs={{0,17},{1,16},{8,25},{9,24},{16,1},{17,0},{24,9},{25,8},{2,19},{3,... | collective-permute-start | bytes 86024 | tf_op jit(solution)/shard_map/ppermute | solution.py:439
  27.6 5.0 %collective-permute-start.9 = (f32[56,128]{1,0:T(8,128)S(1)}, f32[56,128]{1,0:T(8,128)S(1)}, u32[]{:S(2)}, u32[]{:S(2)}) collective-permute-start(f32[56,128]{1,0:T(8,128)S(1)} %add_add_fusion.1), channel_id=1, source_target_pairs={{0,25},{1,24},{8,17},{9,16},{16,9},{17,8},{24,1},{25,0},{2,27},{3,... | collective-permute-start | bytes 86024 | tf_op jit(solution)/shard_map/ppermute | solution.py:439
  28.5 4.1 %collective-permute-start.8 = (f32[56,128]{1,0:T(8,128)S(1)}, f32[56,128]{1,0:T(8,128)S(1)}, u32[]{:S(2)}, u32[]{:S(2)}) collective-permute-start(f32[56,128]{1,0:T(8,128)S(1)} %add_add_fusion.1), channel_id=1, source_target_pairs={{0,9},{1,8},{8,1},{9,0},{16,25},{17,24},{24,17},{25,16},{2,11},{3,... | collective-permute-start | bytes 86024 | tf_op jit(solution)/shard_map/ppermute | solution.py:439
  32.6 4.9 %collective-permute-start.13 = (f32[56,128]{1,0:T(8,128)S(1)}, f32[56,128]{1,0:T(8,128)S(1)}, u32[]{:S(2)}, u32[]{:S(2)}) collective-permute-start(f32[56,128]{1,0:T(8,128)S(1)} %add_add_fusion.own_ref), channel_id=1, source_target_pairs={{0,65},{1,64},{32,97},{33,96},{64,1},{65,0},{96,33},{97,32},{2,67}... | collective-permute-start | bytes 86024 | tf_op jit(solution)/shard_map/ppermute | solution.py:439
  34.8 4.5 %collective-permute-start.12 = (f32[56,128]{1,0:T(8,128)S(1)}, f32[56,128]{1,0:T(8,128)S(1)}, u32[]{:S(2)}, u32[]{:S(2)}) collective-permute-start(f32[56,128]{1,0:T(8,128)S(1)} %add_add_fusion.own_ref), channel_id=1, source_target_pairs={{0,97},{1,96},{32,65},{33,64},{64,33},{65,32},{96,1},{97,0},{2,99}... | collective-permute-start | bytes 86024 | tf_op jit(solution)/shard_map/ppermute | solution.py:439
  35.8 3.5 %collective-permute-start.11 = (f32[56,128]{1,0:T(8,128)S(1)}, f32[56,128]{1,0:T(8,128)S(1)}, u32[]{:S(2)}, u32[]{:S(2)}) collective-permute-start(f32[56,128]{1,0:T(8,128)S(1)} %add_add_fusion.own_ref), channel_id=1, source_target_pairs={{0,33},{1,32},{32,1},{33,0},{64,97},{65,96},{96,65},{97,64},{2,35}... | collective-permute-start | bytes 86024 | tf_op jit(solution)/shard_map/ppermute | solution.py:439

commit v8 on v7

--- a/solution.py
+++ b/solution.py
@@ -28,8 +28,8 @@
 
 
 def one_hot(row):
-    cells = lax.broadcasted_iota(jnp.int32, (C, row.shape[1]), 0)
-    return jnp.where(cells == row, 1.0, 0.0).astype(BF)
+    cells = lax.broadcasted_iota(jnp.int16, (C, row.shape[1]), 0)
+    return jnp.where(cells == row.astype(jnp.int16), jnp.ones((), BF), jnp.zeros((), BF))
 
 
 def dot_nn(a, b):
@@ -166,37 +166,36 @@
 WIDE = FK + 16
 
 
-def face_blocks(first_block, count, nu_ref, basis, pair_ref, jac_ref, flag_ref, hot, got, add, image):
+def face_blocks(first_block, count, nu_ref, basis, pair_ref, jac_ref, flag_ref, hot, got, add):
     for block in range(count):
         base = (first_block + block) * BLOCK
         lanes = slice(base, base + BLOCK)
-        hot[block, :, :BLOCK] = one_hot(pair_ref[0:1, lanes])
-        hot[block, :, BLOCK:] = one_hot(pair_ref[1:2, lanes])
-        got[block] = dot_nn(basis, hot[block])
+        left = 2 * block * BLOCK
+        both = slice(left, left + 2 * BLOCK)
+        hot[:, left : left + BLOCK] = one_hot(pair_ref[0:1, lanes])
+        hot[:, left + BLOCK : left + 2 * BLOCK] = one_hot(pair_ref[1:2, lanes])
+        got[:, both] = dot_nn(basis, hot[:, both]).astype(BF)
         flags = flag_ref[0:1, lanes].astype(F32)
-        add[block, FK:] = jnp.broadcast_to(jnp.concatenate([flags, flags], axis=1), (16, 2 * BLOCK)).astype(BF)
+        add[FK:, both] = jnp.broadcast_to(jnp.concatenate([flags, flags], axis=1), (16, 2 * BLOCK)).astype(BF)
         for tile in range(BLOCK // 128):
             here = slice(base + tile * 128, base + (tile + 1) * 128)
-            at_a = slice(tile * 128, (tile + 1) * 128)
-            at_b = slice(BLOCK + tile * 128, BLOCK + (tile + 1) * 128)
-            damps = [nu_ref[0:1, g : g + 1] * flags[:, at_a] for g in range(F)]
+            at_a = slice(left + tile * 128, left + (tile + 1) * 128)
+            at_b = slice(left + BLOCK + tile * 128, left + BLOCK + (tile + 1) * 128)
+            damps = [nu_ref[0:1, g : g + 1] * flags[:, tile * 128 : (tile + 1) * 128] for g in range(F)]
             for start in range(0, K, CHUNK):
-                a = [got[block, f * K + start : f * K + start + CHUNK, at_a] for f in range(F)]
-                b = [got[block, f * K + start : f * K + start + CHUNK, at_b] for f in range(F)]
+                a = [got[f * K + start : f * K + start + CHUNK, at_a].astype(F32) for f in range(F)]
+                b = [got[f * K + start : f * K + start + CHUNK, at_b].astype(F32) for f in range(F)]
                 for g in range(F):
-                    damp = damps[g]
-                    to_a = (jac_ref[g, g, 0:1, here] - damp) * b[g]
-                    to_b = (jac_ref[g, g, 1:2, here] - damp) * a[g]
+                    to_a = (jac_ref[g, g, 0:1, here] - damps[g]) * b[g]
+                    to_b = (jac_ref[g, g, 1:2, here] - damps[g]) * a[g]
                     for f in range(F):
                         if f != g:
                             to_a = to_a + jac_ref[g, f, 0:1, here] * b[f]
                             to_b = to_b + jac_ref[g, f, 1:2, here] * a[f]
                     rows = slice(g * K + start, g * K + start + CHUNK)
-                    add[block, rows, at_a] = to_a.astype(BF)
-                    add[block, rows, at_b] = to_b.astype(BF)
-    for block in range(count):
-        image = dot_nt(add[block], hot[block]) if image is None else image + dot_nt(add[block], hot[block])
-    return image
+                    add[rows, at_a] = to_a.astype(BF)
+                    add[rows, at_b] = to_b.astype(BF)
+    return dot_nt(add[...], hot[...])
 
 
 def add_diagonal(image_ref, basis_ref, nu_ref, diag_ref):
@@ -223,12 +222,12 @@
     high = coord.astype(BF).astype(F32)
     row = lax.broadcasted_iota(jnp.int32, (16, K), 0)
     coef_ref[...] = jnp.where(row == 0, high, jnp.where(row == 1, coord - high, 0.0)).astype(BF)
-    image_ref[...] = face_blocks(0, EARLY, nu_ref, basis_ref[...], pair_ref, jac_ref, flag_ref, hot, got, add, None)
+    image_ref[...] = face_blocks(0, EARLY, nu_ref, basis_ref[...], pair_ref, jac_ref, flag_ref, hot, got, add)
     add_diagonal(image_ref, basis_ref, nu_ref, diag_ref)
 
 
 def late_kernel(nu_ref, basis_ref, pair_ref, jac_ref, flag_ref, image_ref, out_ref, hot, got, add):
-    image = face_blocks(EARLY, LATE, nu_ref, basis_ref[...], pair_ref, jac_ref, flag_ref, hot, got, add, None)
+    image = face_blocks(EARLY, LATE, nu_ref, basis_ref[...], pair_ref, jac_ref, flag_ref, hot, got, add)
     flagged = image[FK : FK + 1]
     for g in range(F):
         rows = slice(g * K, (g + 1) * K)
@@ -237,11 +236,7 @@
 
 
 def face_scratch(count):
-    return [
-        pltpu.VMEM((count, C, 2 * BLOCK), BF),
-        pltpu.VMEM((count, FK, 2 * BLOCK), F32),
-        pltpu.VMEM((count, WIDE, 2 * BLOCK), BF),
-    ]
+    return [pltpu.VMEM((rows, 2 * count * BLOCK), BF) for rows in (C, FK, WIDE)]
 
 
 def face_cost(count):

time: 43.4 us -> 43.2 us (level)
  Pallas kernels: 11.4 us -> 10.4 us
  starting transfers between devices: 21.5 us -> 22.1 us
    pallas_call x1, Pallas kernels: 3.33 us -> 2.52 us  [early_call(): pl.pallas_call(early_kernel, out_shape=(jax.ShapeDtypeStruct((WIDE, C), F...]
    ppermute x2, starting transfers between devices: 6.93 us -> 7.53 us  [swap_odd(): lax.ppermute(x, axis, [(i, (i + 1) % count if i % 2 else (i - 1) % count)...]
  transfers between devices with their start and end apart: 14 -> 14, of which waited for: 7 -> 7; matrix products, arithmetic and copies ran while one was open for 0% -> 0% of each run, Pallas kernels for 11% -> 9%
where the time goes in v8:
time: 43.2 us; the launch traced here: 43.1 us
  starting transfers between devices  22.1 us (51%)
  Pallas kernels  10.4 us (24%)
  waiting for transfers between devices  9.74 us (23%)
  between operations  0.73 us (2%)
    ppermute x9, starting transfers between devices, cross(): return lax.ppermute(x, (axis, 'col_1'), pairs)  10.2 us
    ppermute x9, waiting for transfers between devices, cross(): return lax.ppermute(x, (axis, 'col_1'), pairs)  8.88 us
    ppermute x2, starting transfers between devices, swap_odd(): lax.ppermute(x, axis, [(i, (i + 1) % count if i % 2 else (i - 1) % count)...  7.53 us
    ppermute x3, starting transfers between devices, swap(): return lax.ppermute(x, axis, [(i, i ^ step) for i in range(count)])  4.37 us
    pallas_call x1, Pallas kernels, solve_call(): pl.pallas_call(functools.partial(solve_kernel, row_scale), out_shape=(jax...  3.79 us
    pallas_call x1, Pallas kernels, early_call(): pl.pallas_call(early_kernel, out_shape=(jax.ShapeDtypeStruct((WIDE, C), F...  2.52 us
    pallas_call x1, Pallas kernels, ghost_call(): pl.pallas_call(ghost_kernel, out_shape=(message,) * 4 + tuple((jax.ShapeD...  1.91 us
    pallas_call x1, Pallas kernels, late_call(): pl.pallas_call(late_kernel, out_shape=jax.ShapeDtypeStruct((FK, C), F32),...  1.22 us
  transfers between devices with their start and end apart: 14, of which 7 were waited for; matrix products, arithmetic and copies ran while one was open for 0% of the time, Pallas kernels for 9%

profile of v8, /device:TPU:1, one launch (start us, length us, event | category | flops | bytes accessed | tf_op | source)
XLA Modules:
  0.0 43.1 jit_solution(5701271554054789002)
XLA Ops:
  0.6 1.9 %ghost.1 = (bf16[240,128]{1,0:T(8,128)(2,1)S(1)}, bf16[240,128]{1,0:T(8,128)(2,1)S(1)}, bf16[240,128]{1,0:T(8,128)(2,1)S(1)}, bf16[240,128]{1,0:T(8,128)(2,1)S(1...) custom-call(s32[1,8]{1,0:T(1,128)} %bitcast.14, ...), custom_call_target="tpu_custom_call" | custom-call | tf_op jit(solution)/shard_map/ghost/pallas_call | solution.py:145
  2.6 2.2 %collective-permute-start = (bf16[240,128]{1,0:T(8,128)(2,1)S(1)}, bf16[240,128]{1,0:T(8,128)(2,1)S(1)}, u32[]{:S(2)}, u32[]{:S(2)}) collective-permute-start(bf16[240,128]{1,0:T(8,128)(2,1)S(1)} %get-tuple-element.33), channel_id=1, source_target_pairs={{0,8},{8,0},{16,24},{24,16},{32,40},{40,32},{48,56},{56,48},{64,72... | collective-permute-start | bytes 184328 | tf_op jit(solution)/shard_map/ppermute | solution.py:429
  4.8 4.1 %collective-permute-start.1 = (bf16[240,128]{1,0:T(8,128)(2,1)S(1)}, bf16[240,128]{1,0:T(8,128)(2,1)S(1)}, u32[]{:S(2)}, u32[]{:S(2)}) collective-permute-start(bf16[240,128]{1,0:T(8,128)(2,1)S(1)} %get-tuple-element.34), channel_id=1, source_target_pairs={{0,120},{8,16},{16,8},{24,32},{32,24},{40,48},{48,40},{56,64},{64,... | collective-permute-start | bytes 184328 | tf_op jit(solution)/shard_map/ppermute | solution.py:439
  8.9 2.5 %early_faces.1 = (f32[496,512]{1,0:T(8,128)S(1)}, bf16[512,256]{1,0:T(8,128)(2,1)S(1)}, bf16[16,96]{1,0:T(8,128)(2,1)S(1)}) custom-call(f32[1,5]{1,0:T(1,128)S(1)} %get-tuple-element.24.nu_ref, bf16[480,512]{1,0:T(8,128)(2,1)S(1)} %get-tuple-element.25.basis_ref, f32[5,5,512]{2,1,0:T(8,128)S(1)} %get-tuple-element.29.diag_ref, ...), custom_call_target="tpu_custom_call" | custom-call | flops 3750000128 | bytes 2000000 | tf_op jit(solution)/shard_map/early_faces/pallas_call | solution.py:247
  11.4 0.0 collective-permute-done.row_a
  11.4 0.0 collective-permute-done.1.row_b
  11.5 3.4 %collective-permute-start.3 = (bf16[240,128]{1,0:T(8,128)(2,1)S(1)}, bf16[240,128]{1,0:T(8,128)(2,1)S(1)}, u32[]{:S(2)}, u32[]{:S(2)}) collective-permute-start(bf16[240,128]{1,0:T(8,128)(2,1)S(1)} %get-tuple-element.45), channel_id=1, source_target_pairs={{0,7},{1,2},{2,1},{3,4},{4,3},{5,6},{6,5},{7,0},{8,15},{9,10},{10,... | collective-permute-start | bytes 184328 | tf_op jit(solution)/shard_map/ppermute | solution.py:439
  14.9 0.8 %collective-permute-start.2 = (bf16[240,128]{1,0:T(8,128)(2,1)S(1)}, bf16[240,128]{1,0:T(8,128)(2,1)S(1)}, u32[]{:S(2)}, u32[]{:S(2)}) collective-permute-start(bf16[240,128]{1,0:T(8,128)(2,1)S(1)} %get-tuple-element.46), channel_id=1, source_target_pairs={{0,1},{1,0},{2,3},{3,2},{4,5},{5,4},{6,7},{7,6},{8,9},{9,8},{10,11... | collective-permute-start | bytes 184328 | tf_op jit(solution)/shard_map/ppermute | solution.py:429
  15.7 1.2 %late_faces.1.image_ref = f32[480,512]{1,0:T(8,128)S(1)} custom-call(f32[1,5]{1,0:T(1,128)S(1)} %get-tuple-element.24.nu_ref, bf16[480,512]{1,0:T(8,128)(2,1)S(1)} %get-tuple-element.25.basis_ref, s32[2,1024]{1,0:T(2,128)S(1)} %get-tuple-element.26.pair_ref, f32[5,5,2,1024]{3,2,1,0:T(2,128)S(1)} %get-tuple-element.27.jac_ref, ...), custom_call_target="tpu_custom_call" | custom-call | flops 1250000000 | bytes 2000000 | tf_op jit(solution)/shard_map/late_faces/pallas_call | solution.py:264
  16.9 0.0 collective-permute-done.3.col_b
  16.9 0.0 collective-permute-done.2.col_a
  17.0 1.0 %finish.1 = (bf16[5,96,512]{2,1,0:T(8,128)(2,1)S(1)}, f32[56,128]{1,0:T(8,128)S(1)}) custom-call(f32[480,512]{1,0:T(8,128)S(1)} %late_faces.1.image_ref, bf16[240,128]{1,0:T(8,128)(2,1)S(1)} %collective-permute-done.row_a, bf16[240,128]{1,0:T(8,128)(2,1)S(1)} %collective-permute-done.1.row_b, bf16[240,128]{1,0:T(8,128)(2,1)S(1)} %collective-permute-done.2.col_a, ...), custom_call_target="tpu_custom_call" | custom-call | tf_op jit(solution)/shard_map/finish/pallas_call | solution.py:336
  18.0 1.4 %collective-permute-start.4 = (f32[56,128]{1,0:T(8,128)S(1)}, f32[56,128]{1,0:T(8,128)S(1)}, u32[]{:S(2)}, u32[]{:S(2)}) collective-permute-start(f32[56,128]{1,0:T(8,128)S(1)} %get-tuple-element.40), channel_id=1, source_target_pairs={{0,1},{1,0},{2,3},{3,2},{4,5},{5,4},{6,7},{7,6},{8,9},{9,8},{10,11... | collective-permute-start | bytes 86024 | tf_op jit(solution)/shard_map/ppermute | solution.py:429
  19.3 0.9 %collective-permute-done.4 = f32[56,128]{1,0:T(8,128)S(1)} collective-permute-done((f32[56,128]{1,0:T(8,128)S(1)}, f32[56,128]{1,0:T(8,128)S(1)}, u32[]{:S(2)}, u32[]{:S(2)}) %collective-permute-start.4) | collective-permute-done | bytes 28704 | tf_op jit(solution)/shard_map/ppermute | solution.py:429
  20.2 2.6 %collective-permute-start.7 = (f32[56,128]{1,0:T(8,128)S(1)}, f32[56,128]{1,0:T(8,128)S(1)}, u32[]{:S(2)}, u32[]{:S(2)}) collective-permute-start(f32[56,128]{1,0:T(8,128)S(1)} %add.36), channel_id=1, source_target_pairs={{0,5},{1,4},{2,7},{3,6},{4,1},{5,0},{6,3},{7,2},{8,13},{9,12},{10,... | collective-permute-start | bytes 86024 | tf_op jit(solution)/shard_map/ppermute | solution.py:434
  22.8 0.6 %collective-permute-start.6 = (f32[56,128]{1,0:T(8,128)S(1)}, f32[56,128]{1,0:T(8,128)S(1)}, u32[]{:S(2)}, u32[]{:S(2)}) collective-permute-start(f32[56,128]{1,0:T(8,128)S(1)} %add.36), channel_id=1, source_target_pairs={{0,7},{1,6},{2,5},{3,4},{4,3},{5,2},{6,1},{7,0},{8,15},{9,14},{10,... | collective-permute-start | bytes 86024 | tf_op jit(solution)/shard_map/ppermute | solution.py:434
  23.4 0.2 collective-permute-start.5
  23.6 1.4 %collective-permute-done.7 = f32[56,128]{1,0:T(8,128)S(1)} collective-permute-done((f32[56,128]{1,0:T(8,128)S(1)}, f32[56,128]{1,0:T(8,128)S(1)}, u32[]{:S(2)}, u32[]{:S(2)}) %collective-permute-start.7) | collective-permute-done | bytes 28704 | tf_op jit(solution)/shard_map/ppermute | solution.py:434
  25.0 2.3 %collective-permute-done.6 = f32[56,128]{1,0:T(8,128)S(1)} collective-permute-done((f32[56,128]{1,0:T(8,128)S(1)}, f32[56,128]{1,0:T(8,128)S(1)}, u32[]{:S(2)}, u32[]{:S(2)}) %collective-permute-start.6) | collective-permute-done | bytes 28704 | tf_op jit(solution)/shard_map/ppermute | solution.py:434
  27.3 0.0 collective-permute-done.5
  27.3 0.1 collective-permute-start.10
  27.4 0.8 %collective-permute-start.9 = (f32[56,128]{1,0:T(8,128)S(1)}, f32[56,128]{1,0:T(8,128)S(1)}, u32[]{:S(2)}, u32[]{:S(2)}) collective-permute-start(f32[56,128]{1,0:T(8,128)S(1)} %add_add_fusion.1), channel_id=1, source_target_pairs={{0,25},{1,24},{8,17},{9,16},{16,9},{17,8},{24,1},{25,0},{2,27},{3,... | collective-permute-start | bytes 86024 | tf_op jit(solution)/shard_map/ppermute | solution.py:434
  28.2 2.1 %collective-permute-start.8 = (f32[56,128]{1,0:T(8,128)S(1)}, f32[56,128]{1,0:T(8,128)S(1)}, u32[]{:S(2)}, u32[]{:S(2)}) collective-permute-start(f32[56,128]{1,0:T(8,128)S(1)} %add_add_fusion.1), channel_id=1, source_target_pairs={{0,9},{1,8},{8,1},{9,0},{16,25},{17,24},{24,17},{25,16},{2,11},{3,... | collective-permute-start | bytes 86024 | tf_op jit(solution)/shard_map/ppermute | solution.py:434
  30.4 1.9 %collective-permute-done.10 = f32[56,128]{1,0:T(8,128)S(1)} collective-permute-done((f32[56,128]{1,0:T(8,128)S(1)}, f32[56,128]{1,0:T(8,128)S(1)}, u32[]{:S(2)}, u32[]{:S(2)}) %collective-permute-start.10) | collective-permute-done | bytes 28704 | tf_op jit(solution)/shard_map/ppermute | solution.py:434
  32.2 0.2 collective-permute-done.9
  32.4 0.0 collective-permute-done.8
  32.4 2.3 %collective-permute-start.13 = (f32[56,128]{1,0:T(8,128)S(1)}, f32[56,128]{1,0:T(8,128)S(1)}, u32[]{:S(2)}, u32[]{:S(2)}) collective-permute-start(f32[56,128]{1,0:T(8,128)S(1)} %add_add_fusion.own_ref), channel_id=1, source_target_pairs={{0,65},{1,64},{32,97},{33,96},{64,1},{65,0},{96,33},{97,32},{2,67}... | collective-permute-start | bytes 86024 | tf_op jit(solution)/shard_map/ppermute | solution.py:434
  34.8 0.9 %collective-permute-start.12 = (f32[56,128]{1,0:T(8,128)S(1)}, f32[56,128]{1,0:T(8,128)S(1)}, u32[]{:S(2)}, u32[]{:S(2)}) collective-permute-start(f32[56,128]{1,0:T(8,128)S(1)} %add_add_fusion.own_ref), channel_id=1, source_target_pairs={{0,97},{1,96},{32,65},{33,64},{64,33},{65,32},{96,1},{97,0},{2,99}... | collective-permute-start | bytes 86024 | tf_op jit(solution)/shard_map/ppermute | solution.py:434
  35.6 0.5 %collective-permute-start.11 = (f32[56,128]{1,0:T(8,128)S(1)}, f32[56,128]{1,0:T(8,128)S(1)}, u32[]{:S(2)}, u32[]{:S(2)}) collective-permute-start(f32[56,128]{1,0:T(8,128)S(1)} %add_add_fusion.own_ref), channel_id=1, source_target_pairs={{0,33},{1,32},{32,1},{33,0},{64,97},{65,96},{96,65},{97,64},{2,35}... | collective-permute-start | bytes 86024 | tf_op jit(solution)/shard_map/ppermute | solution.py:434
  36.2 1.1 %collective-permute-done.13.two_ref = f32[56,128]{1,0:T(8,128)S(1)} collective-permute-done((f32[56,128]{1,0:T(8,128)S(1)}, f32[56,128]{1,0:T(8,128)S(1)}, u32[]{:S(2)}, u32[]{:S(2)}) %collective-permute-start.13) | collective-permute-done | bytes 28704 | tf_op jit(solution)/shard_map/ppermute | solution.py:434
  37.3 2.0 %collective-permute-done.12.three_ref = f32[56,128]{1,0:T(8,128)S(1)} collective-permute-done((f32[56,128]{1,0:T(8,128)S(1)}, f32[56,128]{1,0:T(8,128)S(1)}, u32[]{:S(2)}, u32[]{:S(2)}) %collective-permute-start.12) | collective-permute-done | bytes 28704 | tf_op jit(solution)/shard_map/ppermute | solution.py:434
  39.3 0.0 collective-permute-done.11.one_ref
  39.3 3.8 %solve.1 = (f32[97,97]{1,0:T(8,128)}, f32[1,96]{1,0:T(1,128)}, bf16[5,96,512]{2,1,0:T(8,128)(2,1)}) custom-call(f32[56,128]{1,0:T(8,128)S(1)} %collective-permute-done.11.one_ref, f32[56,128]{1,0:T(8,128)S(1)} %collective-permute-done.12.three_ref, f32[56,128]{1,0:T(8,128)S(1)} %collective-permute-done.13.two_ref, f32[56,128]{1,0:T(8,128)S(1)} %add_add_fusion.own_ref, ...), custom_call_target="tpu_custom_call" | custom-call | tf_op jit(solution)/shard_map/solve/pallas_call | solution.py:412
  (6 shorter events, 0.1 us)
Async XLA Ops:
  2.6 8.9 %collective-permute-start = (bf16[240,128]{1,0:T(8,128)(2,1)S(1)}, bf16[240,128]{1,0:T(8,128)(2,1)S(1)}, u32[]{:S(2)}, u32[]{:S(2)}) collective-permute-start(bf16[240,128]{1,0:T(8,128)(2,1)S(1)} %get-tuple-element.33), channel_id=1, source_target_pairs={{0,8},{8,0},{16,24},{24,16},{32,40},{40,32},{48,56},{56,48},{64,72... | collective-permute-start | bytes 184328 | tf_op jit(solution)/shard_map/ppermute | solution.py:429
  4.8 6.7 %collective-permute-start.1 = (bf16[240,128]{1,0:T(8,128)(2,1)S(1)}, bf16[240,128]{1,0:T(8,128)(2,1)S(1)}, u32[]{:S(2)}, u32[]{:S(2)}) collective-permute-start(bf16[240,128]{1,0:T(8,128)(2,1)S(1)} %get-tuple-element.34), channel_id=1, source_target_pairs={{0,120},{8,16},{16,8},{24,32},{32,24},{40,48},{48,40},{56,64},{64,... | collective-permute-start | bytes 184328 | tf_op jit(solution)/shard_map/ppermute | solution.py:439
  11.5 5.5 %collective-permute-start.3 = (bf16[240,128]{1,0:T(8,128)(2,1)S(1)}, bf16[240,128]{1,0:T(8,128)(2,1)S(1)}, u32[]{:S(2)}, u32[]{:S(2)}) collective-permute-start(bf16[240,128]{1,0:T(8,128)(2,1)S(1)} %get-tuple-element.45), channel_id=1, source_target_pairs={{0,7},{1,2},{2,1},{3,4},{4,3},{5,6},{6,5},{7,0},{8,15},{9,10},{10,... | collective-permute-start | bytes 184328 | tf_op jit(solution)/shard_map/ppermute | solution.py:439
  14.9 2.0 %collective-permute-start.2 = (bf16[240,128]{1,0:T(8,128)(2,1)S(1)}, bf16[240,128]{1,0:T(8,128)(2,1)S(1)}, u32[]{:S(2)}, u32[]{:S(2)}) collective-permute-start(bf16[240,128]{1,0:T(8,128)(2,1)S(1)} %get-tuple-element.46), channel_id=1, source_target_pairs={{0,1},{1,0},{2,3},{3,2},{4,5},{5,4},{6,7},{7,6},{8,9},{9,8},{10,11... | collective-permute-start | bytes 184328 | tf_op jit(solution)/shard_map/ppermute | solution.py:429
  18.0 2.2 %collective-permute-start.4 = (f32[56,128]{1,0:T(8,128)S(1)}, f32[56,128]{1,0:T(8,128)S(1)}, u32[]{:S(2)}, u32[]{:S(2)}) collective-permute-start(f32[56,128]{1,0:T(8,128)S(1)} %get-tuple-element.40), channel_id=1, source_target_pairs={{0,1},{1,0},{2,3},{3,2},{4,5},{5,4},{6,7},{7,6},{8,9},{9,8},{10,11... | collective-permute-start | bytes 86024 | tf_op jit(solution)/shard_map/ppermute | solution.py:429
  20.2 4.8 %collective-permute-start.7 = (f32[56,128]{1,0:T(8,128)S(1)}, f32[56,128]{1,0:T(8,128)S(1)}, u32[]{:S(2)}, u32[]{:S(2)}) collective-permute-start(f32[56,128]{1,0:T(8,128)S(1)} %add.36), channel_id=1, source_target_pairs={{0,5},{1,4},{2,7},{3,6},{4,1},{5,0},{6,3},{7,2},{8,13},{9,12},{10,... | collective-permute-start | bytes 86024 | tf_op jit(solution)/shard_map/ppermute | solution.py:434
  22.8 4.5 %collective-permute-start.6 = (f32[56,128]{1,0:T(8,128)S(1)}, f32[56,128]{1,0:T(8,128)S(1)}, u32[]{:S(2)}, u32[]{:S(2)}) collective-permute-start(f32[56,128]{1,0:T(8,128)S(1)} %add.36), channel_id=1, source_target_pairs={{0,7},{1,6},{2,5},{3,4},{4,3},{5,2},{6,1},{7,0},{8,15},{9,14},{10,... | collective-permute-start | bytes 86024 | tf_op jit(solution)/shard_map/ppermute | solution.py:434
  23.4 3.9 %collective-permute-start.5 = (f32[56,128]{1,0:T(8,128)S(1)}, f32[56,128]{1,0:T(8,128)S(1)}, u32[]{:S(2)}, u32[]{:S(2)}) collective-permute-start(f32[56,128]{1,0:T(8,128)S(1)} %add.36), channel_id=1, source_target_pairs={{0,3},{1,2},{2,1},{3,0},{4,7},{5,6},{6,5},{7,4},{8,11},{9,10},{10,... | collective-permute-start | bytes 86024 | tf_op jit(solution)/shard_map/ppermute | solution.py:434
  27.3 4.9 %collective-permute-start.10 = (f32[56,128]{1,0:T(8,128)S(1)}, f32[56,128]{1,0:T(8,128)S(1)}, u32[]{:S(2)}, u32[]{:S(2)}) collective-permute-start(f32[56,128]{1,0:T(8,128)S(1)} %add_add_fusion.1), channel_id=1, source_target_pairs={{0,17},{1,16},{8,25},{9,24},{16,1},{17,0},{24,9},{25,8},{2,19},{3,... | collective-permute-start | bytes 86024 | tf_op jit(solution)/shard_map/ppermute | solution.py:434
  27.4 5.0 %collective-permute-start.9 = (f32[56,128]{1,0:T(8,128)S(1)}, f32[56,128]{1,0:T(8,128)S(1)}, u32[]{:S(2)}, u32[]{:S(2)}) collective-permute-start(f32[56,128]{1,0:T(8,128)S(1)} %add_add_fusion.1), channel_id=1, source_target_pairs={{0,25},{1,24},{8,17},{9,16},{16,9},{17,8},{24,1},{25,0},{2,27},{3,... | collective-permute-start | bytes 86024 | tf_op jit(solution)/shard_map/ppermute | solution.py:434
  28.2 4.2 %collective-permute-start.8 = (f32[56,128]{1,0:T(8,128)S(1)}, f32[56,128]{1,0:T(8,128)S(1)}, u32[]{:S(2)}, u32[]{:S(2)}) collective-permute-start(f32[56,128]{1,0:T(8,128)S(1)} %add_add_fusion.1), channel_id=1, source_target_pairs={{0,9},{1,8},{8,1},{9,0},{16,25},{17,24},{24,17},{25,16},{2,11},{3,... | collective-permute-start | bytes 86024 | tf_op jit(solution)/shard_map/ppermute | solution.py:434
  32.4 4.9 %collective-permute-start.13 = (f32[56,128]{1,0:T(8,128)S(1)}, f32[56,128]{1,0:T(8,128)S(1)}, u32[]{:S(2)}, u32[]{:S(2)}) collective-permute-start(f32[56,128]{1,0:T(8,128)S(1)} %add_add_fusion.own_ref), channel_id=1, source_target_pairs={{0,65},{1,64},{32,97},{33,96},{64,1},{65,0},{96,33},{97,32},{2,67}... | collective-permute-start | bytes 86024 | tf_op jit(solution)/shard_map/ppermute | solution.py:434
  34.8 4.5 %collective-permute-start.12 = (f32[56,128]{1,0:T(8,128)S(1)}, f32[56,128]{1,0:T(8,128)S(1)}, u32[]{:S(2)}, u32[]{:S(2)}) collective-permute-start(f32[56,128]{1,0:T(8,128)S(1)} %add_add_fusion.own_ref), channel_id=1, source_target_pairs={{0,97},{1,96},{32,65},{33,64},{64,33},{65,32},{96,1},{97,0},{2,99}... | collective-permute-start | bytes 86024 | tf_op jit(solution)/shard_map/ppermute | solution.py:434
  35.6 3.7 %collective-permute-start.11 = (f32[56,128]{1,0:T(8,128)S(1)}, f32[56,128]{1,0:T(8,128)S(1)}, u32[]{:S(2)}, u32[]{:S(2)}) collective-permute-start(f32[56,128]{1,0:T(8,128)S(1)} %add_add_fusion.own_ref), channel_id=1, source_target_pairs={{0,33},{1,32},{32,1},{33,0},{64,97},{65,96},{96,65},{97,64},{2,35}... | collective-permute-start | bytes 86024 | tf_op jit(solution)/shard_map/ppermute | solution.py:434

commit v9 on v8

--- a/solution.py
+++ b/solution.py
@@ -96,8 +96,12 @@
         (nu_hbm, nu_ref),
     )
     copies = [pltpu.make_async_copy(src, dst, sems.at[i]) for i, (src, dst) in enumerate(pairs)]
-    for i in (1, 2, 0, 3, 4, 5, 6, 7, 8, 9, 10, 11):
-        copies[i].start()
+    fields = [
+        pltpu.make_async_copy(basis_hbm.at[f * K : (f + 1) * K], basis_ref.at[f * K : (f + 1) * K], sems.at[12 + f])
+        for f in range(F)
+    ]
+    for copy in copies[1:3] + fields + copies[3:]:
+        copy.start()
     odd_i, odd_j = parities()
     copies[1].wait()
     copies[2].wait()
@@ -118,10 +122,9 @@
     hot = one_hot(jnp.concatenate(send_order(index, -1, odd_i, odd_j), axis=-1))
     copies[3].wait()
     weights = [jnp.concatenate(send_order(jac_ref[g], 0.0, odd_i, odd_j), axis=-1) for g in range(F)]
-    copies[0].wait()
-    taken = dot_nn(basis_ref[...], hot)
     for f in range(F):
-        val[f] = taken[f * K : (f + 1) * K]
+        fields[f].wait()
+        val[f] = dot_nn(basis_ref[f * K : (f + 1) * K], hot)
     low = lax.broadcasted_iota(jnp.int32, (1, 128), 1) < 64
     parts = []
     for g in range(F):
@@ -152,7 +155,7 @@
             pltpu.VMEM((1, S), jnp.int32),
             pltpu.VMEM((F, F, S), F32),
             pltpu.VMEM((F, K, 256), F32),
-            pltpu.SemaphoreType.DMA((12,)),
+            pltpu.SemaphoreType.DMA((17,)),
         ],
         compiler_params=pltpu.CompilerParams(vmem_limit_bytes=VMEM_LIMIT),
         name="ghost",

time: 43.2 us -> 44 us (1.019)
  Pallas kernels: 10.4 us -> 11.2 us
    pallas_call x1, Pallas kernels: 1.91 us -> 2.67 us  [ghost_call(): pl.pallas_call(ghost_kernel, out_shape=(message,) * 4 + tuple((jax.ShapeD...]
where the time goes in v9:
time: 44 us; the launch traced here: 43.9 us
  starting transfers between devices  22.1 us (50%)
  Pallas kernels  11.2 us (25%)
  waiting for transfers between devices  9.75 us (22%)
  between operations  0.73 us (2%)
    ppermute x9, starting transfers between devices, cross(): return lax.ppermute(x, (axis, 'col_1'), pairs)  10.2 us
    ppermute x9, waiting for transfers between devices, cross(): return lax.ppermute(x, (axis, 'col_1'), pairs)  8.89 us
    ppermute x2, starting transfers between devices, swap_odd(): lax.ppermute(x, axis, [(i, (i + 1) % count if i % 2 else (i - 1) % count)...  7.53 us
    ppermute x3, starting transfers between devices, swap(): return lax.ppermute(x, axis, [(i, i ^ step) for i in range(count)])  4.38 us
    pallas_call x1, Pallas kernels, solve_call(): pl.pallas_call(functools.partial(solve_kernel, row_scale), out_shape=(jax...  3.79 us
    pallas_call x1, Pallas kernels, ghost_call(): pl.pallas_call(ghost_kernel, out_shape=(message,) * 4 + tuple((jax.ShapeD...  2.67 us
    pallas_call x1, Pallas kernels, early_call(): pl.pallas_call(early_kernel, out_shape=(jax.ShapeDtypeStruct((WIDE, C), F...  2.52 us
    pallas_call x1, Pallas kernels, late_call(): pl.pallas_call(late_kernel, out_shape=jax.ShapeDtypeStruct((FK, C), F32),...  1.22 us
  transfers between devices with their start and end apart: 14, of which 7 were waited for; matrix products, arithmetic and copies ran while one was open for 0% of the time, Pallas kernels for 9%

profile of v9, /device:TPU:1, one launch (start us, length us, event | category | flops | bytes accessed | tf_op | source)
XLA Modules:
  0.0 43.9 jit_solution(7209846912265205977)
XLA Ops:
  0.6 2.7 %ghost.1 = (bf16[240,128]{1,0:T(8,128)(2,1)S(1)}, bf16[240,128]{1,0:T(8,128)(2,1)S(1)}, bf16[240,128]{1,0:T(8,128)(2,1)S(1)}, bf16[240,128]{1,0:T(8,128)(2,1)S(1...) custom-call(s32[1,8]{1,0:T(1,128)} %bitcast.14, ...), custom_call_target="tpu_custom_call" | custom-call | tf_op jit(solution)/shard_map/ghost/pallas_call | solution.py:148
  3.3 2.2 %collective-permute-start = (bf16[240,128]{1,0:T(8,128)(2,1)S(1)}, bf16[240,128]{1,0:T(8,128)(2,1)S(1)}, u32[]{:S(2)}, u32[]{:S(2)}) collective-permute-start(bf16[240,128]{1,0:T(8,128)(2,1)S(1)} %get-tuple-element.33), channel_id=1, source_target_pairs={{0,8},{8,0},{16,24},{24,16},{32,40},{40,32},{48,56},{56,48},{64,72... | collective-permute-start | bytes 184328 | tf_op jit(solution)/shard_map/ppermute | solution.py:432
  5.5 4.1 %collective-permute-start.1 = (bf16[240,128]{1,0:T(8,128)(2,1)S(1)}, bf16[240,128]{1,0:T(8,128)(2,1)S(1)}, u32[]{:S(2)}, u32[]{:S(2)}) collective-permute-start(bf16[240,128]{1,0:T(8,128)(2,1)S(1)} %get-tuple-element.34), channel_id=1, source_target_pairs={{0,120},{8,16},{16,8},{24,32},{32,24},{40,48},{48,40},{56,64},{64,... | collective-permute-start | bytes 184328 | tf_op jit(solution)/shard_map/ppermute | solution.py:442
  9.6 2.5 %early_faces.1 = (f32[496,512]{1,0:T(8,128)S(1)}, bf16[512,256]{1,0:T(8,128)(2,1)S(1)}, bf16[16,96]{1,0:T(8,128)(2,1)S(1)}) custom-call(f32[1,5]{1,0:T(1,128)S(1)} %get-tuple-element.24.nu_ref, bf16[480,512]{1,0:T(8,128)(2,1)S(1)} %get-tuple-element.25.basis_ref, f32[5,5,512]{2,1,0:T(8,128)S(1)} %get-tuple-element.29.diag_ref, ...), custom_call_target="tpu_custom_call" | custom-call | flops 3750000128 | bytes 2000000 | tf_op jit(solution)/shard_map/early_faces/pallas_call | solution.py:250
  12.2 0.0 collective-permute-done.row_a
  12.2 0.0 collective-permute-done.1.row_b
  12.2 3.4 %collective-permute-start.3 = (bf16[240,128]{1,0:T(8,128)(2,1)S(1)}, bf16[240,128]{1,0:T(8,128)(2,1)S(1)}, u32[]{:S(2)}, u32[]{:S(2)}) collective-permute-start(bf16[240,128]{1,0:T(8,128)(2,1)S(1)} %get-tuple-element.45), channel_id=1, source_target_pairs={{0,7},{1,2},{2,1},{3,4},{4,3},{5,6},{6,5},{7,0},{8,15},{9,10},{10,... | collective-permute-start | bytes 184328 | tf_op jit(solution)/shard_map/ppermute | solution.py:442
  15.7 0.8 %collective-permute-start.2 = (bf16[240,128]{1,0:T(8,128)(2,1)S(1)}, bf16[240,128]{1,0:T(8,128)(2,1)S(1)}, u32[]{:S(2)}, u32[]{:S(2)}) collective-permute-start(bf16[240,128]{1,0:T(8,128)(2,1)S(1)} %get-tuple-element.46), channel_id=1, source_target_pairs={{0,1},{1,0},{2,3},{3,2},{4,5},{5,4},{6,7},{7,6},{8,9},{9,8},{10,11... | collective-permute-start | bytes 184328 | tf_op jit(solution)/shard_map/ppermute | solution.py:432
  16.5 1.2 %late_faces.1.image_ref = f32[480,512]{1,0:T(8,128)S(1)} custom-call(f32[1,5]{1,0:T(1,128)S(1)} %get-tuple-element.24.nu_ref, bf16[480,512]{1,0:T(8,128)(2,1)S(1)} %get-tuple-element.25.basis_ref, s32[2,1024]{1,0:T(2,128)S(1)} %get-tuple-element.26.pair_ref, f32[5,5,2,1024]{3,2,1,0:T(2,128)S(1)} %get-tuple-element.27.jac_ref, ...), custom_call_target="tpu_custom_call" | custom-call | flops 1250000000 | bytes 2000000 | tf_op jit(solution)/shard_map/late_faces/pallas_call | solution.py:267
  17.7 0.0 collective-permute-done.3.col_b
  17.7 0.0 collective-permute-done.2.col_a
  17.7 1.0 %finish.1 = (bf16[5,96,512]{2,1,0:T(8,128)(2,1)S(1)}, f32[56,128]{1,0:T(8,128)S(1)}) custom-call(f32[480,512]{1,0:T(8,128)S(1)} %late_faces.1.image_ref, bf16[240,128]{1,0:T(8,128)(2,1)S(1)} %collective-permute-done.row_a, bf16[240,128]{1,0:T(8,128)(2,1)S(1)} %collective-permute-done.1.row_b, bf16[240,128]{1,0:T(8,128)(2,1)S(1)} %collective-permute-done.2.col_a, ...), custom_call_target="tpu_custom_call" | custom-call | tf_op jit(solution)/shard_map/finish/pallas_call | solution.py:339
  18.7 1.4 %collective-permute-start.4 = (f32[56,128]{1,0:T(8,128)S(1)}, f32[56,128]{1,0:T(8,128)S(1)}, u32[]{:S(2)}, u32[]{:S(2)}) collective-permute-start(f32[56,128]{1,0:T(8,128)S(1)} %get-tuple-element.40), channel_id=1, source_target_pairs={{0,1},{1,0},{2,3},{3,2},{4,5},{5,4},{6,7},{7,6},{8,9},{9,8},{10,11... | collective-permute-start | bytes 86024 | tf_op jit(solution)/shard_map/ppermute | solution.py:432
  20.1 0.9 %collective-permute-done.4 = f32[56,128]{1,0:T(8,128)S(1)} collective-permute-done((f32[56,128]{1,0:T(8,128)S(1)}, f32[56,128]{1,0:T(8,128)S(1)}, u32[]{:S(2)}, u32[]{:S(2)}) %collective-permute-start.4) | collective-permute-done | bytes 28704 | tf_op jit(solution)/shard_map/ppermute | solution.py:432
  20.9 2.6 %collective-permute-start.7 = (f32[56,128]{1,0:T(8,128)S(1)}, f32[56,128]{1,0:T(8,128)S(1)}, u32[]{:S(2)}, u32[]{:S(2)}) collective-permute-start(f32[56,128]{1,0:T(8,128)S(1)} %add.36), channel_id=1, source_target_pairs={{0,5},{1,4},{2,7},{3,6},{4,1},{5,0},{6,3},{7,2},{8,13},{9,12},{10,... | collective-permute-start | bytes 86024 | tf_op jit(solution)/shard_map/ppermute | solution.py:437
  23.6 0.6 %collective-permute-start.6 = (f32[56,128]{1,0:T(8,128)S(1)}, f32[56,128]{1,0:T(8,128)S(1)}, u32[]{:S(2)}, u32[]{:S(2)}) collective-permute-start(f32[56,128]{1,0:T(8,128)S(1)} %add.36), channel_id=1, source_target_pairs={{0,7},{1,6},{2,5},{3,4},{4,3},{5,2},{6,1},{7,0},{8,15},{9,14},{10,... | collective-permute-start | bytes 86024 | tf_op jit(solution)/shard_map/ppermute | solution.py:437
  24.2 0.2 collective-permute-start.5
  24.4 1.4 %collective-permute-done.7 = f32[56,128]{1,0:T(8,128)S(1)} collective-permute-done((f32[56,128]{1,0:T(8,128)S(1)}, f32[56,128]{1,0:T(8,128)S(1)}, u32[]{:S(2)}, u32[]{:S(2)}) %collective-permute-start.7) | collective-permute-done | bytes 28704 | tf_op jit(solution)/shard_map/ppermute | solution.py:437
  25.8 2.3 %collective-permute-done.6 = f32[56,128]{1,0:T(8,128)S(1)} collective-permute-done((f32[56,128]{1,0:T(8,128)S(1)}, f32[56,128]{1,0:T(8,128)S(1)}, u32[]{:S(2)}, u32[]{:S(2)}) %collective-permute-start.6) | collective-permute-done | bytes 28704 | tf_op jit(solution)/shard_map/ppermute | solution.py:437
  28.1 0.0 collective-permute-done.5
  28.1 0.1 collective-permute-start.10
  28.2 0.8 %collective-permute-start.9 = (f32[56,128]{1,0:T(8,128)S(1)}, f32[56,128]{1,0:T(8,128)S(1)}, u32[]{:S(2)}, u32[]{:S(2)}) collective-permute-start(f32[56,128]{1,0:T(8,128)S(1)} %add_add_fusion.1), channel_id=1, source_target_pairs={{0,25},{1,24},{8,17},{9,16},{16,9},{17,8},{24,1},{25,0},{2,27},{3,... | collective-permute-start | bytes 86024 | tf_op jit(solution)/shard_map/ppermute | solution.py:437
  29.0 2.1 %collective-permute-start.8 = (f32[56,128]{1,0:T(8,128)S(1)}, f32[56,128]{1,0:T(8,128)S(1)}, u32[]{:S(2)}, u32[]{:S(2)}) collective-permute-start(f32[56,128]{1,0:T(8,128)S(1)} %add_add_fusion.1), channel_id=1, source_target_pairs={{0,9},{1,8},{8,1},{9,0},{16,25},{17,24},{24,17},{25,16},{2,11},{3,... | collective-permute-start | bytes 86024 | tf_op jit(solution)/shard_map/ppermute | solution.py:437
  31.2 1.9 %collective-permute-done.10 = f32[56,128]{1,0:T(8,128)S(1)} collective-permute-done((f32[56,128]{1,0:T(8,128)S(1)}, f32[56,128]{1,0:T(8,128)S(1)}, u32[]{:S(2)}, u32[]{:S(2)}) %collective-permute-start.10) | collective-permute-done | bytes 28704 | tf_op jit(solution)/shard_map/ppermute | solution.py:437
  33.0 0.2 collective-permute-done.9
  33.2 0.0 collective-permute-done.8
  33.2 2.4 %collective-permute-start.13 = (f32[56,128]{1,0:T(8,128)S(1)}, f32[56,128]{1,0:T(8,128)S(1)}, u32[]{:S(2)}, u32[]{:S(2)}) collective-permute-start(f32[56,128]{1,0:T(8,128)S(1)} %add_add_fusion.own_ref), channel_id=1, source_target_pairs={{0,65},{1,64},{32,97},{33,96},{64,1},{65,0},{96,33},{97,32},{2,67}... | collective-permute-start | bytes 86024 | tf_op jit(solution)/shard_map/ppermute | solution.py:437
  35.5 0.9 %collective-permute-start.12 = (f32[56,128]{1,0:T(8,128)S(1)}, f32[56,128]{1,0:T(8,128)S(1)}, u32[]{:S(2)}, u32[]{:S(2)}) collective-permute-start(f32[56,128]{1,0:T(8,128)S(1)} %add_add_fusion.own_ref), channel_id=1, source_target_pairs={{0,97},{1,96},{32,65},{33,64},{64,33},{65,32},{96,1},{97,0},{2,99}... | collective-permute-start | bytes 86024 | tf_op jit(solution)/shard_map/ppermute | solution.py:437
  36.4 0.5 %collective-permute-start.11 = (f32[56,128]{1,0:T(8,128)S(1)}, f32[56,128]{1,0:T(8,128)S(1)}, u32[]{:S(2)}, u32[]{:S(2)}) collective-permute-start(f32[56,128]{1,0:T(8,128)S(1)} %add_add_fusion.own_ref), channel_id=1, source_target_pairs={{0,33},{1,32},{32,1},{33,0},{64,97},{65,96},{96,65},{97,64},{2,35}... | collective-permute-start | bytes 86024 | tf_op jit(solution)/shard_map/ppermute | solution.py:437
  36.9 1.1 %collective-permute-done.13.two_ref = f32[56,128]{1,0:T(8,128)S(1)} collective-permute-done((f32[56,128]{1,0:T(8,128)S(1)}, f32[56,128]{1,0:T(8,128)S(1)}, u32[]{:S(2)}, u32[]{:S(2)}) %collective-permute-start.13) | collective-permute-done | bytes 28704 | tf_op jit(solution)/shard_map/ppermute | solution.py:437
  38.1 2.0 %collective-permute-done.12.three_ref = f32[56,128]{1,0:T(8,128)S(1)} collective-permute-done((f32[56,128]{1,0:T(8,128)S(1)}, f32[56,128]{1,0:T(8,128)S(1)}, u32[]{:S(2)}, u32[]{:S(2)}) %collective-permute-start.12) | collective-permute-done | bytes 28704 | tf_op jit(solution)/shard_map/ppermute | solution.py:437
  40.1 0.0 collective-permute-done.11.one_ref
  40.1 3.8 %solve.1 = (f32[97,97]{1,0:T(8,128)}, f32[1,96]{1,0:T(1,128)}, bf16[5,96,512]{2,1,0:T(8,128)(2,1)}) custom-call(f32[56,128]{1,0:T(8,128)S(1)} %collective-permute-done.11.one_ref, f32[56,128]{1,0:T(8,128)S(1)} %collective-permute-done.12.three_ref, f32[56,128]{1,0:T(8,128)S(1)} %collective-permute-done.13.two_ref, f32[56,128]{1,0:T(8,128)S(1)} %add_add_fusion.own_ref, ...), custom_call_target="tpu_custom_call" | custom-call | tf_op jit(solution)/shard_map/solve/pallas_call | solution.py:415
  (6 shorter events, 0.1 us)
Async XLA Ops:
  3.3 8.8 %collective-permute-start = (bf16[240,128]{1,0:T(8,128)(2,1)S(1)}, bf16[240,128]{1,0:T(8,128)(2,1)S(1)}, u32[]{:S(2)}, u32[]{:S(2)}) collective-permute-start(bf16[240,128]{1,0:T(8,128)(2,1)S(1)} %get-tuple-element.33), channel_id=1, source_target_pairs={{0,8},{8,0},{16,24},{24,16},{32,40},{40,32},{48,56},{56,48},{64,72... | collective-permute-start | bytes 184328 | tf_op jit(solution)/shard_map/ppermute | solution.py:432
  5.5 6.6 %collective-permute-start.1 = (bf16[240,128]{1,0:T(8,128)(2,1)S(1)}, bf16[240,128]{1,0:T(8,128)(2,1)S(1)}, u32[]{:S(2)}, u32[]{:S(2)}) collective-permute-start(bf16[240,128]{1,0:T(8,128)(2,1)S(1)} %get-tuple-element.34), channel_id=1, source_target_pairs={{0,120},{8,16},{16,8},{24,32},{32,24},{40,48},{48,40},{56,64},{64,... | collective-permute-start | bytes 184328 | tf_op jit(solution)/shard_map/ppermute | solution.py:442
  12.2 5.5 %collective-permute-start.3 = (bf16[240,128]{1,0:T(8,128)(2,1)S(1)}, bf16[240,128]{1,0:T(8,128)(2,1)S(1)}, u32[]{:S(2)}, u32[]{:S(2)}) collective-permute-start(bf16[240,128]{1,0:T(8,128)(2,1)S(1)} %get-tuple-element.45), channel_id=1, source_target_pairs={{0,7},{1,2},{2,1},{3,4},{4,3},{5,6},{6,5},{7,0},{8,15},{9,10},{10,... | collective-permute-start | bytes 184328 | tf_op jit(solution)/shard_map/ppermute | solution.py:442
  15.7 2.0 %collective-permute-start.2 = (bf16[240,128]{1,0:T(8,128)(2,1)S(1)}, bf16[240,128]{1,0:T(8,128)(2,1)S(1)}, u32[]{:S(2)}, u32[]{:S(2)}) collective-permute-start(bf16[240,128]{1,0:T(8,128)(2,1)S(1)} %get-tuple-element.46), channel_id=1, source_target_pairs={{0,1},{1,0},{2,3},{3,2},{4,5},{5,4},{6,7},{7,6},{8,9},{9,8},{10,11... | collective-permute-start | bytes 184328 | tf_op jit(solution)/shard_map/ppermute | solution.py:432
  18.7 2.2 %collective-permute-start.4 = (f32[56,128]{1,0:T(8,128)S(1)}, f32[56,128]{1,0:T(8,128)S(1)}, u32[]{:S(2)}, u32[]{:S(2)}) collective-permute-start(f32[56,128]{1,0:T(8,128)S(1)} %get-tuple-element.40), channel_id=1, source_target_pairs={{0,1},{1,0},{2,3},{3,2},{4,5},{5,4},{6,7},{7,6},{8,9},{9,8},{10,11... | collective-permute-start | bytes 86024 | tf_op jit(solution)/shard_map/ppermute | solution.py:432
  20.9 4.8 %collective-permute-start.7 = (f32[56,128]{1,0:T(8,128)S(1)}, f32[56,128]{1,0:T(8,128)S(1)}, u32[]{:S(2)}, u32[]{:S(2)}) collective-permute-start(f32[56,128]{1,0:T(8,128)S(1)} %add.36), channel_id=1, source_target_pairs={{0,5},{1,4},{2,7},{3,6},{4,1},{5,0},{6,3},{7,2},{8,13},{9,12},{10,... | collective-permute-start | bytes 86024 | tf_op jit(solution)/shard_map/ppermute | solution.py:437
  23.6 4.5 %collective-permute-start.6 = (f32[56,128]{1,0:T(8,128)S(1)}, f32[56,128]{1,0:T(8,128)S(1)}, u32[]{:S(2)}, u32[]{:S(2)}) collective-permute-start(f32[56,128]{1,0:T(8,128)S(1)} %add.36), channel_id=1, source_target_pairs={{0,7},{1,6},{2,5},{3,4},{4,3},{5,2},{6,1},{7,0},{8,15},{9,14},{10,... | collective-permute-start | bytes 86024 | tf_op jit(solution)/shard_map/ppermute | solution.py:437
  24.2 3.9 %collective-permute-start.5 = (f32[56,128]{1,0:T(8,128)S(1)}, f32[56,128]{1,0:T(8,128)S(1)}, u32[]{:S(2)}, u32[]{:S(2)}) collective-permute-start(f32[56,128]{1,0:T(8,128)S(1)} %add.36), channel_id=1, source_target_pairs={{0,3},{1,2},{2,1},{3,0},{4,7},{5,6},{6,5},{7,4},{8,11},{9,10},{10,... | collective-permute-start | bytes 86024 | tf_op jit(solution)/shard_map/ppermute | solution.py:437
  28.1 4.9 %collective-permute-start.10 = (f32[56,128]{1,0:T(8,128)S(1)}, f32[56,128]{1,0:T(8,128)S(1)}, u32[]{:S(2)}, u32[]{:S(2)}) collective-permute-start(f32[56,128]{1,0:T(8,128)S(1)} %add_add_fusion.1), channel_id=1, source_target_pairs={{0,17},{1,16},{8,25},{9,24},{16,1},{17,0},{24,9},{25,8},{2,19},{3,... | collective-permute-start | bytes 86024 | tf_op jit(solution)/shard_map/ppermute | solution.py:437
  28.2 5.0 %collective-permute-start.9 = (f32[56,128]{1,0:T(8,128)S(1)}, f32[56,128]{1,0:T(8,128)S(1)}, u32[]{:S(2)}, u32[]{:S(2)}) collective-permute-start(f32[56,128]{1,0:T(8,128)S(1)} %add_add_fusion.1), channel_id=1, source_target_pairs={{0,25},{1,24},{8,17},{9,16},{16,9},{17,8},{24,1},{25,0},{2,27},{3,... | collective-permute-start | bytes 86024 | tf_op jit(solution)/shard_map/ppermute | solution.py:437
  29.0 4.2 %collective-permute-start.8 = (f32[56,128]{1,0:T(8,128)S(1)}, f32[56,128]{1,0:T(8,128)S(1)}, u32[]{:S(2)}, u32[]{:S(2)}) collective-permute-start(f32[56,128]{1,0:T(8,128)S(1)} %add_add_fusion.1), channel_id=1, source_target_pairs={{0,9},{1,8},{8,1},{9,0},{16,25},{17,24},{24,17},{25,16},{2,11},{3,... | collective-permute-start | bytes 86024 | tf_op jit(solution)/shard_map/ppermute | solution.py:437
  33.2 4.9 %collective-permute-start.13 = (f32[56,128]{1,0:T(8,128)S(1)}, f32[56,128]{1,0:T(8,128)S(1)}, u32[]{:S(2)}, u32[]{:S(2)}) collective-permute-start(f32[56,128]{1,0:T(8,128)S(1)} %add_add_fusion.own_ref), channel_id=1, source_target_pairs={{0,65},{1,64},{32,97},{33,96},{64,1},{65,0},{96,33},{97,32},{2,67}... | collective-permute-start | bytes 86024 | tf_op jit(solution)/shard_map/ppermute | solution.py:437
  35.5 4.5 %collective-permute-start.12 = (f32[56,128]{1,0:T(8,128)S(1)}, f32[56,128]{1,0:T(8,128)S(1)}, u32[]{:S(2)}, u32[]{:S(2)}) collective-permute-start(f32[56,128]{1,0:T(8,128)S(1)} %add_add_fusion.own_ref), channel_id=1, source_target_pairs={{0,97},{1,96},{32,65},{33,64},{64,33},{65,32},{96,1},{97,0},{2,99}... | collective-permute-start | bytes 86024 | tf_op jit(solution)/shard_map/ppermute | solution.py:437
  36.4 3.7 %collective-permute-start.11 = (f32[56,128]{1,0:T(8,128)S(1)}, f32[56,128]{1,0:T(8,128)S(1)}, u32[]{:S(2)}, u32[]{:S(2)}) collective-permute-start(f32[56,128]{1,0:T(8,128)S(1)} %add_add_fusion.own_ref), channel_id=1, source_target_pairs={{0,33},{1,32},{32,1},{33,0},{64,97},{65,96},{96,65},{97,64},{2,35}... | collective-permute-start | bytes 86024 | tf_op jit(solution)/shard_map/ppermute | solution.py:437
